TPU v7x, 512 devices: a whole 4x8x8 slice. The times are simulated.
512 devices in a mesh: grp: 16 (over y, core), seq: 32 (over z, x).
Axes of the slice: x: 4, y: 8, z: 8, core: 2. Of those that a mesh axis runs over, the one named last changes fastest.
Arguments:
- loader_rows: bfloat16 [229376, 3072], P(('grp', 'seq')), may hold values from -6 to 6
- loader_lengths: int32 [16, 32], P('grp', 'seq'), may hold values from 64 to 448, as said below
- net_lengths: int32 [64], replicated, may hold values from 1 to 4096, 131072 in all
- feature_map: float32 [128, 256], replicated, may hold values from -2.5 to 2.5
- carried_state: float32 [8, 256, 128], replicated, may hold values from -18000 to 18000
- carried_norm: float32 [8, 256], replicated, may hold values from 200 to 4000
Outputs:
- attended: float32 [131072, 1024], P(('grp', 'seq'))
Inputs may be any that keep to these rules, and one draw needn't show every extreme that they name: `loader_lengths`: in each index of grp the lengths sum to 8192, and the first d of them sum to within 96 of d * 256; rows of a loader shard past its length are padding. `net_lengths`: the lengths sum to 131072.
All inputs are finite; a program needn't handle non-finite values.
Results may differ from a plain program's by a relative error of at most 0.0005.
Values may be sent and summed in bfloat16 or wider, within the bound.
No kernel may reach another device: no remote copies, remote signals or barrier semaphores. Data moves between devices by JAX's collectives and lax.ppermute only.
A program may use at most 128 MiB of HBM per device.

v0:
```python
import jax
import jax.numpy as jnp
from jax import lax
from jax.sharding import PartitionSpec as P

H = 8
DH = 128
TOK_DEV = 256
NET_SPAN = 16
DRIFT = 96


highest_level = lax.Precision.HIGHEST


def entering(value, axis, join, neutral):
    count, mine = (lax.axis_size(axis), lax.axis_index(axis))
    pieces = lax.all_gather(value, axis)
    so_far = jnp.full_like(value, 0) + jnp.asarray(neutral, value.dtype)

    def hop(position, so_far):
        longer = join(so_far, pieces[position])
        return jnp.where(position < mine, longer, so_far)

    return lax.fori_loop(0, count - 1, hop, so_far)


def shifted(block, axis, distance):
    devices = range(lax.axis_size(axis))
    route = [(i - distance, i) for i in devices if i - distance in devices]
    return lax.ppermute(block, axis, route)


def features(split_part, feature_map):
    value_rows = split_part.astype(jnp.float32)
    scale = lax.rsqrt(
        jnp.mean(value_rows * value_rows, axis=-1, keepdims=True) + 1e-06
    ) * value_rows.shape[-1] ** (-0.5)
    return jnp.exp(
        jnp.einsum("rhd,dm->rhm", value_rows * scale, feature_map, precision=highest_level)
    )


def net_begins(net_lengths):
    net_ends = jnp.cumsum(net_lengths)
    begins = net_ends - net_lengths
    return jnp.where(jnp.arange(net_lengths.shape[0]) == 0, -1, begins)


def local_terms(row_block, positions, valid_rows, begins, feature_map):
    count = row_block.shape[0]
    split_rows = row_block.reshape(count, 3, H, DH)
    query_features = features(split_rows[:, 0], feature_map)
    key_feat = features(split_rows[:, 1], feature_map)
    value_rows = split_rows[:, 2].astype(jnp.float32)
    net_begin = jnp.max(
        jnp.where(begins[None, :] <= positions[:, None], begins[None, :], -1), axis=1
    )
    offsets = jnp.arange(count, dtype=jnp.int32)
    allowed = (
        (net_begin[:, None] == net_begin[None, :])
        & (offsets[None, :] <= offsets[:, None])
        & valid_rows[None, :]
    )
    scores = (
        jnp.einsum("rhm,shm->hrs", query_features, key_feat, precision=highest_level)
        * jnp.where(allowed, 1.0, 0.0).astype(jnp.float32)[None]
    )
    numerator_output = jnp.einsum("hrs,shd->rhd", scores, value_rows, precision=highest_level)
    denominator = jnp.transpose(jnp.sum(scores, axis=2))
    last_begin = jnp.max(jnp.where(valid_rows, net_begin, -2))
    weights = jnp.where(valid_rows & (net_begin == last_begin), 1.0, 0.0).astype(jnp.float32)
    weighted_values = key_feat * weights[:, None, None]
    state_running_sum = jnp.einsum(
        "qyu,qyo->yuo", weighted_values, value_rows, precision=highest_level
    )
    norm_sum = jnp.sum(weighted_values, axis=0)
    restart = (
        jnp.max(jnp.where(valid_rows & (net_begin == positions), 1.0, 0.0))
        .astype(jnp.float32)
        .reshape(1)
    )
    return (
        numerator_output,
        denominator,
        query_features,
        net_begin,
        (restart, norm_sum, state_running_sum),
    )


def finish(
    numerator_output,
    denominator,
    query_features,
    net_begin,
    valid_rows,
    block_start,
    incoming_state,
    norm_in,
):
    incoming_carry = jnp.where(net_begin < block_start, 1.0, 0.0).astype(jnp.float32)
    numerator_output = numerator_output + incoming_carry[:, None, None] * jnp.einsum(
        "lqc,qcf->lqf", query_features, incoming_state, precision=highest_level
    )
    denominator = denominator + incoming_carry[:, None] * jnp.einsum(
        "rhm,hm->rh", query_features, norm_in, precision=highest_level
    )
    denominator = jnp.where(valid_rows[:, None], denominator, 1.0)
    return (numerator_output / denominator[:, :, None]).reshape(numerator_output.shape[0], -1)


def add_counts(earlier, later):
    return earlier + later


def join_states(earlier, later):
    restart = jnp.maximum(earlier[0], later[0])
    fresh = later[0][0] > 0
    return (
        restart,
        jnp.where(fresh, later[1], earlier[1] + later[1]),
        jnp.where(fresh, later[2], earlier[2] + later[2]),
    )


def edge_rows(buffer, length):
    picked = jnp.clip(length - DRIFT + jnp.arange(DRIFT, dtype=jnp.int32), 0, buffer.shape[0] - 1)
    return (jnp.take(buffer, picked, axis=0), buffer[:DRIFT])


def assemble(buffer, from_left, from_right, length, drift_now):
    padding = jnp.zeros((DRIFT, buffer.shape[1]), buffer.dtype)
    extended = lax.dynamic_update_slice_in_dim(
        jnp.concatenate([buffer, padding], axis=0), from_right, length, 0
    )
    extended = jnp.concatenate([from_left, extended], axis=0)
    return lax.dynamic_slice_in_dim(extended, DRIFT - drift_now, TOK_DEV, 0)


def local(loader_rows, loader_lengths, net_lengths, feature_map, carried_state, carried_norm):
    before = entering(loader_lengths, "seq", add_counts, jnp.zeros_like(loader_lengths))
    shard_index = lax.axis_index("seq")
    group_index = lax.axis_index("grp")
    length = loader_lengths[0, 0]
    drift_now = before[0, 0] - shard_index * TOK_DEV
    even_start = (group_index * lax.axis_size("seq") + shard_index) * TOK_DEV
    begins = net_begins(net_lengths)
    tail_rows, head_rows = edge_rows(loader_rows, length)
    from_left = shifted(tail_rows, "seq", 1)
    from_right = shifted(head_rows, "seq", -1)
    row_block = assemble(loader_rows, from_left, from_right, length, drift_now)
    valid_rows = jnp.arange(TOK_DEV, dtype=jnp.int32) >= 0
    reach_limit = NET_SPAN
    positions = even_start + jnp.arange(row_block.shape[0], dtype=jnp.int32)
    numerator_output, denominator, query_features, net_begin, element = local_terms(
        row_block, positions, valid_rows, begins, feature_map
    )
    reach_list = [1]
    stride = 1
    while stride < reach_limit:
        reach_list.append(stride)
        stride = stride * 2
    prefix = element
    for round_index, distance in enumerate(reach_list):
        arrived = shifted((prefix[0], prefix[1], prefix[2]), ("grp", "seq"), distance)
        prefix = arrived if round_index == 0 else join_states(arrived, prefix)
    fresh = prefix[0][0] > 0
    incoming_state = jnp.where(fresh, prefix[2], prefix[2] + carried_state)
    norm_in = jnp.where(fresh, prefix[1], prefix[1] + carried_norm)
    attended = finish(
        numerator_output,
        denominator,
        query_features,
        net_begin,
        valid_rows,
        even_start,
        incoming_state,
        norm_in,
    )
    return attended


def solution(mesh):
    in_specs = (P(("grp", "seq"), None), P("grp", "seq"), P(), P(), P(), P())
    out_specs = P(("grp", "seq"), None)
    return jax.shard_map(local, mesh=mesh, in_specs=in_specs, out_specs=out_specs, check_vma=False)
```

profile of v0, /device:TPU:37, one launch (start us, length us, event | category | flops | bytes accessed | tf_op | source)
XLA Modules:
  0.0 304.8 jit_solution(12303332699420331040)
XLA Ops:
  2.0 2.2 collective-permute-start.1
  4.8 3.8 %gather_fusion = bf16[96,3072]{1,0:T(8,128)(2,1)S(1)} fusion(bf16[448,3072]{1,0:T(8,128)(2,1)} %param.8, s32[1024]{0:T(1024)S(1)} %pad_clamp_fusion), kind=kCustom, calls=%fused_computation | custom fusion | bytes 1180032 | tf_op jit(solution)/shard_map/jit(_take)/gather | solution.py:129
  9.6 3.1 %collective-permute-start = (bf16[96,3072]{1,0:T(8,128)(2,1)}, bf16[96,3072]{1,0:T(8,128)(2,1)}, u32[]{:S(2)}, u32[]{:S(2)}) collective-permute-start(bf16[96,3072]{1,0:T(8,128)(2,1)} %broadcast_select_fusion), channel_id=1, source_target_pairs={{0,1},{1,2},{2,3},{3,4},{4,5},{5,6},{6,7},{7,8},{8,9},{9,10},{10,1... | collective-permute-start | bytes 1769480 | tf_op jit(solution)/shard_map/ppermute | solution.py:31
  14.8 27.0 %all-reduce.1 = s32[32]{0:T(128)S(1)} all-reduce(s32[32]{0:T(128)S(1)} %bitcast_dynamic-update-slice_fusion), channel_id=2, replica_groups=mesh['grp'=16,'seq'=32] {'seq'}, use_global_device_ids=true, to_apply=%add.1 | all-reduce | flops 32 | bytes 256
  41.8 39.4 %while.13 = (s32[]{:T(128)}, s32[1,1]{1,0:T(1,128)}, s32[]{:T(128)}, s32[32,1,1]{0,2,1:T(1,128)S(1)}, s32[]{:T(128)}) while((s32[]{:T(128)}, s32[1,1]{1,0:T(1,128)}, s32[]{:T(128)}, s32[32,1,1]{0,2,1:T(1,128)S(1)}, s32[]{:T(128)}) %tuple.40), condition=%wide.region_1.2_spmd, body=%wide.region_0.1_spmd.sunk | while | flops 5 | bytes 107 | solution.py:25
  81.2 2.1 concatenate.6
  85.7 4.2 %dynamic_update_slice.3 = bf16[544,3072]{1,0:T(8,128)(2,1)} dynamic-update-slice(bf16[544,3072]{1,0:T(8,128)(2,1)} %concatenate.6, bf16[96,3072]{1,0:T(8,128)(2,1)} %collective-permute-done.1, s32[]{:T(128)S(6)} %select_n.154, s32[]{:T(128)} %constant.73.clone.1) | dynamic-update-slice | bytes 1179652 | tf_op jit(solution)/shard_map/dynamic_update_slice | solution.py:134
  89.9 2.1 fusion.12
  93.0 2.1 multiply_reduce_fusion
  97.0 5.3 %collective-permute-start.7 = (f32[8,256,128]{2,1,0:T(8,128)S(1)}, f32[8,256,128]{2,1,0:T(8,128)S(1)}, u32[]{:S(2)}, u32[]{:S(2)}) collective-permute-start(f32[8,256,128]{2,1,0:T(8,128)S(1)} %fusion), channel_id=1, source_target_pairs={{0,1},{1,2},{2,3},{3,4},{4,5},{5,6},{6,7},{7,8},{8,9},{9,10},{10,1... | collective-permute-start | bytes 3145736 | tf_op jit(solution)/shard_map/ppermute | solution.py:31
  102.4 17.9 %collective-permute-done.7 = f32[8,256,128]{2,1,0:T(8,128)S(1)} collective-permute-done((f32[8,256,128]{2,1,0:T(8,128)S(1)}, f32[8,256,128]{2,1,0:T(8,128)S(1)}, u32[]{:S(2)}, u32[]{:S(2)}) %collective-permute-start.7) | collective-permute-done | bytes 1048608 | tf_op jit(solution)/shard_map/ppermute | solution.py:31
  120.3 3.6 %collective-permute-start.8 = (f32[8,256,128]{2,1,0:T(8,128)S(1)}, f32[8,256,128]{2,1,0:T(8,128)S(1)}, u32[]{:S(2)}, u32[]{:S(2)}) collective-permute-start(f32[8,256,128]{2,1,0:T(8,128)S(1)} %collective-permute-done.7), channel_id=1, source_target_pairs={{0,1},{1,2},{2,3},{3,4},{4,5},{5,6},{6,7},{7,8},{8,9},{9,10},{10,1... | collective-permute-start | bytes 3145736 | tf_op jit(solution)/shard_map/ppermute | solution.py:31
  123.9 4.3 %collective-permute-start.2 = (f32[1]{0:T(128)}, f32[1]{0:T(128)}, u32[]{:S(2)}, u32[]{:S(2)}) collective-permute-start(f32[1]{0:T(128)} %bitcast.16), channel_id=1, source_target_pairs={{0,1},{1,2},{2,3},{3,4},{4,5},{5,6},{6,7},{7,8},{8,9},{9,10},{10,1... | collective-permute-start | bytes 20 | tf_op jit(solution)/shard_map/ppermute | solution.py:31
  128.2 13.7 %collective-permute-done.2 = f32[1]{0:T(128)} collective-permute-done((f32[1]{0:T(128)}, f32[1]{0:T(128)}, u32[]{:S(2)}, u32[]{:S(2)}) %collective-permute-start.2) | collective-permute-done | bytes 36 | tf_op jit(solution)/shard_map/ppermute | solution.py:31
  142.7 6.5 %collective-permute-start.9 = (f32[8,256,128]{2,1,0:T(8,128)S(1)}, f32[8,256,128]{2,1,0:T(8,128)S(1)}, u32[]{:S(2)}, u32[]{:S(2)}) collective-permute-start(f32[8,256,128]{2,1,0:T(8,128)S(1)} %add_select_fusion.4), channel_id=1, source_target_pairs={{0,2},{1,3},{2,4},{3,5},{4,6},{5,7},{6,8},{7,9},{8,10},{9,11},{10,... | collective-permute-start | bytes 3145736 | tf_op jit(solution)/shard_map/ppermute | solution.py:31
  151.3 2.8 collective-permute-start.3
  154.1 20.8 %collective-permute-done.3 = f32[1]{0:T(128)} collective-permute-done((f32[1]{0:T(128)}, f32[1]{0:T(128)}, u32[]{:S(2)}, u32[]{:S(2)}) %collective-permute-start.3) | collective-permute-done | bytes 36 | tf_op jit(solution)/shard_map/ppermute | solution.py:31
  176.2 2.6 collective-permute-start.4
  178.8 12.9 %collective-permute-done.4 = f32[1]{0:T(128)} collective-permute-done((f32[1]{0:T(128)}, f32[1]{0:T(128)}, u32[]{:S(2)}, u32[]{:S(2)}) %collective-permute-start.4) | collective-permute-done | bytes 36 | tf_op jit(solution)/shard_map/ppermute | solution.py:31
  192.3 2.6 collective-permute-start.5
  195.0 3.5 %collective-permute-done.5 = f32[1]{0:T(128)} collective-permute-done((f32[1]{0:T(128)}, f32[1]{0:T(128)}, u32[]{:S(2)}, u32[]{:S(2)}) %collective-permute-start.5) | collective-permute-done | bytes 36 | tf_op jit(solution)/shard_map/ppermute | solution.py:31
  199.1 2.6 collective-permute-start.6
  201.8 4.4 %collective-permute-done.6 = f32[1]{0:T(128)} collective-permute-done((f32[1]{0:T(128)}, f32[1]{0:T(128)}, u32[]{:S(2)}, u32[]{:S(2)}) %collective-permute-start.6) | collective-permute-done | bytes 36 | tf_op jit(solution)/shard_map/ppermute | solution.py:31
  208.8 2.5 collective-permute-done.13
  211.2 7.5 %collective-permute-start.14 = (f32[8,256]{1,0:T(8,128)S(1)}, f32[8,256]{1,0:T(8,128)S(1)}, u32[]{:S(2)}, u32[]{:S(2)}) collective-permute-start(f32[8,256]{1,0:T(8,128)S(1)} %add_select_fusion.10), channel_id=1, source_target_pairs={{0,2},{1,3},{2,4},{3,5},{4,6},{5,7},{6,8},{7,9},{8,10},{9,11},{10,... | collective-permute-start | bytes 24584 | tf_op jit(solution)/shard_map/ppermute | solution.py:31
  218.9 2.2 collective-permute-start.10
  223.6 2.1 collective-permute-start.15
  225.7 2.7 multiply_reduce_fusion.1
  228.4 22.8 %collective-permute-done.15 = f32[8,256]{1,0:T(8,128)S(1)} collective-permute-done((f32[8,256]{1,0:T(8,128)S(1)}, f32[8,256]{1,0:T(8,128)S(1)}, u32[]{:S(2)}, u32[]{:S(2)}) %collective-permute-start.15) | collective-permute-done | bytes 8224 | tf_op jit(solution)/shard_map/ppermute | solution.py:31
  256.2 3.2 %collective-permute-done.16 = f32[8,256]{1,0:T(8,128)S(1)} collective-permute-done((f32[8,256]{1,0:T(8,128)S(1)}, f32[8,256]{1,0:T(8,128)S(1)}, u32[]{:S(2)}, u32[]{:S(2)}) %collective-permute-start.16) | collective-permute-done | bytes 8224 | tf_op jit(solution)/shard_map/ppermute | solution.py:31
  261.1 39.8 %collective-permute-done.11 = f32[8,256,128]{2,1,0:T(8,128)S(1)} collective-permute-done((f32[8,256,128]{2,1,0:T(8,128)S(1)}, f32[8,256,128]{2,1,0:T(8,128)S(1)}, u32[]{:S(2)}, u32[]{:S(2)}) %collective-permute-start.11) | collective-permute-done | bytes 1048608 | tf_op jit(solution)/shard_map/ppermute | solution.py:31
  301.0 2.6 fusion.22
  (85 shorter events, 44.0 us)
Async XLA Ops:
  0.0 93.0 %copy-start = (f32[128,256]{1,0:T(8,128)S(1)}, f32[128,256]{1,0:T(8,128)}, u32[]{:S(2)}) copy-start(f32[128,256]{1,0:T(8,128)} %param.11) | copy-start | bytes 393220
  2.0 83.7 %collective-permute-start.1 = (bf16[96,3072]{1,0:T(8,128)(2,1)}, bf16[96,3072]{1,0:T(8,128)(2,1)}, u32[]{:S(2)}, u32[]{:S(2)}) collective-permute-start(bf16[96,3072]{1,0:T(8,128)(2,1)} %slice.12), channel_id=1, source_target_pairs={{1,0},{2,1},{3,2},{4,3},{5,4},{6,5},{7,6},{8,7},{9,8},{10,9},{11,1... | collective-permute-start | bytes 1769480 | tf_op jit(solution)/shard_map/ppermute | solution.py:31
  4.8 76.4 %copy-start.1 = (bf16[448,3072]{1,0:T(8,128)(2,1)S(1)}, bf16[448,3072]{1,0:T(8,128)(2,1)}, u32[]{:S(2)}) copy-start(bf16[448,3072]{1,0:T(8,128)(2,1)} %param.8) | copy-start | bytes 8257540
  9.6 80.3 %collective-permute-start = (bf16[96,3072]{1,0:T(8,128)(2,1)}, bf16[96,3072]{1,0:T(8,128)(2,1)}, u32[]{:S(2)}, u32[]{:S(2)}) collective-permute-start(bf16[96,3072]{1,0:T(8,128)(2,1)} %broadcast_select_fusion), channel_id=1, source_target_pairs={{0,1},{1,2},{2,3},{3,4},{4,5},{5,6},{6,7},{7,8},{8,9},{9,10},{10,1... | collective-permute-start | bytes 1769480 | tf_op jit(solution)/shard_map/ppermute | solution.py:31
  81.2 2.1 copy-start.4
  97.0 23.3 %collective-permute-start.7 = (f32[8,256,128]{2,1,0:T(8,128)S(1)}, f32[8,256,128]{2,1,0:T(8,128)S(1)}, u32[]{:S(2)}, u32[]{:S(2)}) collective-permute-start(f32[8,256,128]{2,1,0:T(8,128)S(1)} %fusion), channel_id=1, source_target_pairs={{0,1},{1,2},{2,3},{3,4},{4,5},{5,6},{6,7},{7,8},{8,9},{9,10},{10,1... | collective-permute-start | bytes 3145736 | tf_op jit(solution)/shard_map/ppermute | solution.py:31
  120.3 22.3 %collective-permute-start.8 = (f32[8,256,128]{2,1,0:T(8,128)S(1)}, f32[8,256,128]{2,1,0:T(8,128)S(1)}, u32[]{:S(2)}, u32[]{:S(2)}) collective-permute-start(f32[8,256,128]{2,1,0:T(8,128)S(1)} %collective-permute-done.7), channel_id=1, source_target_pairs={{0,1},{1,2},{2,3},{3,4},{4,5},{5,6},{6,7},{7,8},{8,9},{9,10},{10,1... | collective-permute-start | bytes 3145736 | tf_op jit(solution)/shard_map/ppermute | solution.py:31
  123.9 18.0 %collective-permute-start.2 = (f32[1]{0:T(128)}, f32[1]{0:T(128)}, u32[]{:S(2)}, u32[]{:S(2)}) collective-permute-start(f32[1]{0:T(128)} %bitcast.16), channel_id=1, source_target_pairs={{0,1},{1,2},{2,3},{3,4},{4,5},{5,6},{6,7},{7,8},{8,9},{9,10},{10,1... | collective-permute-start | bytes 20 | tf_op jit(solution)/shard_map/ppermute | solution.py:31
  142.7 76.0 %collective-permute-start.9 = (f32[8,256,128]{2,1,0:T(8,128)S(1)}, f32[8,256,128]{2,1,0:T(8,128)S(1)}, u32[]{:S(2)}, u32[]{:S(2)}) collective-permute-start(f32[8,256,128]{2,1,0:T(8,128)S(1)} %add_select_fusion.4), channel_id=1, source_target_pairs={{0,2},{1,3},{2,4},{3,5},{4,6},{5,7},{6,8},{7,9},{8,10},{9,11},{10,... | collective-permute-start | bytes 3145736 | tf_op jit(solution)/shard_map/ppermute | solution.py:31
  149.3 57.5 %collective-permute-start.12 = (f32[8,256]{1,0:T(8,128)S(1)}, f32[8,256]{1,0:T(8,128)S(1)}, u32[]{:S(2)}, u32[]{:S(2)}) collective-permute-start(f32[8,256]{1,0:T(8,128)S(1)} %get-tuple-element.114), channel_id=1, source_target_pairs={{0,1},{1,2},{2,3},{3,4},{4,5},{5,6},{6,7},{7,8},{8,9},{9,10},{10,1... | collective-permute-start | bytes 24584 | tf_op jit(solution)/shard_map/ppermute | solution.py:31
  151.3 23.6 %collective-permute-start.3 = (f32[1]{0:T(128)}, f32[1]{0:T(128)}, u32[]{:S(2)}, u32[]{:S(2)}) collective-permute-start(f32[1]{0:T(128)} %collective-permute-done.2), channel_id=1, source_target_pairs={{0,1},{1,2},{2,3},{3,4},{4,5},{5,6},{6,7},{7,8},{8,9},{9,10},{10,1... | collective-permute-start | bytes 20 | tf_op jit(solution)/shard_map/ppermute | solution.py:31
  176.2 15.5 %collective-permute-start.4 = (f32[1]{0:T(128)}, f32[1]{0:T(128)}, u32[]{:S(2)}, u32[]{:S(2)}) collective-permute-start(f32[1]{0:T(128)} %max.22), channel_id=1, source_target_pairs={{0,2},{1,3},{2,4},{3,5},{4,6},{5,7},{6,8},{7,9},{8,10},{9,11},{10,... | collective-permute-start | bytes 20 | tf_op jit(solution)/shard_map/ppermute | solution.py:31
  192.3 6.2 %collective-permute-start.5 = (f32[1]{0:T(128)}, f32[1]{0:T(128)}, u32[]{:S(2)}, u32[]{:S(2)}) collective-permute-start(f32[1]{0:T(128)} %max.23), channel_id=1, source_target_pairs={{0,4},{1,5},{2,6},{3,7},{4,8},{5,9},{6,10},{7,11},{8,12},{9,13},{1... | collective-permute-start | bytes 20 | tf_op jit(solution)/shard_map/ppermute | solution.py:31
  199.1 7.1 %collective-permute-start.6 = (f32[1]{0:T(128)}, f32[1]{0:T(128)}, u32[]{:S(2)}, u32[]{:S(2)}) collective-permute-start(f32[1]{0:T(128)} %max.24), channel_id=1, source_target_pairs={{0,8},{1,9},{2,10},{3,11},{4,12},{5,13},{6,14},{7,15},{8,16},{9,17... | collective-permute-start | bytes 20 | tf_op jit(solution)/shard_map/ppermute | solution.py:31
  206.8 4.4 %collective-permute-start.13 = (f32[8,256]{1,0:T(8,128)S(1)}, f32[8,256]{1,0:T(8,128)S(1)}, u32[]{:S(2)}, u32[]{:S(2)}) collective-permute-start(f32[8,256]{1,0:T(8,128)S(1)} %collective-permute-done.12), channel_id=1, source_target_pairs={{0,1},{1,2},{2,3},{3,4},{4,5},{5,6},{6,7},{7,8},{8,9},{9,10},{10,1... | collective-permute-start | bytes 24584 | tf_op jit(solution)/shard_map/ppermute | solution.py:31
  211.2 12.3 %collective-permute-start.14 = (f32[8,256]{1,0:T(8,128)S(1)}, f32[8,256]{1,0:T(8,128)S(1)}, u32[]{:S(2)}, u32[]{:S(2)}) collective-permute-start(f32[8,256]{1,0:T(8,128)S(1)} %add_select_fusion.10), channel_id=1, source_target_pairs={{0,2},{1,3},{2,4},{3,5},{4,6},{5,7},{6,8},{7,9},{8,10},{9,11},{10,... | collective-permute-start | bytes 24584 | tf_op jit(solution)/shard_map/ppermute | solution.py:31
  218.9 34.2 %collective-permute-start.10 = (f32[8,256,128]{2,1,0:T(8,128)S(1)}, f32[8,256,128]{2,1,0:T(8,128)S(1)}, u32[]{:S(2)}, u32[]{:S(2)}) collective-permute-start(f32[8,256,128]{2,1,0:T(8,128)S(1)} %add_select_fusion.3), channel_id=1, source_target_pairs={{0,4},{1,5},{2,6},{3,7},{4,8},{5,9},{6,10},{7,11},{8,12},{9,13},{1... | collective-permute-start | bytes 3145736 | tf_op jit(solution)/shard_map/ppermute | solution.py:31
  223.6 27.6 %collective-permute-start.15 = (f32[8,256]{1,0:T(8,128)S(1)}, f32[8,256]{1,0:T(8,128)S(1)}, u32[]{:S(2)}, u32[]{:S(2)}) collective-permute-start(f32[8,256]{1,0:T(8,128)S(1)} %add_select_fusion.9), channel_id=1, source_target_pairs={{0,4},{1,5},{2,6},{3,7},{4,8},{5,9},{6,10},{7,11},{8,12},{9,13},{1... | collective-permute-start | bytes 24584 | tf_op jit(solution)/shard_map/ppermute | solution.py:31
  251.2 8.2 %collective-permute-start.16 = (f32[8,256]{1,0:T(8,128)S(1)}, f32[8,256]{1,0:T(8,128)S(1)}, u32[]{:S(2)}, u32[]{:S(2)}) collective-permute-start(f32[8,256]{1,0:T(8,128)S(1)} %add_select_fusion.8), channel_id=1, source_target_pairs={{0,8},{1,9},{2,10},{3,11},{4,12},{5,13},{6,14},{7,15},{8,16},{9,17... | collective-permute-start | bytes 24584 | tf_op jit(solution)/shard_map/ppermute | solution.py:31
  253.2 6.1 %copy-start.3 = (f32[8,256]{1,0:T(8,128)S(1)}, f32[8,256]{1,0:T(8,128)}, u32[]{:S(2)}) copy-start(f32[8,256]{1,0:T(8,128)} %param.13) | copy-start | bytes 24580
  253.2 47.7 %collective-permute-start.11 = (f32[8,256,128]{2,1,0:T(8,128)S(1)}, f32[8,256,128]{2,1,0:T(8,128)S(1)}, u32[]{:S(2)}, u32[]{:S(2)}) collective-permute-start(f32[8,256,128]{2,1,0:T(8,128)S(1)} %add_select_fusion.2), channel_id=1, source_target_pairs={{0,8},{1,9},{2,10},{3,11},{4,12},{5,13},{6,14},{7,15},{8,16},{9,17... | collective-permute-start | bytes 3145736 | tf_op jit(solution)/shard_map/ppermute | solution.py:31
  255.2 45.8 %copy-start.2 = (f32[8,256,128]{2,1,0:T(8,128)S(1)}, f32[8,256,128]{2,1,0:T(8,128)}, u32[]{:S(2)}) copy-start(f32[8,256,128]{2,1,0:T(8,128)} %param.12) | copy-start | bytes 3145732
where the time goes:
time: 306 us; the launch traced here: 305 us
  waiting for transfers between devices  142 us (46%)
  starting transfers between devices  55.2 us (18%)
  local copies, waits for them, and re-layouts  35.2 us (12%)
  blocking collectives  27 us (9%)
  loops' own time  20.4 us (7%)
  matrix products  14 us (5%)
  other arithmetic  6.06 us (2%)
  between operations  4.84 us (2%)
    ppermute x17, waiting for transfers between devices, shifted(): return lax.ppermute(block, axis, route)  142 us
    ppermute x17, starting transfers between devices, shifted(): return lax.ppermute(block, axis, route)  55.2 us
    unnamed x1, blocking collectives  27 us
    another operation x1, loops' own time, entering(): return lax.fori_loop(0, count - 1, hop, so_far)  20.4 us
    dynamic_slice x31, local copies, waits for them, and re-layouts, hop(): longer = join(so_far, pieces[position])  18.9 us
  transfers between devices with their start and end apart: 17, of which 11 were waited for; matrix products, arithmetic and copies ran while one was open for 14% of the time, Pallas kernels for 0%

commit v1 on v0

v1 whole, which is shorter than its diff:
```python
import functools

import jax
import jax.numpy as jnp
from jax import lax
from jax.experimental import pallas as pl
from jax.experimental.pallas import tpu as pltpu
from jax.sharding import PartitionSpec as P

H = 8
DH = 128
M = 256
TOK_DEV = 256
DRIFT = 96
CAP = 448
SHARDS = 32
DEVICES = 512
GROUP = 8
NETS = 64
TAIL = 112
AUG = 136
HB = 2
F32 = jnp.float32
BF16 = jnp.bfloat16
NT = (((1,), (1,)), ((), ()))


def dot(a, b):
    return jnp.dot(a, b, preferred_element_type=F32)


def dot_nt(a, b):
    return lax.dot_general(a, b, NT, preferred_element_type=F32)


def split(x):
    high = x.astype(BF16)
    return high, (x - high.astype(F32)).astype(BF16)


def tail_start(length):
    start = jnp.maximum(length - DRIFT, 0)
    return jnp.minimum(start - lax.rem(start, 16), CAP - TAIL)


def windows_kernel(length_ref, rows_ref, tail_ref, head_ref, sem):
    start = pl.multiple_of(tail_start(length_ref[0, 0]), 16)
    tail = pltpu.make_async_copy(rows_ref.at[pl.ds(start, TAIL), :], tail_ref, sem.at[0])
    head = pltpu.make_async_copy(rows_ref.at[pl.ds(0, DRIFT), :], head_ref, sem.at[1])
    tail.start()
    head.start()
    tail.wait()
    head.wait()


def windows(rows, length):
    return pl.pallas_call(
        windows_kernel,
        out_shape=(
            jax.ShapeDtypeStruct((TAIL, 3 * H * DH), BF16),
            jax.ShapeDtypeStruct((DRIFT, 3 * H * DH), BF16),
        ),
        in_specs=[pl.BlockSpec(memory_space=pltpu.SMEM), pl.BlockSpec(memory_space=pl.ANY)],
        out_specs=(pl.BlockSpec(memory_space=pl.ANY), pl.BlockSpec(memory_space=pl.ANY)),
        scratch_shapes=[pltpu.SemaphoreType.DMA((2,))],
        name="windows",
    )(length, rows)


def build_selection(lengths_ref, seq_index, own_ref, left_ref, right_ref):
    before = lax.fori_loop(0, seq_index, lambda i, s: s + lengths_ref[i], jnp.int32(0))
    length = lengths_ref[seq_index]
    length_left = lengths_ref[jnp.maximum(seq_index - 1, 0)]
    drift = before - seq_index * TOK_DEV

    def one_hot(width, shift, valid):
        row = lax.broadcasted_iota(jnp.int32, (TOK_DEV, width), 0) - drift
        column = lax.broadcasted_iota(jnp.int32, (TOK_DEV, width), 1)
        return jnp.where((column == row + shift) & valid(row), 1.0, 0.0).astype(BF16)

    own_ref[...] = one_hot(CAP, 0, lambda i: (i >= 0) & (i < length))
    left_ref[...] = one_hot(TAIL, length_left - tail_start(length_left), lambda i: i < 0)
    right_ref[...] = one_hot(DRIFT, -length, lambda i: i >= length)


def pick(selection, pieces):
    total = dot(selection[0][...], pieces[0])
    for one_hot, piece in zip(selection[1:], pieces[1:]):
        total = total + dot(one_hot[...], piece)
    return total


def feature_map_pair(map_ref, pair_ref):
    high, low = split(map_ref[...])
    pair_ref[:DH, :] = high
    pair_ref[DH:, :] = low


def features(part, pair_ref):
    scale = lax.rsqrt(jnp.mean(part * part, axis=-1, keepdims=True) + 1e-06) * DH ** (-0.5)
    twice = part.astype(BF16)
    return jnp.exp(dot(jnp.concatenate([twice, twice], axis=1), pair_ref[...]) * scale)


def state_kernel(
    lengths_ref, where_ref, map_ref, *refs
):
    parts, (out_ref, own, left, right, pair) = refs[:6], refs[6:]

    @pl.when(pl.program_id(0) == 0)
    def _():
        build_selection(lengths_ref, where_ref[0], own, left, right)
        feature_map_pair(map_ref, pair)

    first = where_ref[1]
    valid = lax.broadcasted_iota(jnp.int32, (TOK_DEV, 1), 0) >= first
    norm_rows = jnp.where(
        lax.broadcasted_iota(jnp.int32, (AUG - DH, TOK_DEV), 1) >= first, 1.0, 0.0
    ).astype(BF16)
    keys = pick((own, left, right), [parts[i][...] for i in (0, 2, 4)])
    values = pick((own, left, right), [parts[i][...] for i in (1, 3, 5)])
    for i in range(HB):
        columns = slice(i * DH, (i + 1) * DH)
        high, low = split(features(keys[:, columns], pair))
        masked = jnp.where(valid, values[:, columns], 0.0)
        turned = jnp.concatenate([masked.T.astype(BF16), norm_rows], axis=0)
        out_ref[i] = dot(turned, high) + dot(turned, low)


def part_specs(parts):
    specs = []
    for rows in (CAP, TAIL, DRIFT):
        for part in parts:
            specs.append(
                pl.BlockSpec((rows, HB * DH), lambda i, *_, part=part: (0, part * (H // HB) + i))
            )
    return specs


def selection_scratch():
    return [
        pltpu.VMEM((TOK_DEV, CAP), BF16),
        pltpu.VMEM((TOK_DEV, TAIL), BF16),
        pltpu.VMEM((TOK_DEV, DRIFT), BF16),
        pltpu.VMEM((2 * DH, M), BF16),
    ]


def local_states(lengths, where, feature_map, rows, from_left, from_right):
    return pl.pallas_call(
        state_kernel,
        out_shape=jax.ShapeDtypeStruct((H, AUG, M), F32),
        grid_spec=pltpu.PrefetchScalarGridSpec(
            num_scalar_prefetch=2,
            grid=(H // HB,),
            in_specs=[pl.BlockSpec((DH, M), lambda i, *_: (0, 0))] + part_specs((1, 2)),
            out_specs=pl.BlockSpec((HB, AUG, M), lambda i, *_: (i, 0, 0)),
            scratch_shapes=selection_scratch(),
        ),
        compiler_params=pltpu.CompilerParams(vmem_limit_bytes=32 << 20),
        name="local_states",
    )(lengths, where, feature_map, rows, rows, from_left, from_left, from_right, from_right)


def attention_kernel(lengths_ref, where_ref, begin_ref, map_ref, *refs):
    parts, rest = refs[:9], refs[9:]
    high_ref, low_ref, out_ref, own, left, right, pair = rest

    @pl.when(pl.program_id(0) == 0)
    def _():
        build_selection(lengths_ref, where_ref[0], own, left, right)
        feature_map_pair(map_ref, pair)

    query = lax.broadcasted_iota(jnp.int32, (TOK_DEV, TOK_DEV), 0)
    key = lax.broadcasted_iota(jnp.int32, (TOK_DEV, TOK_DEV), 1)
    allowed = (key <= query) & (key >= begin_ref[...])
    queries, keys, values = (
        pick((own, left, right), [parts[i][...] for i in (j, j + 3, j + 6)]) for j in range(3)
    )
    for i in range(HB):
        columns = slice(i * DH, (i + 1) * DH)
        q_high, q_low = split(features(queries[:, columns], pair))
        k_high, k_low = split(features(keys[:, columns], pair))
        high_ref[i] = q_high
        low_ref[i] = q_low
        scores = dot_nt(q_high, k_high) + dot_nt(q_high, k_low) + dot_nt(q_low, k_high)
        s_high, s_low = split(jnp.where(allowed, scores, 0.0))
        value = jnp.concatenate(
            [values[:, columns].astype(BF16), jnp.ones((TOK_DEV, DH), BF16)], axis=1
        )
        out_ref[i] = dot(s_high, value) + dot(s_low, value)


def local_attention(lengths, where, begin, feature_map, rows, from_left, from_right):
    by_head = pl.BlockSpec((HB, TOK_DEV, M), lambda i, *_: (i, 0, 0))
    return pl.pallas_call(
        attention_kernel,
        out_shape=(
            jax.ShapeDtypeStruct((H, TOK_DEV, M), BF16),
            jax.ShapeDtypeStruct((H, TOK_DEV, M), BF16),
            jax.ShapeDtypeStruct((H, TOK_DEV, 2 * DH), F32),
        ),
        grid_spec=pltpu.PrefetchScalarGridSpec(
            num_scalar_prefetch=2,
            grid=(H // HB,),
            in_specs=[
                pl.BlockSpec((TOK_DEV, 1), lambda i, *_: (0, 0)),
                pl.BlockSpec((DH, M), lambda i, *_: (0, 0)),
            ]
            + part_specs((0, 1, 2)),
            out_specs=(by_head, by_head, by_head),
            scratch_shapes=selection_scratch(),
        ),
        compiler_params=pltpu.CompilerParams(vmem_limit_bytes=48 << 20),
        cost_estimate=pl.CostEstimate(
            flops=6_000_000_000, transcendentals=1_000_000, bytes_accessed=8_000_000
        ),
        name="local_attention",
    )(lengths, where, begin, feature_map, *([rows] * 3), *([from_left] * 3), *([from_right] * 3))


def tail_kernel(where_ref, states_ref, out_ref):
    restart = [where_ref[4 + j] for j in range(GROUP)]
    total = states_ref[0]
    for j in range(1, GROUP):
        keep = restart[j] == 0
        total = jnp.where(keep, total, 0.0) + states_ref[j]
    out_ref[...] = total


def group_tail(where, states):
    return pl.pallas_call(
        tail_kernel,
        out_shape=jax.ShapeDtypeStruct((AUG, M), F32),
        in_specs=[pl.BlockSpec(memory_space=pltpu.SMEM), pl.BlockSpec(memory_space=pltpu.VMEM)],
        out_specs=pl.BlockSpec(memory_space=pltpu.VMEM),
        name="group_tail",
    )(where, states)


def prefix_kernel(
    where_ref, states_ref, near_ref, far_ref, state_ref, norm_ref, out_ref, running
):
    running[...] = near_ref[...] + jnp.where(where_ref[2] == 0, far_ref[...], 0.0)

    @pl.when(where_ref[3] != 0)
    def _():
        running[:DH, :] += state_ref[0].T
        running[DH:, :] += jnp.broadcast_to(norm_ref[0], (AUG - DH, M))

    total = running[...]
    for j in range(GROUP):
        out_ref[j] = total
        total = jnp.where(where_ref[4 + j] == 0, total, 0.0) + states_ref[j]


def entering_states(where, states, near, far, carried_state, carried_norm):
    whole = lambda *shape: pl.BlockSpec(shape, lambda i, *_: (0,) * len(shape))
    return pl.pallas_call(
        prefix_kernel,
        out_shape=jax.ShapeDtypeStruct((GROUP, AUG, M), F32),
        grid_spec=pltpu.PrefetchScalarGridSpec(
            num_scalar_prefetch=1,
            grid=(1,),
            in_specs=[
                whole(GROUP, AUG, M),
                whole(AUG, M),
                whole(AUG, M),
                pl.BlockSpec((1, M, DH), lambda i, where: (where[12], 0, 0)),
                pl.BlockSpec((1, 1, M), lambda i, where: (where[12], 0, 0)),
            ],
            out_specs=whole(GROUP, AUG, M),
            scratch_shapes=[pltpu.VMEM((AUG, M), F32)],
        ),
        name="entering_states",
    )(where, states, near, far, carried_state, carried_norm.reshape(H, 1, M))


def finish_kernel(begin_ref, state_ref, high_ref, low_ref, local_ref, out_ref):
    carried = begin_ref[...] < 0
    for i in range(HB):
        state = jnp.concatenate(
            [state_ref[i, :DH, :], jnp.broadcast_to(state_ref[i, DH : DH + 1, :], (DH, M))], axis=0
        )
        s_high, s_low = split(state)
        q_high = high_ref[i]
        entering = dot_nt(q_high, s_high) + dot_nt(q_high, s_low) + dot_nt(low_ref[i], s_high)
        total = local_ref[i] + jnp.where(carried, entering, 0.0)
        out_ref[:, i * DH : (i + 1) * DH] = total[:, :DH] / total[:, DH:]


def finish(begin, states, high, low, local_sums):
    by_head = pl.BlockSpec((HB, TOK_DEV, M), lambda i: (i, 0, 0))
    return pl.pallas_call(
        finish_kernel,
        out_shape=jax.ShapeDtypeStruct((TOK_DEV, H * DH), F32),
        grid=(H // HB,),
        in_specs=[
            pl.BlockSpec((TOK_DEV, 1), lambda i: (0, 0)),
            pl.BlockSpec((HB, AUG, M), lambda i: (i, 0, 0)),
            by_head,
            by_head,
            by_head,
        ],
        out_specs=pl.BlockSpec((TOK_DEV, HB * DH), lambda i: (0, i)),
        compiler_params=pltpu.CompilerParams(vmem_limit_bytes=32 << 20),
        name="finish",
    )(begin, states, high, low, local_sums)


def shifted(block, axis, count, distance):
    return lax.ppermute(block, axis, [(i - distance, i) for i in range(distance, count)])


def local(loader_rows, loader_lengths, net_lengths, feature_map, carried_state, carried_norm):
    seq_index = lax.axis_index("seq")
    device = lax.axis_index("grp") * SHARDS + seq_index
    start = device * TOK_DEV
    groups = [list(range(i, i + GROUP)) for i in range(0, SHARDS, GROUP)]

    tail_rows, head_rows = windows(loader_rows, loader_lengths)
    from_left = shifted(tail_rows, "seq", SHARDS, 1)
    from_right = lax.ppermute(head_rows, "seq", [(i + 1, i) for i in range(SHARDS - 1)])
    lengths = lax.all_to_all(
        jnp.broadcast_to(loader_lengths.reshape(1), (SHARDS,)), "seq", 0, 0, tiled=True
    )

    begins = jnp.cumsum(net_lengths) - net_lengths
    begins = jnp.where(jnp.arange(NETS) == 0, -1, begins).astype(jnp.int32)
    positions = start + jnp.arange(TOK_DEV, dtype=jnp.int32)
    net_begin = jnp.max(jnp.where(begins[None, :] <= positions[:, None], begins[None, :], -1), axis=1)
    begin = (net_begin - start).astype(jnp.int32)[:, None]
    last_begin = jnp.max(jnp.where(begins < start + TOK_DEV, begins, -1)) - start
    group_start = (device // GROUP) * GROUP
    member = group_start + jnp.arange(GROUP, dtype=jnp.int32)
    restarts = begins // TOK_DEV
    real = jnp.arange(NETS) > 0
    restart = jnp.any((restarts[None, :] == member[:, None]) & real[None, :], axis=1)
    nearby = real & (restarts >= group_start - GROUP) & (restarts < group_start)
    earlier = real & (restarts < group_start)
    where = jnp.concatenate(
        [
            jnp.stack(
                [
                    seq_index,
                    last_begin,
                    jnp.any(nearby).astype(jnp.int32),
                    1 - jnp.any(earlier).astype(jnp.int32),
                ]
            ),
            restart.astype(jnp.int32),
            lax.rem(seq_index, GROUP)[None],
        ]
    ).astype(jnp.int32)

    states = local_states(lengths, where, feature_map, loader_rows, from_left, from_right)
    states = lax.all_to_all(states, "seq", 0, 0, axis_index_groups=groups, tiled=True)
    high, low, sums = local_attention(
        lengths, where, begin, feature_map, loader_rows, from_left, from_right
    )
    states = states.reshape(GROUP, AUG, M)
    tail = group_tail(where, states)
    near = shifted(tail, ("grp", "seq"), DEVICES, GROUP)
    far = shifted(tail, ("grp", "seq"), DEVICES, 2 * GROUP)
    states = entering_states(where, states, near, far, carried_state, carried_norm)
    states = lax.all_to_all(states, "seq", 0, 0, axis_index_groups=groups, tiled=True)
    return finish(begin, states, high, low, sums)


def solution(mesh):
    in_specs = (P(("grp", "seq"), None), P("grp", "seq"), P(), P(), P(), P())
    out_specs = P(("grp", "seq"), None)
    return jax.shard_map(local, mesh=mesh, in_specs=in_specs, out_specs=out_specs, check_vma=False)
```

time: 306 us -> 146 us (0.48)
  the two profiles are of different devices: /device:TPU:37 before, /device:TPU:32 now
where the time goes in v1:
time: 146 us
  Pallas kernels  62 us (42%)
  starting transfers between devices  30.3 us (21%)
  blocking collectives  20.3 us (14%)
  waiting for transfers between devices  19.7 us (13%)
  local copies, waits for them, and re-layouts  8.24 us (6%)
  between operations  2.8 us (2%)
  other arithmetic  2.53 us (2%)
    pallas_call x1, Pallas kernels, windows(): pl.pallas_call(windows_kernel, out_shape=(jax.ShapeDtypeStruct((TAIL, 3 *...  39.8 us
    all_to_all x1, blocking collectives, local(): lax.all_to_all(states, 'seq', 0, 0, axis_index_groups=groups, tiled=True)  20.3 us
    all_to_all x1, starting transfers between devices, local(): lax.all_to_all(jnp.broadcast_to(loader_lengths.reshape(1), (SHARDS,)), 's...  15.1 us
    ppermute x3, starting transfers between devices, shifted(): lax.ppermute(block, axis, [(i - distance, i) for i in range(distance, cou...  10.2 us
    ppermute x3, waiting for transfers between devices, shifted(): lax.ppermute(block, axis, [(i - distance, i) for i in range(distance, cou...  9.86 us
    pallas_call x1, Pallas kernels, local_attention(): pl.pallas_call(attention_kernel, out_shape=(jax.ShapeDtypeStruct((H, TOK_...  9.18 us
    unnamed x26, local copies, waits for them, and re-layouts  6.71 us
    all_to_all x1, waiting for transfers between devices, local(): lax.all_to_all(jnp.broadcast_to(loader_lengths.reshape(1), (SHARDS,)), 's...  5.79 us
  transfers between devices with their start and end apart: 6, of which 4 were waited for; matrix products, arithmetic and copies ran while one was open for 3% of the time, Pallas kernels for 6%

profile of v1, /device:TPU:32, one launch (start us, length us, event | category | flops | bytes accessed | tf_op | source)
XLA Modules:
  0.0 145.9 jit_solution(17248151699277189302)
XLA Ops:
  0.7 39.8 %windows.1 = (bf16[112,3072]{1,0:T(8,128)(2,1)}, bf16[96,3072]{1,0:T(8,128)(2,1)}) custom-call(s32[1,1]{1,0:T(1,128)} %copy.20.length_ref, bf16[448,3072]{1,0:T(8,128)(2,1)} %refs_2_.1), custom_call_target="tpu_custom_call" | custom-call | tf_op jit(solution)/shard_map/windows/pallas_call | solution.py:57
  40.5 3.4 %collective-permute-start = (bf16[112,3072]{1,0:T(8,128)(2,1)}, bf16[112,3072]{1,0:T(8,128)(2,1)S(1)}, u32[]{:S(2)}, u32[]{:S(2)}) collective-permute-start(bf16[112,3072]{1,0:T(8,128)(2,1)} %get-tuple-element.10), channel_id=1, source_target_pairs={{0,1},{1,2},{2,3},{3,4},{4,5},{5,6},{6,7},{7,8},{8,9},{9,10},{10,1... | collective-permute-start | bytes 2064392 | tf_op jit(solution)/shard_map/ppermute | solution.py:312
  44.0 1.3 collective-permute-start.1
  45.3 0.6 broadcast_in_dim.37
  45.9 15.1 %all-to-all-start = ((s32[32,1,1]{2,1,0:T(1,128)}), s32[32,1,1]{2,1,0:T(1,128)S(1)}, u32[]{:S(2)}, u32[]{:S(2)}) async-start(s32[32,1,1]{2,1,0:T(1,128)} %broadcast_in_dim.37), calls=%async_computation | async-start | bytes 32768 | tf_op jit(solution)/shard_map/all_to_all | solution.py:324
  61.0 0.1 copy.17
  61.2 0.1 reduce
  61.3 0.7 and_reduce_fusion.1
  63.3 0.7 fusion
  64.6 0.2 and_reduce_fusion
  64.9 5.8 %all-to-all-done = s32[32,1,1]{2,1,0:T(1,128)S(1)} async-done(((s32[32,1,1]{2,1,0:T(1,128)}), s32[32,1,1]{2,1,0:T(1,128)S(1)}, u32[]{:S(2)}, u32[]{:S(2)}) %all-to-all-start) | async-done | bytes 160 | tf_op jit(solution)/shard_map/all_to_all | solution.py:324
  70.7 0.7 reduce.1.lengths_ref
  71.4 0.9 copy-done.5
  72.3 5.2 %local_states.1 = f32[8,136,256]{2,1,0:T(8,128)S(1)} custom-call(s32[32]{0:T(128)S(1)} %reduce.1.lengths_ref, s32[13]{0:T(128)S(1)} %concatenate.3.where_ref, f32[128,256]{1,0:T(8,128)S(1)} %copy-done.5, bf16[448,3072]{1,0:T(8,128)(2,1)S(1)} %copy-done, bf16[448,3072]{1,0:T(8,128)(2,1)S(1)} %copy-done, ...), custom_call_target="tpu_custom_call" | custom-call | tf_op jit(solution)/shard_map/local_states/pallas_call | solution.py:150
  77.5 20.3 %all_to_all.18.states_ref = f32[8,136,256]{2,1,0:T(8,128)} all-to-all(f32[8,136,256]{2,1,0:T(8,128)S(1)} %local_states.1), channel_id=1, replica_groups={{0,1,2,3,4,5,6,7},{8,9,10,11,12,13,14,15},{16,17,18,19,20,21,22,23},{24..., dimensions={0} | all-to-all | bytes 2228224 | tf_op jit(solution)/shard_map/all_to_all | solution.py:357
  97.8 2.0 %group_tail.1 = f32[136,256]{1,0:T(8,128)} custom-call(s32[13]{0:T(128)} %copy-done.7, f32[8,136,256]{2,1,0:T(8,128)} %all_to_all.18.states_ref), custom_call_target="tpu_custom_call" | custom-call | tf_op jit(solution)/shard_map/group_tail/pallas_call | solution.py:232
  99.8 4.2 %collective-permute-start.3 = (f32[136,256]{1,0:T(8,128)}, f32[136,256]{1,0:T(8,128)S(1)}, u32[]{:S(2)}, u32[]{:S(2)}) collective-permute-start(f32[136,256]{1,0:T(8,128)} %group_tail.1), channel_id=1, source_target_pairs={{0,16},{1,17},{2,18},{3,19},{4,20},{5,21},{6,22},{7,23},{8,24},{9,... | collective-permute-start | bytes 417800 | tf_op jit(solution)/shard_map/ppermute | solution.py:312
  104.0 2.6 %collective-permute-start.2 = (f32[136,256]{1,0:T(8,128)}, f32[136,256]{1,0:T(8,128)S(1)}, u32[]{:S(2)}, u32[]{:S(2)}) collective-permute-start(f32[136,256]{1,0:T(8,128)} %group_tail.1), channel_id=1, source_target_pairs={{0,8},{1,9},{2,10},{3,11},{4,12},{5,13},{6,14},{7,15},{8,16},{9,17... | collective-permute-start | bytes 417800 | tf_op jit(solution)/shard_map/ppermute | solution.py:312
  106.6 0.6 reshape.58.norm_ref
  107.2 7.7 %collective-permute-done.3.far_ref = f32[136,256]{1,0:T(8,128)S(1)} collective-permute-done((f32[136,256]{1,0:T(8,128)}, f32[136,256]{1,0:T(8,128)S(1)}, u32[]{:S(2)}, u32[]{:S(2)}) %collective-permute-start.3) | collective-permute-done | bytes 139296 | tf_op jit(solution)/shard_map/ppermute | solution.py:312
  114.9 2.1 %collective-permute-done.2.near_ref = f32[136,256]{1,0:T(8,128)S(1)} collective-permute-done((f32[136,256]{1,0:T(8,128)}, f32[136,256]{1,0:T(8,128)S(1)}, u32[]{:S(2)}, u32[]{:S(2)}) %collective-permute-start.2) | collective-permute-done | bytes 139296 | tf_op jit(solution)/shard_map/ppermute | solution.py:312
  117.1 0.7 copy-done.10
  117.7 3.2 %entering_states.1 = f32[8,136,256]{2,1,0:T(8,128)} custom-call(s32[13]{0:T(128)} %copy-done.7, f32[8,136,256]{2,1,0:T(8,128)} %all_to_all.18.states_ref, f32[136,256]{1,0:T(8,128)} %copy-done.10, f32[136,256]{1,0:T(8,128)} %copy-done.9, f32[8,256,128]{2,1,0:T(8,128)} %state_ref.1, f32[8,1,256]{2,1,0:T(1,128)} %reshape.58.norm_ref), custom_call_target="tpu_custom_call" | custom-call | tf_op jit(solution)/shard_map/entering_states/pallas_call | solution.py:259
  120.9 3.7 %all-to-all-start.2 = ((f32[8,136,256]{2,1,0:T(8,128)}), f32[8,136,256]{2,1,0:T(8,128)S(1)}, u32[]{:S(2)}, u32[]{:S(2)}) async-start(f32[8,136,256]{2,1,0:T(8,128)} %entering_states.1), calls=%async_computation.2 | async-start | bytes 2228224 | tf_op jit(solution)/shard_map/all_to_all | solution.py:366
  124.7 0.1 copy.19.begin_ref
  124.9 9.2 %local_attention.1 = (bf16[8,256,256]{2,1,0:T(8,128)(2,1)S(1)}, bf16[8,256,256]{2,1,0:T(8,128)(2,1)S(1)}, f32[8,256,256]{2,1,0:T(8,128)S(1)}) custom-call(s32[32]{0:T(128)S(1)} %reduce.1.lengths_ref, s32[13]{0:T(128)S(1)} %copy-done.8, s32[256,1]{1,0:T(8,128)S(1)} %copy.19.begin_ref, f32[128,256]{1,0:T(8,128)S(1)} %copy-done.6, bf16[448,3072]{1,0:T(8,128)(2,1)} %refs_2_.1, ...), custom_call_target="tpu_custom_call" | custom-call | flops 6000000000 | bytes 8000000 | tf_op jit(solution)/shard_map/local_attention/pallas_call | solution.py:196
  134.1 1.3 copy-done.1
  135.4 1.0 copy-done.3
  136.4 4.0 %all-to-all-done.2.state_ref = f32[8,136,256]{2,1,0:T(8,128)S(1)} async-done(((f32[8,136,256]{2,1,0:T(8,128)}), f32[8,136,256]{2,1,0:T(8,128)S(1)}, u32[]{:S(2)}, u32[]{:S(2)}) %all-to-all-start.2) | async-done | bytes 1114144 | tf_op jit(solution)/shard_map/all_to_all | solution.py:366
  140.4 1.6 %copy-done.2 = f32[8,256,256]{2,1,0:T(8,128)S(1)} copy-done((f32[8,256,256]{2,1,0:T(8,128)S(1)}, f32[8,256,256]{2,1,0:T(8,128)}, u32[]{:S(2)}) %copy-start.2) | copy-done | bytes 2097176
  142.0 1.2 copy-done.4
  143.2 2.7 %finish.1 = f32[256,1024]{1,0:T(8,128)} custom-call(s32[256,1]{1,0:T(8,128)S(1)} %copy.19.begin_ref, f32[8,136,256]{2,1,0:T(8,128)S(1)} %all-to-all-done.2.state_ref, bf16[8,256,256]{2,1,0:T(8,128)(2,1)S(1)} %get-tuple-element.12.high_ref, bf16[8,256,256]{2,1,0:T(8,128)(2,1)S(1)} %copy-done.4, f32[8,256,256]{2,1,0:T(8,128)S(1)} %copy-done.2), custom_call_target="tpu_custom_call" | custom-call | tf_op jit(solution)/shard_map/finish/pallas_call | solution.py:294
  (29 shorter events, 0.3 us)
Async XLA Ops:
  0.7 60.4 %copy-start.12 = (s32[64]{0:T(128)S(1)}, s32[64]{0:T(128)}, u32[]{:S(2)}) copy-start(s32[64]{0:T(128)} %param.8) | copy-start | bytes 772
  0.7 70.7 %copy-start = (bf16[448,3072]{1,0:T(8,128)(2,1)S(1)}, bf16[448,3072]{1,0:T(8,128)(2,1)}, u32[]{:S(2)}) copy-start(bf16[448,3072]{1,0:T(8,128)(2,1)} %refs_2_.1) | copy-start | bytes 8257540
  40.5 30.8 %collective-permute-start = (bf16[112,3072]{1,0:T(8,128)(2,1)}, bf16[112,3072]{1,0:T(8,128)(2,1)S(1)}, u32[]{:S(2)}, u32[]{:S(2)}) collective-permute-start(bf16[112,3072]{1,0:T(8,128)(2,1)} %get-tuple-element.10), channel_id=1, source_target_pairs={{0,1},{1,2},{2,3},{3,4},{4,5},{5,6},{6,7},{7,8},{8,9},{9,10},{10,1... | collective-permute-start | bytes 2064392 | tf_op jit(solution)/shard_map/ppermute | solution.py:312
  44.0 27.4 %collective-permute-start.1 = (bf16[96,3072]{1,0:T(8,128)(2,1)}, bf16[96,3072]{1,0:T(8,128)(2,1)}, u32[]{:S(2)}, u32[]{:S(2)}) collective-permute-start(bf16[96,3072]{1,0:T(8,128)(2,1)} %get-tuple-element.11), channel_id=1, source_target_pairs={{1,0},{2,1},{3,2},{4,3},{5,4},{6,5},{7,6},{8,7},{9,8},{10,9},{11,1... | collective-permute-start | bytes 1769480 | tf_op jit(solution)/shard_map/ppermute | solution.py:323
  45.9 24.8 %all-to-all-start = ((s32[32,1,1]{2,1,0:T(1,128)}), s32[32,1,1]{2,1,0:T(1,128)S(1)}, u32[]{:S(2)}, u32[]{:S(2)}) async-start(s32[32,1,1]{2,1,0:T(1,128)} %broadcast_in_dim.37), calls=%async_computation | async-start | bytes 32768 | tf_op jit(solution)/shard_map/all_to_all | solution.py:324
  64.9 12.6 %copy-start.7 = (s32[13]{0:T(128)}, s32[13]{0:T(128)S(1)}, u32[]{:S(2)}) copy-start(s32[13]{0:T(128)S(1)} %concatenate.3.where_ref) | copy-start | bytes 160
  71.4 0.9 copy-start.5
  97.8 8.8 %copy-start.11 = (f32[8,256]{1,0:T(8,128)S(1)}, f32[8,256]{1,0:T(8,128)}, u32[]{:S(2)}) copy-start(f32[8,256]{1,0:T(8,128)} %param.11) | copy-start | bytes 24580
  99.8 15.2 %collective-permute-start.3 = (f32[136,256]{1,0:T(8,128)}, f32[136,256]{1,0:T(8,128)S(1)}, u32[]{:S(2)}, u32[]{:S(2)}) collective-permute-start(f32[136,256]{1,0:T(8,128)} %group_tail.1), channel_id=1, source_target_pairs={{0,16},{1,17},{2,18},{3,19},{4,20},{5,21},{6,22},{7,23},{8,24},{9,... | collective-permute-start | bytes 417800 | tf_op jit(solution)/shard_map/ppermute | solution.py:312
  104.0 13.0 %collective-permute-start.2 = (f32[136,256]{1,0:T(8,128)}, f32[136,256]{1,0:T(8,128)S(1)}, u32[]{:S(2)}, u32[]{:S(2)}) collective-permute-start(f32[136,256]{1,0:T(8,128)} %group_tail.1), channel_id=1, source_target_pairs={{0,8},{1,9},{2,10},{3,11},{4,12},{5,13},{6,14},{7,15},{8,16},{9,17... | collective-permute-start | bytes 417800 | tf_op jit(solution)/shard_map/ppermute | solution.py:312
  114.9 2.1 %copy-start.9 = (f32[136,256]{1,0:T(8,128)}, f32[136,256]{1,0:T(8,128)S(1)}, u32[]{:S(2)}) copy-start(f32[136,256]{1,0:T(8,128)S(1)} %collective-permute-done.3.far_ref) | copy-start | bytes 417796
  117.1 0.7 copy-start.10
  120.9 4.0 %copy-start.6 = (f32[128,256]{1,0:T(8,128)S(1)}, f32[128,256]{1,0:T(8,128)}, u32[]{:S(2)}) copy-start(f32[128,256]{1,0:T(8,128)} %map_ref.3) | copy-start | bytes 393220
  120.9 4.0 %copy-start.8 = (s32[13]{0:T(128)S(1)}, s32[13]{0:T(128)}, u32[]{:S(2)}) copy-start(s32[13]{0:T(128)} %copy-done.7) | copy-start | bytes 160
  120.9 19.5 %all-to-all-start.2 = ((f32[8,136,256]{2,1,0:T(8,128)}), f32[8,136,256]{2,1,0:T(8,128)S(1)}, u32[]{:S(2)}, u32[]{:S(2)}) async-start(f32[8,136,256]{2,1,0:T(8,128)} %entering_states.1), calls=%async_computation.2 | async-start | bytes 2228224 | tf_op jit(solution)/shard_map/all_to_all | solution.py:366
  134.1 1.3 copy-start.1
  135.4 1.0 copy-start.3
  140.4 1.6 %copy-start.2 = (f32[8,256,256]{2,1,0:T(8,128)S(1)}, f32[8,256,256]{2,1,0:T(8,128)}, u32[]{:S(2)}) copy-start(f32[8,256,256]{2,1,0:T(8,128)} %copy-done.1) | copy-start | bytes 6291460
  142.0 1.2 copy-start.4

commit v2 on v1

--- a/solution.py
+++ b/solution.py
@@ -17,9 +17,10 @@
 DEVICES = 512
 GROUP = 8
 NETS = 64
-TAIL = 112
+TAIL = 104
 AUG = 136
 HB = 2
+HALF = M // 2
 F32 = jnp.float32
 BF16 = jnp.bfloat16
 NT = (((1,), (1,)), ((), ()))
@@ -40,11 +41,11 @@
 
 def tail_start(length):
     start = jnp.maximum(length - DRIFT, 0)
-    return jnp.minimum(start - lax.rem(start, 16), CAP - TAIL)
+    return jnp.minimum(start - lax.rem(start, 8), CAP - TAIL)
 
 
 def windows_kernel(length_ref, rows_ref, tail_ref, head_ref, sem):
-    start = pl.multiple_of(tail_start(length_ref[0, 0]), 16)
+    start = pl.multiple_of(tail_start(length_ref[0, 0]), 8)
     tail = pltpu.make_async_copy(rows_ref.at[pl.ds(start, TAIL), :], tail_ref, sem.at[0])
     head = pltpu.make_async_copy(rows_ref.at[pl.ds(0, DRIFT), :], head_ref, sem.at[1])
     tail.start()
@@ -61,7 +62,7 @@
             jax.ShapeDtypeStruct((DRIFT, 3 * H * DH), BF16),
         ),
         in_specs=[pl.BlockSpec(memory_space=pltpu.SMEM), pl.BlockSpec(memory_space=pl.ANY)],
-        out_specs=(pl.BlockSpec(memory_space=pl.ANY), pl.BlockSpec(memory_space=pl.ANY)),
+        out_specs=(pl.BlockSpec(memory_space=pltpu.VMEM), pl.BlockSpec(memory_space=pltpu.VMEM)),
         scratch_shapes=[pltpu.SemaphoreType.DMA((2,))],
         name="windows",
     )(length, rows)
@@ -246,7 +247,7 @@
     @pl.when(where_ref[3] != 0)
     def _():
         running[:DH, :] += state_ref[0].T
-        running[DH:, :] += jnp.broadcast_to(norm_ref[0], (AUG - DH, M))
+        running[DH:, :] += jnp.broadcast_to(norm_ref[0], (AUG - DH, HALF))
 
     total = running[...]
     for j in range(GROUP):
@@ -255,22 +256,23 @@
 
 
 def entering_states(where, states, near, far, carried_state, carried_norm):
-    whole = lambda *shape: pl.BlockSpec(shape, lambda i, *_: (0,) * len(shape))
+    by_group = pl.BlockSpec((GROUP, AUG, HALF), lambda i, where: (0, 0, i))
+    one = pl.BlockSpec((AUG, HALF), lambda i, where: (0, i))
     return pl.pallas_call(
         prefix_kernel,
         out_shape=jax.ShapeDtypeStruct((GROUP, AUG, M), F32),
         grid_spec=pltpu.PrefetchScalarGridSpec(
             num_scalar_prefetch=1,
-            grid=(1,),
+            grid=(M // HALF,),
             in_specs=[
-                whole(GROUP, AUG, M),
-                whole(AUG, M),
-                whole(AUG, M),
-                pl.BlockSpec((1, M, DH), lambda i, where: (where[12], 0, 0)),
-                pl.BlockSpec((1, 1, M), lambda i, where: (where[12], 0, 0)),
+                by_group,
+                one,
+                one,
+                pl.BlockSpec((1, HALF, DH), lambda i, where: (where[12], i, 0)),
+                pl.BlockSpec((1, 1, HALF), lambda i, where: (where[12], 0, i)),
             ],
-            out_specs=whole(GROUP, AUG, M),
-            scratch_shapes=[pltpu.VMEM((AUG, M), F32)],
+            out_specs=by_group,
+            scratch_shapes=[pltpu.VMEM((AUG, HALF), F32)],
         ),
         name="entering_states",
     )(where, states, near, far, carried_state, carried_norm.reshape(H, 1, M))
@@ -358,7 +360,7 @@
     high, low, sums = local_attention(
         lengths, where, begin, feature_map, loader_rows, from_left, from_right
     )
-    states = states.reshape(GROUP, AUG, M)
+    states, high, low, sums = lax.optimization_barrier((states, high, low, sums))
     tail = group_tail(where, states)
     near = shifted(tail, ("grp", "seq"), DEVICES, GROUP)
     far = shifted(tail, ("grp", "seq"), DEVICES, 2 * GROUP)

time: 146 us -> 108 us (0.74)
  the two profiles are of different devices: /device:TPU:32 before, /device:TPU:33 now
where the time goes in v2:
time: 108 us; the launch traced here: 107 us
  starting transfers between devices  32.6 us (30%)
  blocking collectives  27.6 us (26%)
  Pallas kernels  24.4 us (23%)
  waiting for transfers between devices  8.24 us (8%)
  local copies, waits for them, and re-layouts  6.47 us (6%)
  other arithmetic  5.18 us (5%)
  between operations  2.8 us (3%)
    all_to_all x1, blocking collectives, local(): lax.all_to_all(states, 'seq', 0, 0, axis_index_groups=groups, tiled=True)  27.6 us
    all_to_all x1, starting transfers between devices, local(): lax.all_to_all(jnp.broadcast_to(loader_lengths.reshape(1), (SHARDS,)), 's...  14.7 us
    ppermute x3, starting transfers between devices, shifted(): lax.ppermute(block, axis, [(i - distance, i) for i in range(distance, cou...  11.3 us
    pallas_call x1, Pallas kernels, local_attention(): pl.pallas_call(attention_kernel, out_shape=(jax.ShapeDtypeStruct((H, TOK_...  9.18 us
    ppermute x3, waiting for transfers between devices, shifted(): lax.ppermute(block, axis, [(i - distance, i) for i in range(distance, cou...  6.35 us
    all_to_all x1, starting transfers between devices, local(): lax.all_to_all(states, 'seq', 0, 0, axis_index_groups=groups, tiled=True)  5.4 us
    pallas_call x1, Pallas kernels, local_states(): pl.pallas_call(state_kernel, out_shape=jax.ShapeDtypeStruct((H, AUG, M),...  5.18 us
    unnamed x22, local copies, waits for them, and re-layouts  3.69 us
  transfers between devices with their start and end apart: 6, of which 4 were waited for; matrix products, arithmetic and copies ran while one was open for 7% of the time, Pallas kernels for 9%

profile of v2, /device:TPU:33, one launch (start us, length us, event | category | flops | bytes accessed | tf_op | source)
XLA Modules:
  0.0 107.3 jit_solution(1265462420453980945)
XLA Ops:
  0.7 2.5 %windows.1 = (bf16[104,3072]{1,0:T(8,128)(2,1)}, bf16[96,3072]{1,0:T(8,128)(2,1)}) custom-call(s32[1,1]{1,0:T(1,128)} %copy.20.length_ref, bf16[448,3072]{1,0:T(8,128)(2,1)} %refs_2_.1), custom_call_target="tpu_custom_call" | custom-call | tf_op jit(solution)/shard_map/windows/pallas_call | solution.py:58
  3.1 3.2 %collective-permute-start = (bf16[104,3072]{1,0:T(8,128)(2,1)}, bf16[104,3072]{1,0:T(8,128)(2,1)S(1)}, u32[]{:S(2)}, u32[]{:S(2)}) collective-permute-start(bf16[104,3072]{1,0:T(8,128)(2,1)} %get-tuple-element.14), channel_id=1, source_target_pairs={{0,1},{1,2},{2,3},{3,4},{4,5},{5,6},{6,7},{7,8},{8,9},{9,10},{10,1... | collective-permute-start | bytes 1916936 | tf_op jit(solution)/shard_map/ppermute | solution.py:314
  6.3 1.3 %collective-permute-start.1 = (bf16[96,3072]{1,0:T(8,128)(2,1)}, bf16[96,3072]{1,0:T(8,128)(2,1)}, u32[]{:S(2)}, u32[]{:S(2)}) collective-permute-start(bf16[96,3072]{1,0:T(8,128)(2,1)} %get-tuple-element.15), channel_id=1, source_target_pairs={{1,0},{2,1},{3,2},{4,3},{5,4},{6,5},{7,6},{8,7},{9,8},{10,9},{11,1... | collective-permute-start | bytes 1769480 | tf_op jit(solution)/shard_map/ppermute | solution.py:325
  7.6 0.6 broadcast_in_dim.37
  8.2 14.7 %all-to-all-start = ((s32[32,1,1]{2,1,0:T(1,128)}), s32[32,1,1]{2,1,0:T(1,128)}, u32[]{:S(2)}, u32[]{:S(2)}) async-start(s32[32,1,1]{2,1,0:T(1,128)} %broadcast_in_dim.37), calls=%async_computation | async-start | bytes 32768 | tf_op jit(solution)/shard_map/all_to_all | solution.py:326
  22.9 1.3 %copy.17 = s32[64,1]{1,0:T(8,128)} copy(s32[64,1]{0,1:T(1,128)} %bitcast.10) | data formatting | bytes 512 | tf_op jit(solution)/shard_map/reshape.44
  24.3 0.9 reduce-window.9
  25.1 0.6 reduce
  25.7 1.4 %and_reduce_fusion.1 = (pred[]{:T(512)}, pred[]{:T(512)}, s32[64]{0:T(128)S(1)}, s32[64]{0:T(128)S(1)}, pred[64]{0:T(512)(128)(4,1)S(1)}) fusion(s32[]{:T(128)S(6)} %mul.11, s32[]{:T(128)S(6)} %sub.42, s32[64]{0:T(128)} %reduce, s32[64]{0:T(128)} %param.8), kind=kLoop, calls=%fused_computation.3 | loop fusion | flops 1662 | bytes 1098 | tf_op jit(solution)/shard_map/reduce_or | solution.py:350
  28.4 0.7 fusion
  29.7 0.2 and_reduce_fusion
  30.0 1.4 %all-to-all-done = s32[32,1,1]{2,1,0:T(1,128)} async-done(((s32[32,1,1]{2,1,0:T(1,128)}), s32[32,1,1]{2,1,0:T(1,128)}, u32[]{:S(2)}, u32[]{:S(2)}) %all-to-all-start) | async-done | bytes 160 | tf_op jit(solution)/shard_map/all_to_all | solution.py:326
  31.4 1.4 %reduce.1.lengths_ref = s32[32]{0:T(128)S(1)} reduce(s32[32,1,1]{2,1,0:T(1,128)} %all-to-all-done, s32[]{:T(128)} %constant.40.clone.1), dimensions={1,2}, to_apply=%all_to_all.11.reduce_sub_computation | reduce | bytes 260 | tf_op jit(solution)/shard_map/all_to_all | solution.py:326
  32.8 5.2 %local_states.1 = f32[8,136,256]{2,1,0:T(8,128)S(1)} custom-call(s32[32]{0:T(128)S(1)} %reduce.1.lengths_ref, s32[13]{0:T(128)S(1)} %concatenate.3.where_ref, f32[128,256]{1,0:T(8,128)S(1)} %copy-done.6, bf16[448,3072]{1,0:T(8,128)(2,1)S(1)} %copy-done, bf16[448,3072]{1,0:T(8,128)(2,1)S(1)} %copy-done, ...), custom_call_target="tpu_custom_call" | custom-call | tf_op jit(solution)/shard_map/local_states/pallas_call | solution.py:151
  38.0 1.0 copy-done.1
  39.1 5.4 %all-to-all-start.1 = ((f32[8,136,256]{2,1,0:T(8,128)}), f32[8,136,256]{2,1,0:T(8,128)}, u32[]{:S(2)}, u32[]{:S(2)}) async-start(f32[8,136,256]{2,1,0:T(8,128)} %copy-done.1), calls=%async_computation.1 | async-start | bytes 2228224 | tf_op jit(solution)/shard_map/all_to_all | solution.py:359
  44.5 0.1 select_reduce_fusion
  44.6 0.1 copy.19.begin_ref
  44.7 9.2 %local_attention.1 = (bf16[8,256,256]{2,1,0:T(8,128)(2,1)S(1)}, bf16[8,256,256]{2,1,0:T(8,128)(2,1)S(1)}, f32[8,256,256]{2,1,0:T(8,128)S(1)}) custom-call(s32[32]{0:T(128)S(1)} %reduce.1.lengths_ref, s32[13]{0:T(128)S(1)} %concatenate.3.where_ref, s32[256,1]{1,0:T(8,128)S(1)} %copy.19.begin_ref, f32[128,256]{1,0:T(8,128)S(1)} %copy-done.6, ...), custom_call_target="tpu_custom_call" | custom-call | flops 6000000000 | bytes 8000000 | tf_op jit(solution)/shard_map/local_attention/pallas_call | solution.py:197
  53.9 1.0 copy-done.2
  54.9 1.0 copy-done.4
  55.9 0.5 all-to-all-done.1.states_ref
  56.3 2.0 %group_tail.1 = f32[136,256]{1,0:T(8,128)} custom-call(s32[13]{0:T(128)} %copy-done.7, f32[8,136,256]{2,1,0:T(8,128)} %all-to-all-done.1.states_ref), custom_call_target="tpu_custom_call" | custom-call | tf_op jit(solution)/shard_map/group_tail/pallas_call | solution.py:233
  58.3 5.6 %collective-permute-start.3 = (f32[136,256]{1,0:T(8,128)}, f32[136,256]{1,0:T(8,128)S(1)}, u32[]{:S(2)}, u32[]{:S(2)}) collective-permute-start(f32[136,256]{1,0:T(8,128)} %group_tail.1), channel_id=1, source_target_pairs={{0,16},{1,17},{2,18},{3,19},{4,20},{5,21},{6,22},{7,23},{8,24},{9,... | collective-permute-start | bytes 417800 | tf_op jit(solution)/shard_map/ppermute | solution.py:314
  64.0 2.5 %collective-permute-start.2 = (f32[136,256]{1,0:T(8,128)}, f32[136,256]{1,0:T(8,128)S(1)}, u32[]{:S(2)}, u32[]{:S(2)}) collective-permute-start(f32[136,256]{1,0:T(8,128)} %group_tail.1), channel_id=1, source_target_pairs={{0,8},{1,9},{2,10},{3,11},{4,12},{5,13},{6,14},{7,15},{8,16},{9,17... | collective-permute-start | bytes 417800 | tf_op jit(solution)/shard_map/ppermute | solution.py:314
  66.5 0.6 reshape.58.norm_ref
  67.1 4.6 %collective-permute-done.3.far_ref = f32[136,256]{1,0:T(8,128)S(1)} collective-permute-done((f32[136,256]{1,0:T(8,128)}, f32[136,256]{1,0:T(8,128)S(1)}, u32[]{:S(2)}, u32[]{:S(2)}) %collective-permute-start.3) | collective-permute-done | bytes 139296 | tf_op jit(solution)/shard_map/ppermute | solution.py:314
  71.7 1.7 %collective-permute-done.2.near_ref = f32[136,256]{1,0:T(8,128)S(1)} collective-permute-done((f32[136,256]{1,0:T(8,128)}, f32[136,256]{1,0:T(8,128)S(1)}, u32[]{:S(2)}, u32[]{:S(2)}) %collective-permute-start.2) | collective-permute-done | bytes 139296 | tf_op jit(solution)/shard_map/ppermute | solution.py:314
  73.4 0.7 copy-done.9
  74.1 2.9 %entering_states.1 = f32[8,136,256]{2,1,0:T(8,128)} custom-call(s32[13]{0:T(128)} %copy-done.7, f32[8,136,256]{2,1,0:T(8,128)} %all-to-all-done.1.states_ref, f32[136,256]{1,0:T(8,128)} %copy-done.9, f32[136,256]{1,0:T(8,128)} %copy-done.8, f32[8,256,128]{2,1,0:T(8,128)} %state_ref.1, f32[8,1,256]{2,1,0:T(1,128)} %reshape.58.norm_ref), custom_call_target="tpu_custom_call" | custom-call | tf_op jit(solution)/shard_map/entering_states/pallas_call | solution.py:261
  77.0 27.6 %all_to_all.18.state_ref = f32[8,136,256]{2,1,0:T(8,128)S(1)} all-to-all(f32[8,136,256]{2,1,0:T(8,128)} %entering_states.1), channel_id=1, replica_groups={{0,1,2,3,4,5,6,7},{8,9,10,11,12,13,14,15},{16,17,18,19,20,21,22,23},{24..., dimensions={0} | all-to-all | bytes 2228224 | tf_op jit(solution)/shard_map/all_to_all | solution.py:368
  104.7 2.7 %finish.1 = f32[256,1024]{1,0:T(8,128)} custom-call(s32[256,1]{1,0:T(8,128)S(1)} %copy.19.begin_ref, f32[8,136,256]{2,1,0:T(8,128)S(1)} %all_to_all.18.state_ref, bf16[8,256,256]{2,1,0:T(8,128)(2,1)S(1)} %copy-done.3, bf16[8,256,256]{2,1,0:T(8,128)(2,1)S(1)} %copy-done.5, f32[8,256,256]{2,1,0:T(8,128)S(1)} %get-tuple-element.22.local_ref), custom_call_target="tpu_custom_call" | custom-call | tf_op jit(solution)/shard_map/finish/pallas_call | solution.py:296
  (25 shorter events, 0.1 us)
Async XLA Ops:
  0.7 32.2 %copy-start = (bf16[448,3072]{1,0:T(8,128)(2,1)S(1)}, bf16[448,3072]{1,0:T(8,128)(2,1)}, u32[]{:S(2)}) copy-start(bf16[448,3072]{1,0:T(8,128)(2,1)} %refs_2_.1) | copy-start | bytes 8257540
  0.7 32.2 %copy-start.6 = (f32[128,256]{1,0:T(8,128)S(1)}, f32[128,256]{1,0:T(8,128)}, u32[]{:S(2)}) copy-start(f32[128,256]{1,0:T(8,128)} %map_ref.3) | copy-start | bytes 393220
  3.1 29.7 %collective-permute-start = (bf16[104,3072]{1,0:T(8,128)(2,1)}, bf16[104,3072]{1,0:T(8,128)(2,1)S(1)}, u32[]{:S(2)}, u32[]{:S(2)}) collective-permute-start(bf16[104,3072]{1,0:T(8,128)(2,1)} %get-tuple-element.14), channel_id=1, source_target_pairs={{0,1},{1,2},{2,3},{3,4},{4,5},{5,6},{6,7},{7,8},{8,9},{9,10},{10,1... | collective-permute-start | bytes 1916936 | tf_op jit(solution)/shard_map/ppermute | solution.py:314
  6.3 26.5 %collective-permute-start.1 = (bf16[96,3072]{1,0:T(8,128)(2,1)}, bf16[96,3072]{1,0:T(8,128)(2,1)}, u32[]{:S(2)}, u32[]{:S(2)}) collective-permute-start(bf16[96,3072]{1,0:T(8,128)(2,1)} %get-tuple-element.15), channel_id=1, source_target_pairs={{1,0},{2,1},{3,2},{4,3},{5,4},{6,5},{7,6},{8,7},{9,8},{10,9},{11,1... | collective-permute-start | bytes 1769480 | tf_op jit(solution)/shard_map/ppermute | solution.py:325
  8.2 23.2 %all-to-all-start = ((s32[32,1,1]{2,1,0:T(1,128)}), s32[32,1,1]{2,1,0:T(1,128)}, u32[]{:S(2)}, u32[]{:S(2)}) async-start(s32[32,1,1]{2,1,0:T(1,128)} %broadcast_in_dim.37), calls=%async_computation | async-start | bytes 32768 | tf_op jit(solution)/shard_map/all_to_all | solution.py:326
  30.0 14.7 %copy-start.7 = (s32[13]{0:T(128)}, s32[13]{0:T(128)S(1)}, u32[]{:S(2)}) copy-start(s32[13]{0:T(128)S(1)} %concatenate.3.where_ref) | copy-start | bytes 160
  38.0 1.1 copy-start.1
  39.1 17.3 %all-to-all-start.1 = ((f32[8,136,256]{2,1,0:T(8,128)}), f32[8,136,256]{2,1,0:T(8,128)}, u32[]{:S(2)}, u32[]{:S(2)}) async-start(f32[8,136,256]{2,1,0:T(8,128)} %copy-done.1), calls=%async_computation.1 | async-start | bytes 2228224 | tf_op jit(solution)/shard_map/all_to_all | solution.py:359
  53.9 1.0 copy-start.2
  54.9 1.0 copy-start.4
  55.9 10.6 %copy-start.10 = (f32[8,256]{1,0:T(8,128)S(1)}, f32[8,256]{1,0:T(8,128)}, u32[]{:S(2)}) copy-start(f32[8,256]{1,0:T(8,128)} %param.11) | copy-start | bytes 24580
  58.3 13.3 %collective-permute-start.3 = (f32[136,256]{1,0:T(8,128)}, f32[136,256]{1,0:T(8,128)S(1)}, u32[]{:S(2)}, u32[]{:S(2)}) collective-permute-start(f32[136,256]{1,0:T(8,128)} %group_tail.1), channel_id=1, source_target_pairs={{0,16},{1,17},{2,18},{3,19},{4,20},{5,21},{6,22},{7,23},{8,24},{9,... | collective-permute-start | bytes 417800 | tf_op jit(solution)/shard_map/ppermute | solution.py:314
  64.0 9.5 %collective-permute-start.2 = (f32[136,256]{1,0:T(8,128)}, f32[136,256]{1,0:T(8,128)S(1)}, u32[]{:S(2)}, u32[]{:S(2)}) collective-permute-start(f32[136,256]{1,0:T(8,128)} %group_tail.1), channel_id=1, source_target_pairs={{0,8},{1,9},{2,10},{3,11},{4,12},{5,13},{6,14},{7,15},{8,16},{9,17... | collective-permute-start | bytes 417800 | tf_op jit(solution)/shard_map/ppermute | solution.py:314
  71.7 1.7 %copy-start.8 = (f32[136,256]{1,0:T(8,128)}, f32[136,256]{1,0:T(8,128)S(1)}, u32[]{:S(2)}) copy-start(f32[136,256]{1,0:T(8,128)S(1)} %collective-permute-done.3.far_ref) | copy-start | bytes 417796
  73.4 0.7 copy-start.9
  77.0 27.7 %copy-start.3 = (bf16[8,256,256]{2,1,0:T(8,128)(2,1)S(1)}, bf16[8,256,256]{2,1,0:T(8,128)(2,1)}, u32[]{:S(2)}) copy-start(bf16[8,256,256]{2,1,0:T(8,128)(2,1)} %copy-done.2) | copy-start | bytes 3145732
  77.0 27.7 %copy-start.5 = (bf16[8,256,256]{2,1,0:T(8,128)(2,1)S(1)}, bf16[8,256,256]{2,1,0:T(8,128)(2,1)}, u32[]{:S(2)}) copy-start(bf16[8,256,256]{2,1,0:T(8,128)(2,1)} %copy-done.4) | copy-start | bytes 3145732

commit v3 on v2

v3 whole, which is shorter than its diff:
```python
import functools

import jax
import jax.numpy as jnp
from jax import lax
from jax.experimental import pallas as pl
from jax.experimental.pallas import tpu as pltpu
from jax.sharding import PartitionSpec as P

H = 8
DH = 128
M = 256
TOK_DEV = 256
DRIFT = 96
CAP = 448
SHARDS = 32
DEVICES = 512
GROUP = 8
NETS = 64
TAIL = 104
REST = DRIFT + TAIL
LATER = 128
AUG = 136
CODED = 144
HB = 2
HALF = M // 2
F32 = jnp.float32
BF16 = jnp.bfloat16
I16 = jnp.int16
I32 = jnp.int32
TOP = 32768.0
NT = (((1,), (1,)), ((), ()))


def dot(a, b):
    return jnp.dot(a, b, preferred_element_type=F32)


def dot_nt(a, b):
    return lax.dot_general(a, b, NT, preferred_element_type=F32)


def in_hbm(x):
    return pltpu.with_memory_space_constraint(x, pltpu.HBM)


def split(x):
    high = x.astype(BF16)
    return high, (x - high.astype(F32)).astype(BF16)


def tail_start(length):
    start = jnp.maximum(length - DRIFT, 0)
    return jnp.minimum(start - lax.rem(start, 8), CAP - TAIL)


def windows_kernel(length_ref, rows_ref, tail_ref, head_ref, lengths_ref, sem):
    start = pl.multiple_of(tail_start(length_ref[0, 0]), 8)
    tail = pltpu.make_async_copy(rows_ref.at[pl.ds(start, TAIL), :], tail_ref, sem.at[0])
    head = pltpu.make_async_copy(rows_ref.at[pl.ds(0, DRIFT), :], head_ref, sem.at[1])
    tail.start()
    head.start()
    lengths_ref[...] = jnp.full((SHARDS, 1, 1), length_ref[0, 0], I32)
    tail.wait()
    head.wait()


def windows(rows, length):
    return pl.pallas_call(
        windows_kernel,
        out_shape=(
            jax.ShapeDtypeStruct((TAIL, 3 * H * DH), BF16),
            jax.ShapeDtypeStruct((DRIFT, 3 * H * DH), BF16),
            jax.ShapeDtypeStruct((SHARDS, 1, 1), I32),
        ),
        in_specs=[pl.BlockSpec(memory_space=pltpu.SMEM), pl.BlockSpec(memory_space=pl.ANY)],
        out_specs=[pl.BlockSpec(memory_space=pltpu.VMEM)] * 3,
        scratch_shapes=[pltpu.SemaphoreType.DMA((2,))],
        name="windows",
    )(length, rows)


def flags_kernel(place_ref, nets_ref, out_ref):
    device = place_ref[0]
    start = device * TOK_DEV
    member = lax.rem(device, GROUP)
    group_start = device - member
    for i in range(16):
        out_ref[i] = 0

    def one(n, carry):
        begin, last, first, nearby, earlier = carry
        begin = begin + nets_ref[n - 1]
        row = begin - start
        last = jnp.where(row < TOK_DEV, row, last)
        first = jnp.where(row >= 0, jnp.minimum(first, row), first)
        at = lax.shift_right_logical(begin, 8) - group_start
        inside = (at >= 0) & (at < GROUP)
        out_ref[jnp.where(inside, 4 + at, 15)] = 1
        nearby = jnp.where((at < 0) & (at >= -GROUP), 1, nearby)
        earlier = jnp.where(at < 0, 1, earlier)
        return begin, last, first, nearby, earlier

    zero = jnp.int32(0)
    _, last, first, nearby, earlier = lax.fori_loop(
        1, NETS, one, (zero, -1 - start, jnp.int32(TOK_DEV), zero, zero)
    )
    out_ref[0] = lax.rem(device, SHARDS)
    out_ref[1] = last
    out_ref[2] = nearby
    out_ref[3] = 1 - earlier
    out_ref[12] = member
    out_ref[13] = first
    out_ref[14] = start


def net_flags(place, net_lengths):
    smem = pl.BlockSpec(memory_space=pltpu.SMEM)
    return pl.pallas_call(
        flags_kernel,
        out_shape=jax.ShapeDtypeStruct((16,), I32),
        in_specs=[smem, smem],
        out_specs=smem,
        name="net_flags",
    )(place, net_lengths)


def exponent(top):
    return jnp.ceil(jnp.log2(jnp.maximum(top, 1e-30)))


def encode(state, norm):
    power = exponent(jnp.max(jnp.abs(state), axis=0, keepdims=True))
    codes = jnp.clip(jnp.round(state * jnp.exp2(15.0 - power)), 1.0 - TOP, TOP - 1.0)
    norm_power = exponent(norm)
    scaled = norm * jnp.exp2(15.0 - norm_power)
    high = jnp.minimum(jnp.round(scaled), TOP - 1.0)
    low = jnp.minimum(jnp.round((scaled - high) * TOP), TOP - 1.0)
    row = lax.broadcasted_iota(I32, (CODED - DH, state.shape[1]), 0)
    rest = jnp.where(row == 0, high, jnp.where(row == 1, low, jnp.where(row == 2, power, norm_power)))
    return jnp.concatenate([codes, rest], axis=0).astype(I32).astype(I16)


def decode(coded):
    codes = coded.astype(I32).astype(F32)
    high, low, power, norm_power = (codes[DH + i : DH + i + 1] for i in range(4))
    state = codes[:DH] * jnp.exp2(power - 15.0)
    return state, (high + low * (1.0 / TOP)) * jnp.exp2(norm_power - 15.0)


def build_selection(lengths_ref, seq_index, main_ref, rest_ref, drift_ref):
    before = lax.fori_loop(0, seq_index, lambda i, s: s + lengths_ref[i, 0, 0], jnp.int32(0))
    length = lengths_ref[seq_index, 0, 0]
    length_left = lengths_ref[jnp.maximum(seq_index - 1, 0), 0, 0]
    drift = before - seq_index * TOK_DEV
    drift_ref[0] = drift
    own = lax.broadcasted_iota(I32, (TOK_DEV, TOK_DEV), 0) - drift
    column = lax.broadcasted_iota(I32, (TOK_DEV, TOK_DEV), 1)
    main_ref[...] = jnp.where((column == own) & (own < length), 1.0, 0.0).astype(BF16)
    own = lax.broadcasted_iota(I32, (TOK_DEV, REST), 0) - drift
    column = lax.broadcasted_iota(I32, (TOK_DEV, REST), 1)
    late = jnp.where(drift >= 0, length_left - tail_start(length_left), -TOK_DEV)
    of_right = (own >= length) & (column == own - length) & (column < DRIFT)
    of_left = (column == own + late + DRIFT) & (column >= DRIFT)
    of_left = of_left & (own < jnp.where(drift >= 0, 0, length))
    rest_ref[...] = jnp.where(of_right | of_left, 1.0, 0.0).astype(BF16)


def pick(selection, main, later, left, right):
    main_ref, rest_ref, drift_ref = selection
    other = jnp.where(drift_ref[0] >= 0, left[...], later[:TAIL, :])
    rest = jnp.concatenate([right[...], other], axis=0)
    return dot(main_ref[...], main[...]) + dot(rest_ref[...], rest)


def feature_map_pair(map_ref, pair_ref):
    high, low = split(map_ref[...])
    pair_ref[:DH, :] = high
    pair_ref[DH:, :] = low


def features(part, pair_ref):
    scale = lax.rsqrt(jnp.mean(part * part, axis=-1, keepdims=True) + 1e-06) * DH ** (-0.5)
    twice = part.astype(BF16)
    return jnp.exp(dot(jnp.concatenate([twice, twice], axis=1), pair_ref[...]) * scale)


def state_kernel(where_ref, lengths_ref, map_ref, *refs):
    keys, values, (out_ref, pair, *selection) = refs[:4], refs[4:8], refs[8:]

    @pl.when(pl.program_id(0) == 0)
    def _():
        build_selection(lengths_ref, where_ref[0], *selection)
        feature_map_pair(map_ref, pair)

    first = where_ref[1]
    valid = lax.broadcasted_iota(I32, (TOK_DEV, 1), 0) >= first
    norm_rows = jnp.where(
        lax.broadcasted_iota(I32, (AUG - DH, TOK_DEV), 1) >= first, 1.0, 0.0
    ).astype(BF16)
    keys = pick(selection, *keys)
    values = pick(selection, *values)
    for i in range(HB):
        columns = slice(i * DH, (i + 1) * DH)
        high, low = split(features(keys[:, columns], pair))
        masked = jnp.where(valid, values[:, columns], 0.0)
        turned = jnp.concatenate([masked.T.astype(BF16), norm_rows], axis=0)
        total = dot(turned, high) + dot(turned, low)
        out_ref[i] = encode(total[:DH], total[DH : DH + 1])


def part_specs(part, first):
    column = part * (H // HB) + first
    return [
        pl.BlockSpec((TOK_DEV, HB * DH), lambda i, *_: (0, column + i)),
        pl.BlockSpec((LATER, HB * DH), lambda i, *_: (TOK_DEV // LATER, column + i)),
        pl.BlockSpec((TAIL, HB * DH), lambda i, *_: (0, column + i)),
        pl.BlockSpec((DRIFT, HB * DH), lambda i, *_: (0, column + i)),
    ]


def selection_scratch():
    return [
        pltpu.VMEM((2 * DH, M), BF16),
        pltpu.VMEM((TOK_DEV, TOK_DEV), BF16),
        pltpu.VMEM((TOK_DEV, REST), BF16),
        pltpu.SMEM((1,), I32),
    ]


def local_states(where, lengths, feature_map, rows, left, right):
    smem = pl.BlockSpec(memory_space=pltpu.SMEM)
    return pl.pallas_call(
        state_kernel,
        out_shape=pltpu.HBM((H, CODED, M), I16),
        grid=(H // HB,),
        in_specs=[
            smem,
            smem,
            pl.BlockSpec((DH, M), lambda i: (0, 0)),
            *part_specs(1, 0),
            *part_specs(2, 0),
        ],
        out_specs=pl.BlockSpec((HB, CODED, M), lambda i: (i, 0, 0)),
        scratch_shapes=selection_scratch(),
        compiler_params=pltpu.CompilerParams(vmem_limit_bytes=12 << 20),
        name="local_states",
    )(where, lengths, in_hbm(feature_map), *([rows, rows, left, right] * 2))


def attention_kernel(where_ref, lengths_ref, nets_ref, map_ref, *refs):
    queries, keys, values = refs[:4], refs[4:8], refs[8:12]
    high_ref, low_ref, out_ref, norm_ref, begin_ref, pair, *selection = refs[12:]

    @pl.when(pl.program_id(0) == 0)
    def _():
        build_selection(lengths_ref, where_ref[0], *selection)
        feature_map_pair(map_ref, pair)
        row = lax.broadcasted_iota(I32, (8, TOK_DEV), 1)

        def one(n, carry):
            begin, latest = carry
            begin = begin + nets_ref[n - 1]
            return begin, jnp.where(row >= begin, begin, latest)

        start = where_ref[14]
        _, latest = lax.fori_loop(
            1, NETS, one, (-start, jnp.full((8, TOK_DEV), -1 - start, I32))
        )
        begin_ref[...] = latest.astype(F32).T
        norm_ref[...] = jnp.zeros((TOK_DEV, DH), F32)

    query = lax.broadcasted_iota(I32, (TOK_DEV, TOK_DEV), 0)
    key = lax.broadcasted_iota(I32, (TOK_DEV, TOK_DEV), 1)
    allowed = (key <= query) & (key.astype(F32) >= begin_ref[:, :1])
    lane = lax.broadcasted_iota(I32, (TOK_DEV, DH), 1)
    queries = pick(selection, *queries)
    keys = pick(selection, *keys)
    values = pick(selection, *values)
    for i in range(HB):
        columns = slice(i * DH, (i + 1) * DH)
        q_high, q_low = split(features(queries[:, columns], pair))
        k_high, k_low = split(features(keys[:, columns], pair))
        high_ref[i] = q_high
        low_ref[i] = q_low
        scores = dot_nt(q_high, k_high) + dot_nt(q_high, k_low) + dot_nt(q_low, k_high)
        s_high, s_low = split(jnp.where(allowed, scores, 0.0))
        value = jnp.concatenate(
            [values[:, columns].astype(BF16), jnp.ones((TOK_DEV, DH), BF16)], axis=1
        )
        total = dot(s_high, value) + dot(s_low, value)
        out_ref[i] = total[:, :DH]
        mine = lane == pl.program_id(0) * HB + i
        norm_ref[...] = jnp.where(mine, total[:, DH:], norm_ref[...])


def local_attention(where, lengths, nets, feature_map, rows, left, right, half):
    steps = H // HB // 2
    by_head = lambda width: pl.BlockSpec((HB, TOK_DEV, width), lambda i: (i, 0, 0))
    smem = pl.BlockSpec(memory_space=pltpu.SMEM)
    specs = [spec for part in range(3) for spec in part_specs(part, half * steps)]
    return pl.pallas_call(
        attention_kernel,
        out_shape=(
            pltpu.HBM((H // 2, TOK_DEV, M), BF16),
            pltpu.HBM((H // 2, TOK_DEV, M), BF16),
            pltpu.HBM((H // 2, TOK_DEV, DH), F32),
            pltpu.HBM((TOK_DEV, DH), F32),
        ),
        grid=(steps,),
        in_specs=[smem, smem, smem, pl.BlockSpec((DH, M), lambda i: (0, 0)), *specs],
        out_specs=(
            by_head(M),
            by_head(M),
            by_head(DH),
            pl.BlockSpec((TOK_DEV, DH), lambda i: (0, 0)),
        ),
        scratch_shapes=[pltpu.VMEM((TOK_DEV, 8), F32)] + selection_scratch(),
        compiler_params=pltpu.CompilerParams(vmem_limit_bytes=20 << 20),
        cost_estimate=pl.CostEstimate(
            flops=3_000_000_000, transcendentals=500_000, bytes_accessed=4_000_000
        ),
        name="local_attention",
    )(where, lengths, nets, in_hbm(feature_map), *([rows, rows, left, right] * 3))


def tail_kernel(where_ref, states_ref, out_ref):
    state, norm = decode(states_ref[0])
    for j in range(1, GROUP):
        keep = where_ref[4 + j] == 0
        more, more_norm = decode(states_ref[j])
        state = jnp.where(keep, state, 0.0) + more
        norm = jnp.where(keep, norm, 0.0) + more_norm
    out_ref[...] = encode(state, norm)


def group_tail(where, states):
    vmem = pl.BlockSpec(memory_space=pltpu.VMEM)
    return pl.pallas_call(
        tail_kernel,
        out_shape=jax.ShapeDtypeStruct((CODED, M), I16),
        in_specs=[pl.BlockSpec(memory_space=pltpu.SMEM), vmem],
        out_specs=vmem,
        name="group_tail",
    )(where, states)


def prefix_kernel(
    where_ref, states_ref, near_ref, far_ref, state_ref, norm_ref, out_ref, running, running_norm
):
    near, near_norm = decode(near_ref[...])
    far, far_norm = decode(far_ref[...])
    reaches = where_ref[2] == 0
    running[...] = near + jnp.where(reaches, far, 0.0)
    running_norm[...] = near_norm + jnp.where(reaches, far_norm, 0.0)

    @pl.when(where_ref[3] != 0)
    def _():
        running[...] += state_ref[0].T
        running_norm[...] += norm_ref[0]

    state, norm = running[...], running_norm[...]
    for j in range(GROUP):
        out_ref[j] = encode(state, norm)
        if j < GROUP - 1:
            keep = where_ref[4 + j] == 0
            more, more_norm = decode(states_ref[j])
            state = jnp.where(keep, state, 0.0) + more
            norm = jnp.where(keep, norm, 0.0) + more_norm


def entering_states(where, states, near, far, carried_state, carried_norm):
    by_group = pl.BlockSpec((GROUP, CODED, HALF), lambda i, where: (0, 0, i))
    one = pl.BlockSpec((CODED, HALF), lambda i, where: (0, i))
    return pl.pallas_call(
        prefix_kernel,
        out_shape=jax.ShapeDtypeStruct((GROUP, CODED, M), I16),
        grid_spec=pltpu.PrefetchScalarGridSpec(
            num_scalar_prefetch=1,
            grid=(M // HALF,),
            in_specs=[
                by_group,
                one,
                one,
                pl.BlockSpec((1, HALF, DH), lambda i, where: (where[12], i, 0)),
                pl.BlockSpec((1, 1, HALF), lambda i, where: (where[12], 0, i)),
            ],
            out_specs=by_group,
            scratch_shapes=[pltpu.VMEM((DH, HALF), F32), pltpu.VMEM((1, HALF), F32)],
        ),
        name="entering_states",
    )(where, states, near, far, carried_state, carried_norm.reshape(H, 1, M))


def finish_kernel(where_ref, state_ref, *refs):
    *halves, out_ref = refs
    carried = lax.broadcasted_iota(I32, (TOK_DEV, 1), 0) < where_ref[13]
    lane = lax.broadcasted_iota(I32, (TOK_DEV, DH), 1)
    step = pl.program_id(0)

    def run(high_ref, low_ref, local_ref, local_norm_ref, before):
        for i in range(HB):
            mine = lane == (step - before) * HB + i
            local_norm = jnp.sum(
                jnp.where(mine, local_norm_ref[...], 0.0), axis=1, keepdims=True
            )
            state, norm = decode(state_ref[i])
            state = jnp.concatenate([state, jnp.broadcast_to(norm, (DH, M))], axis=0)
            s_high, s_low = split(state)
            q_high = high_ref[i]
            entering = dot_nt(q_high, s_high) + dot_nt(q_high, s_low) + dot_nt(low_ref[i], s_high)
            entering = jnp.where(carried, entering, 0.0)
            total = local_ref[i] + entering[:, :DH]
            out_ref[:, i * DH : (i + 1) * DH] = total / (local_norm + entering[:, DH:])

    steps = H // HB // 2
    pl.when(step < steps)(lambda: run(*halves[:4], 0))
    pl.when(step >= steps)(lambda: run(*halves[4:], steps))


def finish(where, states, *halves):
    steps = H // HB // 2

    def specs(half):
        top = lambda i: jnp.minimum(i, steps - 1) if half == 0 else jnp.maximum(i - steps, 0)
        by_head = lambda width: pl.BlockSpec((HB, TOK_DEV, width), lambda i: (top(i), 0, 0))
        whole = pl.BlockSpec((TOK_DEV, DH), lambda i: (0, 0))
        return [by_head(M), by_head(M), by_head(DH), whole]

    return pl.pallas_call(
        finish_kernel,
        out_shape=jax.ShapeDtypeStruct((TOK_DEV, H * DH), F32),
        grid=(H // HB,),
        in_specs=[
            pl.BlockSpec(memory_space=pltpu.SMEM),
            pl.BlockSpec((HB, CODED, M), lambda i: (i, 0, 0)),
            *specs(0),
            *specs(1),
        ],
        out_specs=pl.BlockSpec((TOK_DEV, HB * DH), lambda i: (0, i)),
        compiler_params=pltpu.CompilerParams(vmem_limit_bytes=20 << 20),
        name="finish",
    )(where, states, *(in_hbm(half) for half in halves))


def shifted(block, axis, count, distance):
    ahead = max(distance, 0)
    return lax.ppermute(
        block, axis, [(i - distance, i) for i in range(ahead, count + min(distance, 0))]
    )


def local(loader_rows, loader_lengths, net_lengths, feature_map, carried_state, carried_norm):
    device = lax.axis_index("grp") * SHARDS + lax.axis_index("seq")
    groups = [list(range(i, i + GROUP)) for i in range(0, SHARDS, GROUP)]

    tail, head, length = windows(loader_rows, loader_lengths)
    left = shifted(tail, "seq", SHARDS, 1)
    right = shifted(head, "seq", SHARDS, -1)
    lengths = lax.all_to_all(length, "seq", 0, 0, tiled=True)
    where = net_flags(device.astype(I32)[None], net_lengths)
    states = local_states(where, lengths, feature_map, loader_rows, left, right)
    states = lax.all_to_all(states, "seq", 0, 0, axis_index_groups=groups, tiled=True)
    attend = functools.partial(
        local_attention, where, lengths, net_lengths, feature_map, loader_rows, left, right
    )
    first = attend(0)
    states, *first = lax.optimization_barrier((states, *first))
    states = states.reshape(GROUP, CODED, M)
    tail = group_tail(where, states)
    far = shifted(tail, ("grp", "seq"), DEVICES, 2 * GROUP)
    near = shifted(tail, ("grp", "seq"), DEVICES, GROUP)
    second = attend(1)
    near, far, *second = lax.optimization_barrier((near, far, *second))
    states = entering_states(where, states, near, far, carried_state, carried_norm)
    states = lax.all_to_all(states, "seq", 0, 0, axis_index_groups=groups, tiled=True)
    return finish(where, states, *first, *second)


def solution(mesh):
    in_specs = (P(("grp", "seq"), None), P("grp", "seq"), P(), P(), P(), P())
    out_specs = P(("grp", "seq"), None)
    return jax.shard_map(local, mesh=mesh, in_specs=in_specs, out_specs=out_specs, check_vma=False)
```

time: 108 us -> 92 us (0.85)
  the two profiles are of different devices: /device:TPU:33 before, /device:TPU:32 now
where the time goes in v3:
time: 92 us; the launch traced here: 91.3 us
  starting transfers between devices  33.1 us (36%)
  Pallas kernels  31.5 us (34%)
  blocking collectives  12.6 us (14%)
  waiting for transfers between devices  12 us (13%)
  local copies, waits for them, and re-layouts  1.28 us (1%)
  between operations  0.94 us (1%)
    all_to_all x1, starting transfers between devices, local(): lengths = lax.all_to_all(length, 'seq', 0, 0, tiled=True)  15.1 us
    all_to_all x1, blocking collectives, local(): lax.all_to_all(states, 'seq', 0, 0, axis_index_groups=groups, tiled=True)  12.6 us
    pallas_call x2, Pallas kernels, local_attention(): pl.pallas_call(attention_kernel, out_shape=(pltpu.HBM((H // 2, TOK_DEV, M...  11.8 us
    ppermute x4, starting transfers between devices, shifted(): lax.ppermute(block, axis, [(i - distance, i) for i in range(ahead, count...  11.6 us
    all_to_all x1, waiting for transfers between devices, local(): lengths = lax.all_to_all(length, 'seq', 0, 0, tiled=True)  7.37 us
    all_to_all x1, starting transfers between devices, local(): lax.all_to_all(states, 'seq', 0, 0, axis_index_groups=groups, tiled=True)  6.32 us
    pallas_call x1, Pallas kernels, local_states(): pl.pallas_call(state_kernel, out_shape=pltpu.HBM((H, CODED, M), I16), gri...  5.18 us
    pallas_call x1, Pallas kernels, finish(): pl.pallas_call(finish_kernel, out_shape=jax.ShapeDtypeStruct((TOK_DEV, H...  4.97 us
  transfers between devices with their start and end apart: 6, of which 3 were waited for; matrix products, arithmetic and copies ran while one was open for 1% of the time, Pallas kernels for 15%

profile of v3, /device:TPU:32, one launch (start us, length us, event | category | flops | bytes accessed | tf_op | source)
XLA Modules:
  0.0 91.3 jit_solution(7475033741013365501)
XLA Ops:
  0.8 2.3 %windows.1 = (bf16[104,3072]{1,0:T(8,128)(2,1)}, bf16[96,3072]{1,0:T(8,128)(2,1)}, s32[32,1,1]{2,1,0:T(1,128)}) custom-call(s32[1,1]{1,0:T(1,128)S(6)} %copy.7.length_ref, bf16[448,3072]{1,0:T(8,128)(2,1)} %refs_9_.3), custom_call_target="tpu_custom_call" | custom-call | tf_op jit(solution)/shard_map/windows/pallas_call | solution.py:69
  3.1 3.4 %collective-permute-start = (bf16[104,3072]{1,0:T(8,128)(2,1)}, bf16[104,3072]{1,0:T(8,128)(2,1)S(1)}, u32[]{:S(2)}, u32[]{:S(2)}) collective-permute-start(bf16[104,3072]{1,0:T(8,128)(2,1)} %get-tuple-element.28), channel_id=1, source_target_pairs={{0,1},{1,2},{2,3},{3,4},{4,5},{5,6},{6,7},{7,8},{8,9},{9,10},{10,1... | collective-permute-start | bytes 1916936 | tf_op jit(solution)/shard_map/ppermute | solution.py:448
  6.6 1.3 %collective-permute-start.1 = (bf16[96,3072]{1,0:T(8,128)(2,1)}, bf16[96,3072]{1,0:T(8,128)(2,1)}, u32[]{:S(2)}, u32[]{:S(2)}) collective-permute-start(bf16[96,3072]{1,0:T(8,128)(2,1)} %get-tuple-element.29), channel_id=1, source_target_pairs={{1,0},{2,1},{3,2},{4,3},{5,4},{6,5},{7,6},{8,7},{9,8},{10,9},{11,1... | collective-permute-start | bytes 1769480 | tf_op jit(solution)/shard_map/ppermute | solution.py:448
  7.9 15.1 %all-to-all-start = ((s32[32,1,1]{2,1,0:T(1,128)}), s32[32,1,1]{2,1,0:T(1,128)S(1)}, u32[]{:S(2)}, u32[]{:S(2)}) async-start(s32[32,1,1]{2,1,0:T(1,128)} %get-tuple-element.27), calls=%async_computation | async-start | bytes 32768 | tf_op jit(solution)/shard_map/all_to_all | solution.py:460
  23.0 0.0 copy-start.5
  23.0 2.2 %net_flags.1.where_ref = s32[16]{0:T(128)} custom-call(s32[1]{0:T(128)} %bitcast.place_ref, s32[64]{0:T(128)} %nets_ref.5), custom_call_target="tpu_custom_call" | custom-call | tf_op jit(solution)/shard_map/net_flags/pallas_call | solution.py:119
  25.2 7.4 %all-to-all-done.lengths_ref = s32[32,1,1]{2,1,0:T(1,128)S(1)} async-done(((s32[32,1,1]{2,1,0:T(1,128)}), s32[32,1,1]{2,1,0:T(1,128)S(1)}, u32[]{:S(2)}, u32[]{:S(2)}) %all-to-all-start) | async-done | bytes 160 | tf_op jit(solution)/shard_map/all_to_all | solution.py:460
  32.6 0.0 collective-permute-done.1.refs_3_.refs_7_.refs_11_
  32.6 0.0 collective-permute-done.refs_2_.refs_6_.refs_10_
  32.6 0.0 copy-done
  32.6 0.0 copy-start.1
  32.6 0.7 copy-done.1
  33.3 5.2 %local_states.1 = s16[8,144,256]{2,1,0:T(8,128)(2,1)} custom-call(s32[16]{0:T(128)S(1)} %copy-done.1, s32[32,1,1]{2,1,0:T(1,128)S(1)} %all-to-all-done.lengths_ref, f32[128,256]{1,0:T(8,128)} %map_ref.5, bf16[448,3072]{1,0:T(8,128)(2,1)S(1)} %copy-done, bf16[448,3072]{1,0:T(8,128)(2,1)S(1)} %copy-done, ...), custom_call_target="tpu_custom_call" | custom-call | tf_op jit(solution)/shard_map/local_states/pallas_call | solution.py:233
  38.5 6.3 %all-to-all-start.1 = ((s16[8,144,256]{2,1,0:T(8,128)(2,1)}), s16[8,144,256]{2,1,0:T(8,128)(2,1)}, u32[]{:S(2)}, u32[]{:S(2)}) async-start(s16[8,144,256]{2,1,0:T(8,128)(2,1)} %local_states.1), calls=%async_computation.1 | async-start | bytes 1179648 | tf_op jit(solution)/shard_map/all_to_all | solution.py:463
  44.8 0.0 copy-done.7
  44.8 0.6 reshape.3.norm_ref
  45.4 0.0 copy-done.5
  45.4 0.0 copy-done.2
  45.4 5.9 %local_attention.2 = (bf16[4,256,256]{2,1,0:T(8,128)(2,1)}, bf16[4,256,256]{2,1,0:T(8,128)(2,1)}, f32[4,256,128]{2,1,0:T(8,128)}, f32[256,128]{1,0:T(8,128)}) custom-call(s32[16]{0:T(128)S(1)} %copy-done.2, s32[32,1,1]{2,1,0:T(1,128)S(1)} %all-to-all-done.lengths_ref, s32[64]{0:T(128)S(1)} %copy-done.5, f32[128,256]{1,0:T(8,128)} %map_ref.5, ...), custom_call_target="tpu_custom_call" | custom-call | flops 3000000000 | bytes 4000000 | tf_op jit(solution)/shard_map/local_attention/pallas_call | solution.py:302
  51.3 2.4 %all-to-all-done.1.states_ref = s16[8,144,256]{2,1,0:T(8,128)(2,1)} async-done(((s16[8,144,256]{2,1,0:T(8,128)(2,1)}), s16[8,144,256]{2,1,0:T(8,128)(2,1)}, u32[]{:S(2)}, u32[]{:S(2)}) %all-to-all-start.1) | async-done | bytes 589856 | tf_op jit(solution)/shard_map/all_to_all | solution.py:463
  53.7 2.0 %group_tail.1 = s16[144,256]{1,0:T(8,128)(2,1)} custom-call(s32[16]{0:T(128)} %net_flags.1.where_ref, s16[8,144,256]{2,1,0:T(8,128)(2,1)} %all-to-all-done.1.states_ref), custom_call_target="tpu_custom_call" | custom-call | tf_op jit(solution)/shard_map/group_tail/pallas_call | solution.py:339
  55.7 4.4 %collective-permute-start.3 = (s16[144,256]{1,0:T(8,128)(2,1)}, s16[144,256]{1,0:T(8,128)(2,1)S(1)}, u32[]{:S(2)}, u32[]{:S(2)}) collective-permute-start(s16[144,256]{1,0:T(8,128)(2,1)} %group_tail.1), channel_id=1, source_target_pairs={{0,16},{1,17},{2,18},{3,19},{4,20},{5,21},{6,22},{7,23},{8,24},{9,... | collective-permute-start | bytes 221192 | tf_op jit(solution)/shard_map/ppermute | solution.py:448
  60.0 2.5 %collective-permute-start.2 = (s16[144,256]{1,0:T(8,128)(2,1)}, s16[144,256]{1,0:T(8,128)(2,1)}, u32[]{:S(2)}, u32[]{:S(2)}) collective-permute-start(s16[144,256]{1,0:T(8,128)(2,1)} %group_tail.1), channel_id=1, source_target_pairs={{0,8},{1,9},{2,10},{3,11},{4,12},{5,13},{6,14},{7,15},{8,16},{9,17... | collective-permute-start | bytes 221192 | tf_op jit(solution)/shard_map/ppermute | solution.py:448
  62.6 0.0 copy-done.3
  62.6 5.9 %local_attention.3 = (bf16[4,256,256]{2,1,0:T(8,128)(2,1)}, bf16[4,256,256]{2,1,0:T(8,128)(2,1)}, f32[4,256,128]{2,1,0:T(8,128)}, f32[256,128]{1,0:T(8,128)}) custom-call(s32[16]{0:T(128)S(1)} %copy-done.3, s32[32,1,1]{2,1,0:T(1,128)S(1)} %all-to-all-done.lengths_ref, s32[64]{0:T(128)S(1)} %copy-done.5, f32[128,256]{1,0:T(8,128)} %map_ref.5, ...), custom_call_target="tpu_custom_call" | custom-call | flops 3000000000 | bytes 4000000 | tf_op jit(solution)/shard_map/local_attention/pallas_call | solution.py:302
  68.5 0.0 copy-start.4
  68.5 0.0 collective-permute-done.3.far_ref
  68.5 2.2 %collective-permute-done.2.near_ref = s16[144,256]{1,0:T(8,128)(2,1)} collective-permute-done((s16[144,256]{1,0:T(8,128)(2,1)}, s16[144,256]{1,0:T(8,128)(2,1)}, u32[]{:S(2)}, u32[]{:S(2)}) %collective-permute-start.2) | collective-permute-done | bytes 73760 | tf_op jit(solution)/shard_map/ppermute | solution.py:448
  70.8 0.0 copy-done.6
  70.8 3.0 %entering_states.1 = s16[8,144,256]{2,1,0:T(8,128)(2,1)} custom-call(s32[16]{0:T(128)} %net_flags.1.where_ref, s16[8,144,256]{2,1,0:T(8,128)(2,1)} %all-to-all-done.1.states_ref, s16[144,256]{1,0:T(8,128)(2,1)} %collective-permute-done.2.near_ref, s16[144,256]{1,0:T(8,128)(2,1)} %copy-done.6, f32[8,256,128]{2,1,0:T(8,128)} %state_ref.1, ...), custom_call_target="tpu_custom_call" | custom-call | tf_op jit(solution)/shard_map/entering_states/pallas_call | solution.py:375
  73.7 12.6 %all_to_all.15.state_ref = s16[8,144,256]{2,1,0:T(8,128)(2,1)S(1)} all-to-all(s16[8,144,256]{2,1,0:T(8,128)(2,1)} %entering_states.1), channel_id=1, replica_groups={{0,1,2,3,4,5,6,7},{8,9,10,11,12,13,14,15},{16,17,18,19,20,21,22,23},{24..., dimensions={0} | all-to-all | bytes 1179648 | tf_op jit(solution)/shard_map/all_to_all | solution.py:476
  86.3 5.0 %finish.1 = f32[256,1024]{1,0:T(8,128)} custom-call(s32[16]{0:T(128)S(1)} %copy-done.4, s16[8,144,256]{2,1,0:T(8,128)(2,1)S(1)} %all_to_all.15.state_ref, bf16[4,256,256]{2,1,0:T(8,128)(2,1)} %get-tuple-element.41.refs_0_, bf16[4,256,256]{2,1,0:T(8,128)(2,1)} %get-tuple-element.42.refs_1_, f32[4,256,128]{2,1,0:T(8,128)} %get-tuple-element.43.refs_2_, ...), custom_call_target="tpu_custom_call" | custom-call | tf_op jit(solution)/shard_map/finish/pallas_call | solution.py:430
  (6 shorter events, 0.0 us)
Async XLA Ops:
  0.0 32.6 %copy-start = (bf16[448,3072]{1,0:T(8,128)(2,1)S(1)}, bf16[448,3072]{1,0:T(8,128)(2,1)}, u32[]{:S(2)}) copy-start(bf16[448,3072]{1,0:T(8,128)(2,1)} %refs_9_.3) | copy-start | bytes 8257540
  3.1 29.5 %collective-permute-start = (bf16[104,3072]{1,0:T(8,128)(2,1)}, bf16[104,3072]{1,0:T(8,128)(2,1)S(1)}, u32[]{:S(2)}, u32[]{:S(2)}) collective-permute-start(bf16[104,3072]{1,0:T(8,128)(2,1)} %get-tuple-element.28), channel_id=1, source_target_pairs={{0,1},{1,2},{2,3},{3,4},{4,5},{5,6},{6,7},{7,8},{8,9},{9,10},{10,1... | collective-permute-start | bytes 1916936 | tf_op jit(solution)/shard_map/ppermute | solution.py:448
  6.6 26.0 %collective-permute-start.1 = (bf16[96,3072]{1,0:T(8,128)(2,1)}, bf16[96,3072]{1,0:T(8,128)(2,1)}, u32[]{:S(2)}, u32[]{:S(2)}) collective-permute-start(bf16[96,3072]{1,0:T(8,128)(2,1)} %get-tuple-element.29), channel_id=1, source_target_pairs={{1,0},{2,1},{3,2},{4,3},{5,4},{6,5},{7,6},{8,7},{9,8},{10,9},{11,1... | collective-permute-start | bytes 1769480 | tf_op jit(solution)/shard_map/ppermute | solution.py:448
  7.9 24.7 %all-to-all-start = ((s32[32,1,1]{2,1,0:T(1,128)}), s32[32,1,1]{2,1,0:T(1,128)S(1)}, u32[]{:S(2)}, u32[]{:S(2)}) async-start(s32[32,1,1]{2,1,0:T(1,128)} %get-tuple-element.27), calls=%async_computation | async-start | bytes 32768 | tf_op jit(solution)/shard_map/all_to_all | solution.py:460
  23.0 22.4 %copy-start.5 = (s32[64]{0:T(128)S(1)}, s32[64]{0:T(128)}, u32[]{:S(2)}) copy-start(s32[64]{0:T(128)} %nets_ref.5) | copy-start | bytes 772
  32.6 0.7 copy-start.1
  33.3 11.5 %copy-start.7 = (f32[8,256]{1,0:T(8,128)S(1)}, f32[8,256]{1,0:T(8,128)}, u32[]{:S(2)}) copy-start(f32[8,256]{1,0:T(8,128)} %param.11) | copy-start | bytes 24580
  33.3 12.1 %copy-start.2 = (s32[16]{0:T(128)S(1)}, s32[16]{0:T(128)}, u32[]{:S(2)}) copy-start(s32[16]{0:T(128)} %net_flags.1.where_ref) | copy-start | bytes 196
  38.5 15.2 %all-to-all-start.1 = ((s16[8,144,256]{2,1,0:T(8,128)(2,1)}), s16[8,144,256]{2,1,0:T(8,128)(2,1)}, u32[]{:S(2)}, u32[]{:S(2)}) async-start(s16[8,144,256]{2,1,0:T(8,128)(2,1)} %local_states.1), calls=%async_computation.1 | async-start | bytes 1179648 | tf_op jit(solution)/shard_map/all_to_all | solution.py:463
  45.4 17.2 %copy-start.3 = (s32[16]{0:T(128)S(1)}, s32[16]{0:T(128)}, u32[]{:S(2)}) copy-start(s32[16]{0:T(128)} %net_flags.1.where_ref) | copy-start | bytes 196
  55.7 12.9 %collective-permute-start.3 = (s16[144,256]{1,0:T(8,128)(2,1)}, s16[144,256]{1,0:T(8,128)(2,1)S(1)}, u32[]{:S(2)}, u32[]{:S(2)}) collective-permute-start(s16[144,256]{1,0:T(8,128)(2,1)} %group_tail.1), channel_id=1, source_target_pairs={{0,16},{1,17},{2,18},{3,19},{4,20},{5,21},{6,22},{7,23},{8,24},{9,... | collective-permute-start | bytes 221192 | tf_op jit(solution)/shard_map/ppermute | solution.py:448
  60.0 10.8 %collective-permute-start.2 = (s16[144,256]{1,0:T(8,128)(2,1)}, s16[144,256]{1,0:T(8,128)(2,1)}, u32[]{:S(2)}, u32[]{:S(2)}) collective-permute-start(s16[144,256]{1,0:T(8,128)(2,1)} %group_tail.1), channel_id=1, source_target_pairs={{0,8},{1,9},{2,10},{3,11},{4,12},{5,13},{6,14},{7,15},{8,16},{9,17... | collective-permute-start | bytes 221192 | tf_op jit(solution)/shard_map/ppermute | solution.py:448
  68.5 17.8 %copy-start.4 = (s32[16]{0:T(128)S(1)}, s32[16]{0:T(128)}, u32[]{:S(2)}) copy-start(s32[16]{0:T(128)} %net_flags.1.where_ref) | copy-start | bytes 196
  68.5 2.2 %copy-start.6 = (s16[144,256]{1,0:T(8,128)(2,1)}, s16[144,256]{1,0:T(8,128)(2,1)S(1)}, u32[]{:S(2)}) copy-start(s16[144,256]{1,0:T(8,128)(2,1)S(1)} %collective-permute-done.3.far_ref) | copy-start | bytes 221188

commit v4 on v3

--- a/solution.py
+++ b/solution.py
@@ -22,7 +22,7 @@
 LATER = 128
 AUG = 136
 CODED = 144
-HB = 2
+HB = 4
 HALF = M // 2
 F32 = jnp.float32
 BF16 = jnp.bfloat16
@@ -166,11 +166,11 @@
     rest_ref[...] = jnp.where(of_right | of_left, 1.0, 0.0).astype(BF16)
 
 
-def pick(selection, main, later, left, right):
+def pick(selection, own, left, right):
     main_ref, rest_ref, drift_ref = selection
-    other = jnp.where(drift_ref[0] >= 0, left[...], later[:TAIL, :])
-    rest = jnp.concatenate([right[...], other], axis=0)
-    return dot(main_ref[...], main[...]) + dot(rest_ref[...], rest)
+    other = jnp.where(drift_ref[0] >= 0, left, own[TOK_DEV : TOK_DEV + TAIL])
+    rest = jnp.concatenate([right, other], axis=0)
+    return dot(main_ref[...], own[:TOK_DEV]) + dot(rest_ref[...], rest)
 
 
 def feature_map_pair(map_ref, pair_ref):
@@ -185,35 +185,40 @@
     return jnp.exp(dot(jnp.concatenate([twice, twice], axis=1), pair_ref[...]) * scale)
 
 
-def state_kernel(where_ref, lengths_ref, map_ref, *refs):
-    keys, values, (out_ref, pair, *selection) = refs[:4], refs[4:8], refs[8:]
-
-    @pl.when(pl.program_id(0) == 0)
-    def _():
-        build_selection(lengths_ref, where_ref[0], *selection)
-        feature_map_pair(map_ref, pair)
-
+def state_kernel(
+    where_ref, lengths_ref, map_ref, rows_ref, left_ref, right_ref, out_ref, pair, *selection
+):
+    build_selection(lengths_ref, where_ref[0], *selection)
+    feature_map_pair(map_ref, pair)
     first = where_ref[1]
     valid = lax.broadcasted_iota(I32, (TOK_DEV, 1), 0) >= first
     norm_rows = jnp.where(
         lax.broadcasted_iota(I32, (AUG - DH, TOK_DEV), 1) >= first, 1.0, 0.0
     ).astype(BF16)
-    keys = pick(selection, *keys)
-    values = pick(selection, *values)
-    for i in range(HB):
-        columns = slice(i * DH, (i + 1) * DH)
-        high, low = split(features(keys[:, columns], pair))
-        masked = jnp.where(valid, values[:, columns], 0.0)
-        turned = jnp.concatenate([masked.T.astype(BF16), norm_rows], axis=0)
-        total = dot(turned, high) + dot(turned, low)
-        out_ref[i] = encode(total[:DH], total[DH : DH + 1])
+    width = HB * DH
+    for at in range(H // HB):
+        keys, values = (
+            pick(
+                selection,
+                rows_ref[: TOK_DEV + LATER, start : start + width],
+                left_ref[:, start : start + width],
+                right_ref[:, start : start + width],
+            )
+            for start in (H * DH + at * width, 2 * H * DH + at * width)
+        )
+        for i in range(HB):
+            columns = slice(i * DH, (i + 1) * DH)
+            high, low = split(features(keys[:, columns], pair))
+            masked = jnp.where(valid, values[:, columns], 0.0)
+            turned = jnp.concatenate([masked.T.astype(BF16), norm_rows], axis=0)
+            total = dot(turned, high) + dot(turned, low)
+            out_ref[at * HB + i] = encode(total[:DH], total[DH : DH + 1])
 
 
 def part_specs(part, first):
     column = part * (H // HB) + first
     return [
-        pl.BlockSpec((TOK_DEV, HB * DH), lambda i, *_: (0, column + i)),
-        pl.BlockSpec((LATER, HB * DH), lambda i, *_: (TOK_DEV // LATER, column + i)),
+        pl.BlockSpec((TOK_DEV + LATER, HB * DH), lambda i, *_: (0, column + i)),
         pl.BlockSpec((TAIL, HB * DH), lambda i, *_: (0, column + i)),
         pl.BlockSpec((DRIFT, HB * DH), lambda i, *_: (0, column + i)),
     ]
@@ -230,27 +235,24 @@
 
 def local_states(where, lengths, feature_map, rows, left, right):
     smem = pl.BlockSpec(memory_space=pltpu.SMEM)
+    vmem = pl.BlockSpec(memory_space=pltpu.VMEM)
+    whole = lambda *shape: pl.BlockSpec(shape, lambda i: (0,) * len(shape))
     return pl.pallas_call(
         state_kernel,
         out_shape=pltpu.HBM((H, CODED, M), I16),
-        grid=(H // HB,),
-        in_specs=[
-            smem,
-            smem,
-            pl.BlockSpec((DH, M), lambda i: (0, 0)),
-            *part_specs(1, 0),
-            *part_specs(2, 0),
-        ],
-        out_specs=pl.BlockSpec((HB, CODED, M), lambda i: (i, 0, 0)),
+        grid=(1,),
+        in_specs=[smem, smem, whole(DH, M), vmem, vmem, whole(DRIFT, 3 * H * DH)],
+        out_specs=whole(H, CODED, M),
         scratch_shapes=selection_scratch(),
-        compiler_params=pltpu.CompilerParams(vmem_limit_bytes=12 << 20),
+        compiler_params=pltpu.CompilerParams(vmem_limit_bytes=24 << 20),
         name="local_states",
-    )(where, lengths, in_hbm(feature_map), *([rows, rows, left, right] * 2))
+    )(where, lengths, in_hbm(feature_map), rows, left, right)
 
 
 def attention_kernel(where_ref, lengths_ref, nets_ref, map_ref, *refs):
-    queries, keys, values = refs[:4], refs[4:8], refs[8:12]
-    high_ref, low_ref, out_ref, norm_ref, begin_ref, pair, *selection = refs[12:]
+    queries, keys, values = refs[:3], refs[3:6], refs[6:9]
+    feature_ref, out_ref, begin_ref, pair, *selection = refs[9:]
+    norm_ref = out_ref.at[H // 2]
 
     @pl.when(pl.program_id(0) == 0)
     def _():
@@ -274,15 +276,15 @@
     key = lax.broadcasted_iota(I32, (TOK_DEV, TOK_DEV), 1)
     allowed = (key <= query) & (key.astype(F32) >= begin_ref[:, :1])
     lane = lax.broadcasted_iota(I32, (TOK_DEV, DH), 1)
-    queries = pick(selection, *queries)
-    keys = pick(selection, *keys)
-    values = pick(selection, *values)
+    queries, keys, values = (
+        pick(selection, *(ref[...] for ref in part)) for part in (queries, keys, values)
+    )
     for i in range(HB):
         columns = slice(i * DH, (i + 1) * DH)
         q_high, q_low = split(features(queries[:, columns], pair))
         k_high, k_low = split(features(keys[:, columns], pair))
-        high_ref[i] = q_high
-        low_ref[i] = q_low
+        feature_ref[i, 0] = q_high
+        feature_ref[i, 1] = q_low
         scores = dot_nt(q_high, k_high) + dot_nt(q_high, k_low) + dot_nt(q_low, k_high)
         s_high, s_low = split(jnp.where(allowed, scores, 0.0))
         value = jnp.concatenate(
@@ -295,33 +297,25 @@
 
 
 def local_attention(where, lengths, nets, feature_map, rows, left, right, half):
-    steps = H // HB // 2
-    by_head = lambda width: pl.BlockSpec((HB, TOK_DEV, width), lambda i: (i, 0, 0))
     smem = pl.BlockSpec(memory_space=pltpu.SMEM)
-    specs = [spec for part in range(3) for spec in part_specs(part, half * steps)]
+    whole = lambda *shape: pl.BlockSpec(shape, lambda i: (0,) * len(shape))
+    specs = [spec for part in range(3) for spec in part_specs(part, half)]
     return pl.pallas_call(
         attention_kernel,
         out_shape=(
-            pltpu.HBM((H // 2, TOK_DEV, M), BF16),
-            pltpu.HBM((H // 2, TOK_DEV, M), BF16),
-            pltpu.HBM((H // 2, TOK_DEV, DH), F32),
-            pltpu.HBM((TOK_DEV, DH), F32),
+            pltpu.HBM((H // 2, 2, TOK_DEV, M), BF16),
+            pltpu.HBM((H // 2 + 1, TOK_DEV, DH), F32),
         ),
-        grid=(steps,),
-        in_specs=[smem, smem, smem, pl.BlockSpec((DH, M), lambda i: (0, 0)), *specs],
-        out_specs=(
-            by_head(M),
-            by_head(M),
-            by_head(DH),
-            pl.BlockSpec((TOK_DEV, DH), lambda i: (0, 0)),
-        ),
+        grid=(1,),
+        in_specs=[smem, smem, smem, whole(DH, M), *specs],
+        out_specs=(whole(H // 2, 2, TOK_DEV, M), whole(H // 2 + 1, TOK_DEV, DH)),
         scratch_shapes=[pltpu.VMEM((TOK_DEV, 8), F32)] + selection_scratch(),
-        compiler_params=pltpu.CompilerParams(vmem_limit_bytes=20 << 20),
+        compiler_params=pltpu.CompilerParams(vmem_limit_bytes=24 << 20),
         cost_estimate=pl.CostEstimate(
             flops=3_000_000_000, transcendentals=500_000, bytes_accessed=4_000_000
         ),
         name="local_attention",
-    )(where, lengths, nets, in_hbm(feature_map), *([rows, rows, left, right] * 3))
+    )(where, lengths, nets, in_hbm(feature_map), *([rows, left, right] * 3))
 
 
 def tail_kernel(where_ref, states_ref, out_ref):
@@ -345,21 +339,25 @@
     )(where, states)
 
 
-def prefix_kernel(
-    where_ref, states_ref, near_ref, far_ref, state_ref, norm_ref, out_ref, running, running_norm
-):
+def prefix_kernel(where_ref, states_ref, near_ref, far_ref, state_ref, norm_ref, out_ref, carried, sem):
     near, near_norm = decode(near_ref[...])
     far, far_norm = decode(far_ref[...])
     reaches = where_ref[2] == 0
-    running[...] = near + jnp.where(reaches, far, 0.0)
-    running_norm[...] = near_norm + jnp.where(reaches, far_norm, 0.0)
-
-    @pl.when(where_ref[3] != 0)
+    state = near + jnp.where(reaches, far, 0.0)
+    norm = near_norm + jnp.where(reaches, far_norm, 0.0)
+    head = where_ref[12]
+    first = where_ref[3] != 0
+    carried[...] = jnp.zeros_like(carried)
+
+    @pl.when(first)
     def _():
-        running[...] += state_ref[0].T
-        running_norm[...] += norm_ref[0]
-
-    state, norm = running[...], running_norm[...]
+        copy = pltpu.make_async_copy(state_ref.at[head], carried, sem)
+        copy.start()
+        copy.wait()
+
+    mine = lax.broadcasted_iota(I32, (H, M), 0) == jnp.where(first, head, -1)
+    norm = norm + jnp.sum(jnp.where(mine, norm_ref[...], 0.0), axis=0, keepdims=True)
+    state = state + carried[...].T
     for j in range(GROUP):
         out_ref[j] = encode(state, norm)
         if j < GROUP - 1:
@@ -370,75 +368,60 @@
 
 
 def entering_states(where, states, near, far, carried_state, carried_norm):
-    by_group = pl.BlockSpec((GROUP, CODED, HALF), lambda i, where: (0, 0, i))
-    one = pl.BlockSpec((CODED, HALF), lambda i, where: (0, i))
+    vmem = pl.BlockSpec(memory_space=pltpu.VMEM)
     return pl.pallas_call(
         prefix_kernel,
         out_shape=jax.ShapeDtypeStruct((GROUP, CODED, M), I16),
-        grid_spec=pltpu.PrefetchScalarGridSpec(
-            num_scalar_prefetch=1,
-            grid=(M // HALF,),
-            in_specs=[
-                by_group,
-                one,
-                one,
-                pl.BlockSpec((1, HALF, DH), lambda i, where: (where[12], i, 0)),
-                pl.BlockSpec((1, 1, HALF), lambda i, where: (where[12], 0, i)),
-            ],
-            out_specs=by_group,
-            scratch_shapes=[pltpu.VMEM((DH, HALF), F32), pltpu.VMEM((1, HALF), F32)],
-        ),
+        in_specs=[
+            pl.BlockSpec(memory_space=pltpu.SMEM),
+            vmem,
+            vmem,
+            vmem,
+            pl.BlockSpec(memory_space=pl.ANY),
+            vmem,
+        ],
+        out_specs=vmem,
+        scratch_shapes=[pltpu.VMEM((M, DH), F32), pltpu.SemaphoreType.DMA(())],
         name="entering_states",
-    )(where, states, near, far, carried_state, carried_norm.reshape(H, 1, M))
+    )(where, states, near, far, in_hbm(carried_state), carried_norm)
 
 
 def finish_kernel(where_ref, state_ref, *refs):
     *halves, out_ref = refs
     carried = lax.broadcasted_iota(I32, (TOK_DEV, 1), 0) < where_ref[13]
     lane = lax.broadcasted_iota(I32, (TOK_DEV, DH), 1)
-    step = pl.program_id(0)
-
-    def run(high_ref, low_ref, local_ref, local_norm_ref, before):
-        for i in range(HB):
-            mine = lane == (step - before) * HB + i
-            local_norm = jnp.sum(
-                jnp.where(mine, local_norm_ref[...], 0.0), axis=1, keepdims=True
-            )
+
+    def run(feature_ref, local_ref):
+        norms = local_ref[H // 2]
+        for i in range(H // 2):
+            local_norm = jnp.sum(jnp.where(lane == i, norms, 0.0), axis=1, keepdims=True)
             state, norm = decode(state_ref[i])
             state = jnp.concatenate([state, jnp.broadcast_to(norm, (DH, M))], axis=0)
             s_high, s_low = split(state)
-            q_high = high_ref[i]
-            entering = dot_nt(q_high, s_high) + dot_nt(q_high, s_low) + dot_nt(low_ref[i], s_high)
+            q_high, q_low = feature_ref[i, 0], feature_ref[i, 1]
+            entering = dot_nt(q_high, s_high) + dot_nt(q_high, s_low) + dot_nt(q_low, s_high)
             entering = jnp.where(carried, entering, 0.0)
             total = local_ref[i] + entering[:, :DH]
             out_ref[:, i * DH : (i + 1) * DH] = total / (local_norm + entering[:, DH:])
 
-    steps = H // HB // 2
-    pl.when(step < steps)(lambda: run(*halves[:4], 0))
-    pl.when(step >= steps)(lambda: run(*halves[4:], steps))
+    pl.when(pl.program_id(0) == 0)(lambda: run(*halves[:2]))
+    pl.when(pl.program_id(0) == 1)(lambda: run(*halves[2:]))
 
 
 def finish(where, states, *halves):
-    steps = H // HB // 2
-
-    def specs(half):
-        top = lambda i: jnp.minimum(i, steps - 1) if half == 0 else jnp.maximum(i - steps, 0)
-        by_head = lambda width: pl.BlockSpec((HB, TOK_DEV, width), lambda i: (top(i), 0, 0))
-        whole = pl.BlockSpec((TOK_DEV, DH), lambda i: (0, 0))
-        return [by_head(M), by_head(M), by_head(DH), whole]
-
+    half = H // 2
+    whole = lambda *shape: pl.BlockSpec(shape, lambda i: (0,) * len(shape))
     return pl.pallas_call(
         finish_kernel,
         out_shape=jax.ShapeDtypeStruct((TOK_DEV, H * DH), F32),
-        grid=(H // HB,),
+        grid=(2,),
         in_specs=[
             pl.BlockSpec(memory_space=pltpu.SMEM),
-            pl.BlockSpec((HB, CODED, M), lambda i: (i, 0, 0)),
-            *specs(0),
-            *specs(1),
+            pl.BlockSpec((half, CODED, M), lambda i: (i, 0, 0)),
+            *([whole(half, 2, TOK_DEV, M), whole(half + 1, TOK_DEV, DH)] * 2),
         ],
-        out_specs=pl.BlockSpec((TOK_DEV, HB * DH), lambda i: (0, i)),
-        compiler_params=pltpu.CompilerParams(vmem_limit_bytes=20 << 20),
+        out_specs=pl.BlockSpec((TOK_DEV, half * DH), lambda i: (0, i)),
+        compiler_params=pltpu.CompilerParams(vmem_limit_bytes=24 << 20),
         name="finish",
     )(where, states, *(in_hbm(half) for half in halves))
 
@@ -458,7 +441,7 @@
     left = shifted(tail, "seq", SHARDS, 1)
     right = shifted(head, "seq", SHARDS, -1)
     lengths = lax.all_to_all(length, "seq", 0, 0, tiled=True)
-    where = net_flags(device.astype(I32)[None], net_lengths)
+    where = in_hbm(net_flags(device.astype(I32)[None], net_lengths))
     states = local_states(where, lengths, feature_map, loader_rows, left, right)
     states = lax.all_to_all(states, "seq", 0, 0, axis_index_groups=groups, tiled=True)
     attend = functools.partial(
@@ -470,11 +453,9 @@
     tail = group_tail(where, states)
     far = shifted(tail, ("grp", "seq"), DEVICES, 2 * GROUP)
     near = shifted(tail, ("grp", "seq"), DEVICES, GROUP)
-    second = attend(1)
-    near, far, *second = lax.optimization_barrier((near, far, *second))
     states = entering_states(where, states, near, far, carried_state, carried_norm)
     states = lax.all_to_all(states, "seq", 0, 0, axis_index_groups=groups, tiled=True)
-    return finish(where, states, *first, *second)
+    return finish(where, states, *first, *attend(1))
 
 
 def solution(mesh):

time: 92 us -> 88.4 us (0.961)
  the two profiles are of different devices: /device:TPU:32 before, /device:TPU:16 now
where the time goes in v4:
time: 88.4 us; the launch traced here: 87.9 us
  starting transfers between devices  37.1 us (42%)
  Pallas kernels  27.6 us (31%)
  waiting for transfers between devices  22.3 us (25%)
  between operations  0.9 us (1%)
    all_to_all x1, starting transfers between devices, local(): lengths = lax.all_to_all(length, 'seq', 0, 0, tiled=True)  15.1 us
    ppermute x4, starting transfers between devices, shifted(): lax.ppermute(block, axis, [(i - distance, i) for i in range(ahead, count...  11.7 us
    pallas_call x2, Pallas kernels, local_attention(): pl.pallas_call(attention_kernel, out_shape=(pltpu.HBM((H // 2, 2, TOK_DEV...  10.8 us
    all_to_all x2, starting transfers between devices, local(): lax.all_to_all(states, 'seq', 0, 0, axis_index_groups=groups, tiled=True)  10.3 us
    all_to_all x2, waiting for transfers between devices, local(): lax.all_to_all(states, 'seq', 0, 0, axis_index_groups=groups, tiled=True)  7.75 us
    all_to_all x1, waiting for transfers between devices, local(): lengths = lax.all_to_all(length, 'seq', 0, 0, tiled=True)  7.66 us
    ppermute x4, waiting for transfers between devices, shifted(): lax.ppermute(block, axis, [(i - distance, i) for i in range(ahead, count...  6.87 us
    pallas_call x1, Pallas kernels, finish(): pl.pallas_call(finish_kernel, out_shape=jax.ShapeDtypeStruct((TOK_DEV, H...  4.18 us
  transfers between devices with their start and end apart: 7, of which 5 were waited for; matrix products, arithmetic and copies ran while one was open for 0% of the time, Pallas kernels for 15%

profile of v4, /device:TPU:16, one launch (start us, length us, event | category | flops | bytes accessed | tf_op | source)
XLA Modules:
  0.0 87.9 jit_solution(8653296308927375477)
XLA Ops:
  0.0 0.0 copy-start
  0.8 2.3 %windows.1 = (bf16[104,3072]{1,0:T(8,128)(2,1)}, bf16[96,3072]{1,0:T(8,128)(2,1)}, s32[32,1,1]{2,1,0:T(1,128)}) custom-call(s32[1,1]{1,0:T(1,128)S(6)} %copy.7.length_ref, bf16[448,3072]{1,0:T(8,128)(2,1)} %refs_6_.3), custom_call_target="tpu_custom_call" | custom-call | tf_op jit(solution)/shard_map/windows/pallas_call | solution.py:69
  3.1 3.4 %collective-permute-start = (bf16[104,3072]{1,0:T(8,128)(2,1)}, bf16[104,3072]{1,0:T(8,128)(2,1)S(1)}, u32[]{:S(2)}, u32[]{:S(2)}) collective-permute-start(bf16[104,3072]{1,0:T(8,128)(2,1)} %get-tuple-element.16), channel_id=1, source_target_pairs={{0,1},{1,2},{2,3},{3,4},{4,5},{5,6},{6,7},{7,8},{8,9},{9,10},{10,1... | collective-permute-start | bytes 1916936 | tf_op jit(solution)/shard_map/ppermute | solution.py:431
  6.6 1.3 %collective-permute-start.1 = (bf16[96,3072]{1,0:T(8,128)(2,1)}, bf16[96,3072]{1,0:T(8,128)(2,1)}, u32[]{:S(2)}, u32[]{:S(2)}) collective-permute-start(bf16[96,3072]{1,0:T(8,128)(2,1)} %get-tuple-element.17), channel_id=1, source_target_pairs={{1,0},{2,1},{3,2},{4,3},{5,4},{6,5},{7,6},{8,7},{9,8},{10,9},{11,1... | collective-permute-start | bytes 1769480 | tf_op jit(solution)/shard_map/ppermute | solution.py:431
  7.9 15.1 %all-to-all-start = ((s32[32,1,1]{2,1,0:T(1,128)}), s32[32,1,1]{2,1,0:T(1,128)S(1)}, u32[]{:S(2)}, u32[]{:S(2)}) async-start(s32[32,1,1]{2,1,0:T(1,128)} %get-tuple-element.15), calls=%async_computation | async-start | bytes 32768 | tf_op jit(solution)/shard_map/all_to_all | solution.py:443
  23.0 2.1 %net_flags.1.where_ref = s32[16]{0:T(128)} custom-call(s32[1]{0:T(128)} %bitcast.place_ref, s32[64]{0:T(128)} %nets_ref.5), custom_call_target="tpu_custom_call" | custom-call | tf_op jit(solution)/shard_map/net_flags/pallas_call | solution.py:119
  25.1 0.0 copy-start.1
  25.1 7.7 %all-to-all-done.lengths_ref = s32[32,1,1]{2,1,0:T(1,128)S(1)} async-done(((s32[32,1,1]{2,1,0:T(1,128)}), s32[32,1,1]{2,1,0:T(1,128)S(1)}, u32[]{:S(2)}, u32[]{:S(2)}) %all-to-all-start) | async-done | bytes 160 | tf_op jit(solution)/shard_map/all_to_all | solution.py:443
  32.8 0.0 collective-permute-done.1.right_ref.refs_2_.refs_5_.refs_8_
  32.8 0.0 collective-permute-done.left_ref.refs_1_.refs_4_.refs_7_
  32.8 0.0 copy-done
  32.8 3.8 %local_states.1 = s16[8,144,256]{2,1,0:T(8,128)(2,1)} custom-call(s32[16]{0:T(128)} %net_flags.1.where_ref, s32[32,1,1]{2,1,0:T(1,128)S(1)} %all-to-all-done.lengths_ref, f32[128,256]{1,0:T(8,128)} %map_ref.5, bf16[448,3072]{1,0:T(8,128)(2,1)S(1)} %copy-done, bf16[104,3072]{1,0:T(8,128)(2,1)S(1)} %collective-permute-done.left_ref.refs_1_.refs_4_.refs_7_, ...), custom_call_target="tpu_custom_call" | custom-call | tf_op jit(solution)/shard_map/local_states/pallas_call | solution.py:240
  36.6 6.1 %all-to-all-start.1 = ((s16[8,144,256]{2,1,0:T(8,128)(2,1)}), s16[8,144,256]{2,1,0:T(8,128)(2,1)}, u32[]{:S(2)}, u32[]{:S(2)}) async-start(s16[8,144,256]{2,1,0:T(8,128)(2,1)} %local_states.1), calls=%async_computation.1 | async-start | bytes 1179648 | tf_op jit(solution)/shard_map/all_to_all | solution.py:446
  42.6 0.0 copy-done.1
  42.6 5.4 %local_attention.2 = (bf16[4,2,256,256]{3,2,1,0:T(8,128)(2,1)}, f32[5,256,128]{2,1,0:T(8,128)}) custom-call(s32[16]{0:T(128)} %net_flags.1.where_ref, s32[32,1,1]{2,1,0:T(1,128)S(1)} %all-to-all-done.lengths_ref, s32[64]{0:T(128)S(1)} %copy-done.1, f32[128,256]{1,0:T(8,128)} %map_ref.5, bf16[448,3072]{1,0:T(8,128)(2,1)S(1)} %copy-done, ...), custom_call_target="tpu_custom_call" | custom-call | flops 3000000000 | bytes 4000000 | tf_op jit(solution)/shard_map/local_attention/pallas_call | solution.py:303
  48.0 3.4 %all-to-all-done.1.states_ref = s16[8,144,256]{2,1,0:T(8,128)(2,1)} async-done(((s16[8,144,256]{2,1,0:T(8,128)(2,1)}), s16[8,144,256]{2,1,0:T(8,128)(2,1)}, u32[]{:S(2)}, u32[]{:S(2)}) %all-to-all-start.1) | async-done | bytes 589856 | tf_op jit(solution)/shard_map/all_to_all | solution.py:446
  51.4 2.0 %group_tail.1 = s16[144,256]{1,0:T(8,128)(2,1)} custom-call(s32[16]{0:T(128)} %net_flags.1.where_ref, s16[8,144,256]{2,1,0:T(8,128)(2,1)} %all-to-all-done.1.states_ref), custom_call_target="tpu_custom_call" | custom-call | tf_op jit(solution)/shard_map/group_tail/pallas_call | solution.py:333
  53.4 4.5 %collective-permute-start.3 = (s16[144,256]{1,0:T(8,128)(2,1)}, s16[144,256]{1,0:T(8,128)(2,1)S(1)}, u32[]{:S(2)}, u32[]{:S(2)}) collective-permute-start(s16[144,256]{1,0:T(8,128)(2,1)} %group_tail.1), channel_id=1, source_target_pairs={{0,16},{1,17},{2,18},{3,19},{4,20},{5,21},{6,22},{7,23},{8,24},{9,... | collective-permute-start | bytes 221192 | tf_op jit(solution)/shard_map/ppermute | solution.py:431
  57.9 2.5 %collective-permute-start.2 = (s16[144,256]{1,0:T(8,128)(2,1)}, s16[144,256]{1,0:T(8,128)(2,1)}, u32[]{:S(2)}, u32[]{:S(2)}) collective-permute-start(s16[144,256]{1,0:T(8,128)(2,1)} %group_tail.1), channel_id=1, source_target_pairs={{0,8},{1,9},{2,10},{3,11},{4,12},{5,13},{6,14},{7,15},{8,16},{9,17... | collective-permute-start | bytes 221192 | tf_op jit(solution)/shard_map/ppermute | solution.py:431
  60.4 4.6 %collective-permute-done.3.far_ref = s16[144,256]{1,0:T(8,128)(2,1)S(1)} collective-permute-done((s16[144,256]{1,0:T(8,128)(2,1)}, s16[144,256]{1,0:T(8,128)(2,1)S(1)}, u32[]{:S(2)}, u32[]{:S(2)}) %collective-permute-start.3) | collective-permute-done | bytes 73760 | tf_op jit(solution)/shard_map/ppermute | solution.py:431
  65.0 0.0 copy-start.2
  65.0 2.3 %collective-permute-done.2.near_ref = s16[144,256]{1,0:T(8,128)(2,1)} collective-permute-done((s16[144,256]{1,0:T(8,128)(2,1)}, s16[144,256]{1,0:T(8,128)(2,1)}, u32[]{:S(2)}, u32[]{:S(2)}) %collective-permute-start.2) | collective-permute-done | bytes 73760 | tf_op jit(solution)/shard_map/ppermute | solution.py:431
  67.3 0.0 copy-done.2
  67.3 2.4 %entering_states.1 = s16[8,144,256]{2,1,0:T(8,128)(2,1)} custom-call(s32[16]{0:T(128)} %net_flags.1.where_ref, s16[8,144,256]{2,1,0:T(8,128)(2,1)} %all-to-all-done.1.states_ref, s16[144,256]{1,0:T(8,128)(2,1)} %collective-permute-done.2.near_ref, s16[144,256]{1,0:T(8,128)(2,1)} %copy-done.2, f32[8,256,128]{2,1,0:T(8,128)} %state_ref.1, f32[8,256]{1,0:T(8,128)} %norm_ref.1), custom_call_target="tpu_custom_call" | custom-call | tf_op jit(solution)/shard_map/entering_states/pallas_call | solution.py:372
  69.7 4.2 %all-to-all-start.2 = ((s16[8,144,256]{2,1,0:T(8,128)(2,1)}), s16[8,144,256]{2,1,0:T(8,128)(2,1)}, u32[]{:S(2)}, u32[]{:S(2)}) async-start(s16[8,144,256]{2,1,0:T(8,128)(2,1)} %entering_states.1), calls=%async_computation.2 | async-start | bytes 1179648 | tf_op jit(solution)/shard_map/all_to_all | solution.py:457
  73.9 5.4 %local_attention.3 = (bf16[4,2,256,256]{3,2,1,0:T(8,128)(2,1)}, f32[5,256,128]{2,1,0:T(8,128)}) custom-call(s32[16]{0:T(128)} %net_flags.1.where_ref, s32[32,1,1]{2,1,0:T(1,128)S(1)} %all-to-all-done.lengths_ref, s32[64]{0:T(128)S(1)} %copy-done.1, f32[128,256]{1,0:T(8,128)} %map_ref.5, bf16[448,3072]{1,0:T(8,128)(2,1)S(1)} %copy-done, ...), custom_call_target="tpu_custom_call" | custom-call | flops 3000000000 | bytes 4000000 | tf_op jit(solution)/shard_map/local_attention/pallas_call | solution.py:303
  79.3 4.4 %all-to-all-done.2.state_ref = s16[8,144,256]{2,1,0:T(8,128)(2,1)} async-done(((s16[8,144,256]{2,1,0:T(8,128)(2,1)}), s16[8,144,256]{2,1,0:T(8,128)(2,1)}, u32[]{:S(2)}, u32[]{:S(2)}) %all-to-all-start.2) | async-done | bytes 589856 | tf_op jit(solution)/shard_map/all_to_all | solution.py:457
  83.7 4.2 %finish.1 = f32[256,1024]{1,0:T(8,128)} custom-call(s32[16]{0:T(128)} %net_flags.1.where_ref, s16[8,144,256]{2,1,0:T(8,128)(2,1)} %all-to-all-done.2.state_ref, bf16[4,2,256,256]{3,2,1,0:T(8,128)(2,1)} %get-tuple-element.21.refs_0_, f32[5,256,128]{2,1,0:T(8,128)} %get-tuple-element.22.refs_1_, bf16[4,2,256,256]{3,2,1,0:T(8,128)(2,1)} %get-tuple-element.23.refs_2_, ...), custom_call_target="tpu_custom_call" | custom-call | tf_op jit(solution)/shard_map/finish/pallas_call | solution.py:414
Async XLA Ops:
  0.0 32.8 %copy-start = (bf16[448,3072]{1,0:T(8,128)(2,1)S(1)}, bf16[448,3072]{1,0:T(8,128)(2,1)}, u32[]{:S(2)}) copy-start(bf16[448,3072]{1,0:T(8,128)(2,1)} %refs_6_.3) | copy-start | bytes 8257540
  3.1 29.6 %collective-permute-start = (bf16[104,3072]{1,0:T(8,128)(2,1)}, bf16[104,3072]{1,0:T(8,128)(2,1)S(1)}, u32[]{:S(2)}, u32[]{:S(2)}) collective-permute-start(bf16[104,3072]{1,0:T(8,128)(2,1)} %get-tuple-element.16), channel_id=1, source_target_pairs={{0,1},{1,2},{2,3},{3,4},{4,5},{5,6},{6,7},{7,8},{8,9},{9,10},{10,1... | collective-permute-start | bytes 1916936 | tf_op jit(solution)/shard_map/ppermute | solution.py:431
  6.6 26.2 %collective-permute-start.1 = (bf16[96,3072]{1,0:T(8,128)(2,1)}, bf16[96,3072]{1,0:T(8,128)(2,1)}, u32[]{:S(2)}, u32[]{:S(2)}) collective-permute-start(bf16[96,3072]{1,0:T(8,128)(2,1)} %get-tuple-element.17), channel_id=1, source_target_pairs={{1,0},{2,1},{3,2},{4,3},{5,4},{6,5},{7,6},{8,7},{9,8},{10,9},{11,1... | collective-permute-start | bytes 1769480 | tf_op jit(solution)/shard_map/ppermute | solution.py:431
  7.9 24.9 %all-to-all-start = ((s32[32,1,1]{2,1,0:T(1,128)}), s32[32,1,1]{2,1,0:T(1,128)S(1)}, u32[]{:S(2)}, u32[]{:S(2)}) async-start(s32[32,1,1]{2,1,0:T(1,128)} %get-tuple-element.15), calls=%async_computation | async-start | bytes 32768 | tf_op jit(solution)/shard_map/all_to_all | solution.py:443
  25.1 17.5 %copy-start.1 = (s32[64]{0:T(128)S(1)}, s32[64]{0:T(128)}, u32[]{:S(2)}) copy-start(s32[64]{0:T(128)} %nets_ref.5) | copy-start | bytes 772
  36.6 14.8 %all-to-all-start.1 = ((s16[8,144,256]{2,1,0:T(8,128)(2,1)}), s16[8,144,256]{2,1,0:T(8,128)(2,1)}, u32[]{:S(2)}, u32[]{:S(2)}) async-start(s16[8,144,256]{2,1,0:T(8,128)(2,1)} %local_states.1), calls=%async_computation.1 | async-start | bytes 1179648 | tf_op jit(solution)/shard_map/all_to_all | solution.py:446
  53.4 11.6 %collective-permute-start.3 = (s16[144,256]{1,0:T(8,128)(2,1)}, s16[144,256]{1,0:T(8,128)(2,1)S(1)}, u32[]{:S(2)}, u32[]{:S(2)}) collective-permute-start(s16[144,256]{1,0:T(8,128)(2,1)} %group_tail.1), channel_id=1, source_target_pairs={{0,16},{1,17},{2,18},{3,19},{4,20},{5,21},{6,22},{7,23},{8,24},{9,... | collective-permute-start | bytes 221192 | tf_op jit(solution)/shard_map/ppermute | solution.py:431
  57.9 9.4 %collective-permute-start.2 = (s16[144,256]{1,0:T(8,128)(2,1)}, s16[144,256]{1,0:T(8,128)(2,1)}, u32[]{:S(2)}, u32[]{:S(2)}) collective-permute-start(s16[144,256]{1,0:T(8,128)(2,1)} %group_tail.1), channel_id=1, source_target_pairs={{0,8},{1,9},{2,10},{3,11},{4,12},{5,13},{6,14},{7,15},{8,16},{9,17... | collective-permute-start | bytes 221192 | tf_op jit(solution)/shard_map/ppermute | solution.py:431
  65.0 2.3 %copy-start.2 = (s16[144,256]{1,0:T(8,128)(2,1)}, s16[144,256]{1,0:T(8,128)(2,1)S(1)}, u32[]{:S(2)}) copy-start(s16[144,256]{1,0:T(8,128)(2,1)S(1)} %collective-permute-done.3.far_ref) | copy-start | bytes 221188
  69.7 14.0 %all-to-all-start.2 = ((s16[8,144,256]{2,1,0:T(8,128)(2,1)}), s16[8,144,256]{2,1,0:T(8,128)(2,1)}, u32[]{:S(2)}, u32[]{:S(2)}) async-start(s16[8,144,256]{2,1,0:T(8,128)(2,1)} %entering_states.1), calls=%async_computation.2 | async-start | bytes 1179648 | tf_op jit(solution)/shard_map/all_to_all | solution.py:457

commit v5 on v4

--- a/solution.py
+++ b/solution.py
@@ -21,7 +21,7 @@
 REST = DRIFT + TAIL
 LATER = 128
 AUG = 136
-CODED = 144
+CODED = 136
 HB = 4
 HALF = M // 2
 F32 = jnp.float32
@@ -251,7 +251,8 @@
 
 def attention_kernel(where_ref, lengths_ref, nets_ref, map_ref, *refs):
     queries, keys, values = refs[:3], refs[3:6], refs[6:9]
-    feature_ref, out_ref, begin_ref, pair, *selection = refs[9:]
+    feature_ref, sums_ref, begin_ref, pair, *selection = refs[-7:]
+    out_ref = sums_ref.at[0]
     norm_ref = out_ref.at[H // 2]
 
     @pl.when(pl.program_id(0) == 0)
@@ -296,26 +297,29 @@
         norm_ref[...] = jnp.where(mine, total[:, DH:], norm_ref[...])
 
 
-def local_attention(where, lengths, nets, feature_map, rows, left, right, half):
+def local_attention(where, lengths, nets, feature_map, rows, left, right, half, earlier=()):
     smem = pl.BlockSpec(memory_space=pltpu.SMEM)
     whole = lambda *shape: pl.BlockSpec(shape, lambda i: (0,) * len(shape))
-    specs = [spec for part in range(3) for spec in part_specs(part, half)]
+    part = lambda *shape: pl.BlockSpec(shape, lambda i: (half,) + (0,) * (len(shape) - 1))
+    specs = [spec for part_at in range(3) for spec in part_specs(part_at, half)]
     return pl.pallas_call(
         attention_kernel,
         out_shape=(
-            pltpu.HBM((H // 2, 2, TOK_DEV, M), BF16),
-            pltpu.HBM((H // 2 + 1, TOK_DEV, DH), F32),
+            pltpu.HBM((H, 2, TOK_DEV, M), BF16),
+            pltpu.HBM((2, H // 2 + 1, TOK_DEV, DH), F32),
         ),
         grid=(1,),
-        in_specs=[smem, smem, smem, whole(DH, M), *specs],
-        out_specs=(whole(H // 2, 2, TOK_DEV, M), whole(H // 2 + 1, TOK_DEV, DH)),
+        in_specs=[smem, smem, smem, whole(DH, M), *specs]
+        + [pl.BlockSpec(memory_space=pl.ANY)] * len(earlier),
+        out_specs=(part(H // 2, 2, TOK_DEV, M), part(1, H // 2 + 1, TOK_DEV, DH)),
         scratch_shapes=[pltpu.VMEM((TOK_DEV, 8), F32)] + selection_scratch(),
+        input_output_aliases={13 + i: i for i in range(len(earlier))},
         compiler_params=pltpu.CompilerParams(vmem_limit_bytes=24 << 20),
         cost_estimate=pl.CostEstimate(
             flops=3_000_000_000, transcendentals=500_000, bytes_accessed=4_000_000
         ),
         name="local_attention",
-    )(where, lengths, nets, in_hbm(feature_map), *([rows, left, right] * 3))
+    )(where, lengths, nets, in_hbm(feature_map), *([rows, left, right] * 3), *earlier)
 
 
 def tail_kernel(where_ref, states_ref, out_ref):
@@ -383,47 +387,42 @@
         out_specs=vmem,
         scratch_shapes=[pltpu.VMEM((M, DH), F32), pltpu.SemaphoreType.DMA(())],
         name="entering_states",
-    )(where, states, near, far, in_hbm(carried_state), carried_norm)
-
-
-def finish_kernel(where_ref, state_ref, *refs):
-    *halves, out_ref = refs
+    )(where, states, in_hbm(near), in_hbm(far), in_hbm(carried_state), carried_norm)
+
+
+def finish_kernel(where_ref, state_ref, feature_ref, local_ref, out_ref):
     carried = lax.broadcasted_iota(I32, (TOK_DEV, 1), 0) < where_ref[13]
     lane = lax.broadcasted_iota(I32, (TOK_DEV, DH), 1)
-
-    def run(feature_ref, local_ref):
-        norms = local_ref[H // 2]
-        for i in range(H // 2):
-            local_norm = jnp.sum(jnp.where(lane == i, norms, 0.0), axis=1, keepdims=True)
-            state, norm = decode(state_ref[i])
-            state = jnp.concatenate([state, jnp.broadcast_to(norm, (DH, M))], axis=0)
-            s_high, s_low = split(state)
-            q_high, q_low = feature_ref[i, 0], feature_ref[i, 1]
-            entering = dot_nt(q_high, s_high) + dot_nt(q_high, s_low) + dot_nt(q_low, s_high)
-            entering = jnp.where(carried, entering, 0.0)
-            total = local_ref[i] + entering[:, :DH]
-            out_ref[:, i * DH : (i + 1) * DH] = total / (local_norm + entering[:, DH:])
-
-    pl.when(pl.program_id(0) == 0)(lambda: run(*halves[:2]))
-    pl.when(pl.program_id(0) == 1)(lambda: run(*halves[2:]))
-
-
-def finish(where, states, *halves):
+    norms = local_ref[0, H // 2]
+    for i in range(H // 2):
+        local_norm = jnp.sum(jnp.where(lane == i, norms, 0.0), axis=1, keepdims=True)
+        state, norm = decode(state_ref[i])
+        state = jnp.concatenate([state, jnp.broadcast_to(norm, (DH, M))], axis=0)
+        s_high, s_low = split(state)
+        q_high, q_low = feature_ref[i, 0], feature_ref[i, 1]
+        entering = dot_nt(q_high, s_high) + dot_nt(q_high, s_low) + dot_nt(q_low, s_high)
+        entering = jnp.where(carried, entering, 0.0)
+        total = local_ref[0, i] + entering[:, :DH]
+        out_ref[:, i * DH : (i + 1) * DH] = total / (local_norm + entering[:, DH:])
+
+
+def finish(where, states, query_features, sums):
     half = H // 2
-    whole = lambda *shape: pl.BlockSpec(shape, lambda i: (0,) * len(shape))
+    part = lambda *shape: pl.BlockSpec(shape, lambda i: (i,) + (0,) * (len(shape) - 1))
     return pl.pallas_call(
         finish_kernel,
         out_shape=jax.ShapeDtypeStruct((TOK_DEV, H * DH), F32),
         grid=(2,),
         in_specs=[
             pl.BlockSpec(memory_space=pltpu.SMEM),
-            pl.BlockSpec((half, CODED, M), lambda i: (i, 0, 0)),
-            *([whole(half, 2, TOK_DEV, M), whole(half + 1, TOK_DEV, DH)] * 2),
+            part(half, CODED, M),
+            part(half, 2, TOK_DEV, M),
+            part(1, half + 1, TOK_DEV, DH),
         ],
         out_specs=pl.BlockSpec((TOK_DEV, half * DH), lambda i: (0, i)),
         compiler_params=pltpu.CompilerParams(vmem_limit_bytes=24 << 20),
         name="finish",
-    )(where, states, *(in_hbm(half) for half in halves))
+    )(where, states, in_hbm(query_features), in_hbm(sums))
 
 
 def shifted(block, axis, count, distance):
@@ -455,7 +454,7 @@
     near = shifted(tail, ("grp", "seq"), DEVICES, GROUP)
     states = entering_states(where, states, near, far, carried_state, carried_norm)
     states = lax.all_to_all(states, "seq", 0, 0, axis_index_groups=groups, tiled=True)
-    return finish(where, states, *first, *attend(1))
+    return finish(where, states, *attend(1, first))
 
 
 def solution(mesh):

time: 88.4 us -> 87.7 us (level)
  the two profiles are of different devices: /device:TPU:16 before, /device:TPU:32 now
where the time goes in v5:
time: 87.7 us; the launch traced here: 87.2 us
  starting transfers between devices  37.1 us (42%)
  Pallas kernels  27 us (31%)
  waiting for transfers between devices  21.5 us (25%)
  between operations  0.9 us (1%)
    all_to_all x1, starting transfers between devices, local(): lengths = lax.all_to_all(length, 'seq', 0, 0, tiled=True)  15.1 us
    ppermute x4, starting transfers between devices, shifted(): lax.ppermute(block, axis, [(i - distance, i) for i in range(ahead, count...  11.5 us
    pallas_call x2, Pallas kernels, local_attention(): pl.pallas_call(attention_kernel, out_shape=(pltpu.HBM((H, 2, TOK_DEV, M),...  10.8 us
    all_to_all x2, starting transfers between devices, local(): lax.all_to_all(states, 'seq', 0, 0, axis_index_groups=groups, tiled=True)  10.4 us
    ppermute x4, waiting for transfers between devices, shifted(): lax.ppermute(block, axis, [(i - distance, i) for i in range(ahead, count...  7.96 us
    all_to_all x1, waiting for transfers between devices, local(): lengths = lax.all_to_all(length, 'seq', 0, 0, tiled=True)  7.5 us
    all_to_all x2, waiting for transfers between devices, local(): lax.all_to_all(states, 'seq', 0, 0, axis_index_groups=groups, tiled=True)  6.09 us
    pallas_call x1, Pallas kernels, local_states(): pl.pallas_call(state_kernel, out_shape=pltpu.HBM((H, CODED, M), I16), gri...  3.76 us
  transfers between devices with their start and end apart: 7, of which 5 were waited for; matrix products, arithmetic and copies ran while one was open for 0% of the time, Pallas kernels for 15%

profile of v5, /device:TPU:32, one launch (start us, length us, event | category | flops | bytes accessed | tf_op | source)
XLA Modules:
  0.0 87.2 jit_solution(17956131612538280753)
XLA Ops:
  0.0 0.0 copy-start
  0.8 2.3 %windows.1 = (bf16[104,3072]{1,0:T(8,128)(2,1)}, bf16[96,3072]{1,0:T(8,128)(2,1)}, s32[32,1,1]{2,1,0:T(1,128)}) custom-call(s32[1,1]{1,0:T(1,128)S(6)} %copy.11.length_ref, bf16[448,3072]{1,0:T(8,128)(2,1)} %refs_6_.3), custom_call_target="tpu_custom_call" | custom-call | tf_op jit(solution)/shard_map/windows/pallas_call | solution.py:69
  3.1 3.4 %collective-permute-start = (bf16[104,3072]{1,0:T(8,128)(2,1)}, bf16[104,3072]{1,0:T(8,128)(2,1)S(1)}, u32[]{:S(2)}, u32[]{:S(2)}) collective-permute-start(bf16[104,3072]{1,0:T(8,128)(2,1)} %get-tuple-element.16), channel_id=1, source_target_pairs={{0,1},{1,2},{2,3},{3,4},{4,5},{5,6},{6,7},{7,8},{8,9},{9,10},{10,1... | collective-permute-start | bytes 1916936 | tf_op jit(solution)/shard_map/ppermute | solution.py:430
  6.6 1.3 %collective-permute-start.1 = (bf16[96,3072]{1,0:T(8,128)(2,1)}, bf16[96,3072]{1,0:T(8,128)(2,1)}, u32[]{:S(2)}, u32[]{:S(2)}) collective-permute-start(bf16[96,3072]{1,0:T(8,128)(2,1)} %get-tuple-element.17), channel_id=1, source_target_pairs={{1,0},{2,1},{3,2},{4,3},{5,4},{6,5},{7,6},{8,7},{9,8},{10,9},{11,1... | collective-permute-start | bytes 1769480 | tf_op jit(solution)/shard_map/ppermute | solution.py:430
  7.9 15.1 %all-to-all-start = ((s32[32,1,1]{2,1,0:T(1,128)}), s32[32,1,1]{2,1,0:T(1,128)S(1)}, u32[]{:S(2)}, u32[]{:S(2)}) async-start(s32[32,1,1]{2,1,0:T(1,128)} %get-tuple-element.15), calls=%async_computation | async-start | bytes 32768 | tf_op jit(solution)/shard_map/all_to_all | solution.py:442
  23.0 2.1 %net_flags.1.where_ref = s32[16]{0:T(128)} custom-call(s32[1]{0:T(128)} %bitcast.place_ref, s32[64]{0:T(128)} %nets_ref.5), custom_call_target="tpu_custom_call" | custom-call | tf_op jit(solution)/shard_map/net_flags/pallas_call | solution.py:119
  25.1 0.0 copy-start.1
  25.1 7.5 %all-to-all-done.lengths_ref = s32[32,1,1]{2,1,0:T(1,128)S(1)} async-done(((s32[32,1,1]{2,1,0:T(1,128)}), s32[32,1,1]{2,1,0:T(1,128)S(1)}, u32[]{:S(2)}, u32[]{:S(2)}) %all-to-all-start) | async-done | bytes 160 | tf_op jit(solution)/shard_map/all_to_all | solution.py:442
  32.6 0.0 collective-permute-done.1.right_ref.refs_2_.refs_5_.refs_8_
  32.6 0.0 collective-permute-done.left_ref.refs_1_.refs_4_.refs_7_
  32.6 0.0 copy-done
  32.6 3.8 %local_states.1 = s16[8,136,256]{2,1,0:T(8,128)(2,1)} custom-call(s32[16]{0:T(128)} %net_flags.1.where_ref, s32[32,1,1]{2,1,0:T(1,128)S(1)} %all-to-all-done.lengths_ref, f32[128,256]{1,0:T(8,128)} %map_ref.5, bf16[448,3072]{1,0:T(8,128)(2,1)S(1)} %copy-done, bf16[104,3072]{1,0:T(8,128)(2,1)S(1)} %collective-permute-done.left_ref.refs_1_.refs_4_.refs_7_, ...), custom_call_target="tpu_custom_call" | custom-call | tf_op jit(solution)/shard_map/local_states/pallas_call | solution.py:240
  36.4 6.2 %all-to-all-start.1 = ((s16[8,136,256]{2,1,0:T(8,128)(2,1)}), s16[8,136,256]{2,1,0:T(8,128)(2,1)}, u32[]{:S(2)}, u32[]{:S(2)}) async-start(s16[8,136,256]{2,1,0:T(8,128)(2,1)} %local_states.1), calls=%async_computation.1 | async-start | bytes 1114112 | tf_op jit(solution)/shard_map/all_to_all | solution.py:445
  42.6 0.0 copy-done.1
  42.6 5.4 %local_attention.2 = (bf16[8,2,256,256]{3,2,1,0:T(8,128)(2,1)}, f32[2,5,256,128]{3,2,1,0:T(8,128)}) custom-call(s32[16]{0:T(128)} %net_flags.1.where_ref, s32[32,1,1]{2,1,0:T(1,128)S(1)} %all-to-all-done.lengths_ref, s32[64]{0:T(128)S(1)} %copy-done.1, f32[128,256]{1,0:T(8,128)} %map_ref.5, bf16[448,3072]{1,0:T(8,128)(2,1)S(1)} %copy-done, ...), custom_call_target="tpu_custom_call" | custom-call | flops 3000000000 | bytes 4000000 | tf_op jit(solution)/shard_map/local_attention/pallas_call | solution.py:305
  48.0 3.1 %all-to-all-done.1.states_ref = s16[8,136,256]{2,1,0:T(8,128)(2,1)} async-done(((s16[8,136,256]{2,1,0:T(8,128)(2,1)}), s16[8,136,256]{2,1,0:T(8,128)(2,1)}, u32[]{:S(2)}, u32[]{:S(2)}) %all-to-all-start.1) | async-done | bytes 557088 | tf_op jit(solution)/shard_map/all_to_all | solution.py:445
  51.1 2.0 %group_tail.1 = s16[136,256]{1,0:T(8,128)(2,1)} custom-call(s32[16]{0:T(128)} %net_flags.1.where_ref, s16[8,136,256]{2,1,0:T(8,128)(2,1)} %all-to-all-done.1.states_ref), custom_call_target="tpu_custom_call" | custom-call | tf_op jit(solution)/shard_map/group_tail/pallas_call | solution.py:337
  53.1 4.3 %collective-permute-start.3 = (s16[136,256]{1,0:T(8,128)(2,1)}, s16[136,256]{1,0:T(8,128)(2,1)S(1)}, u32[]{:S(2)}, u32[]{:S(2)}) collective-permute-start(s16[136,256]{1,0:T(8,128)(2,1)} %group_tail.1), channel_id=1, source_target_pairs={{0,16},{1,17},{2,18},{3,19},{4,20},{5,21},{6,22},{7,23},{8,24},{9,... | collective-permute-start | bytes 208904 | tf_op jit(solution)/shard_map/ppermute | solution.py:430
  57.4 2.5 %collective-permute-start.2 = (s16[136,256]{1,0:T(8,128)(2,1)}, s16[136,256]{1,0:T(8,128)(2,1)S(1)}, u32[]{:S(2)}, u32[]{:S(2)}) collective-permute-start(s16[136,256]{1,0:T(8,128)(2,1)} %group_tail.1), channel_id=1, source_target_pairs={{0,8},{1,9},{2,10},{3,11},{4,12},{5,13},{6,14},{7,15},{8,16},{9,17... | collective-permute-start | bytes 208904 | tf_op jit(solution)/shard_map/ppermute | solution.py:430
  59.9 5.9 %collective-permute-done.3.far_ref = s16[136,256]{1,0:T(8,128)(2,1)S(1)} collective-permute-done((s16[136,256]{1,0:T(8,128)(2,1)}, s16[136,256]{1,0:T(8,128)(2,1)S(1)}, u32[]{:S(2)}, u32[]{:S(2)}) %collective-permute-start.3) | collective-permute-done | bytes 69664 | tf_op jit(solution)/shard_map/ppermute | solution.py:430
  65.8 0.0 copy-start.2
  65.8 2.0 %collective-permute-done.2.near_ref = s16[136,256]{1,0:T(8,128)(2,1)S(1)} collective-permute-done((s16[136,256]{1,0:T(8,128)(2,1)}, s16[136,256]{1,0:T(8,128)(2,1)S(1)}, u32[]{:S(2)}, u32[]{:S(2)}) %collective-permute-start.2) | collective-permute-done | bytes 69664 | tf_op jit(solution)/shard_map/ppermute | solution.py:430
  67.9 0.0 copy-done.2
  67.9 0.0 copy-start.3
  67.9 0.6 copy-done.3
  68.5 2.4 %entering_states.1 = s16[8,136,256]{2,1,0:T(8,128)(2,1)} custom-call(s32[16]{0:T(128)} %net_flags.1.where_ref, s16[8,136,256]{2,1,0:T(8,128)(2,1)} %all-to-all-done.1.states_ref, s16[136,256]{1,0:T(8,128)(2,1)} %copy-done.3, s16[136,256]{1,0:T(8,128)(2,1)} %copy-done.2, f32[8,256,128]{2,1,0:T(8,128)} %state_ref.1, f32[8,256]{1,0:T(8,128)} %norm_ref.1), custom_call_target="tpu_custom_call" | custom-call | tf_op jit(solution)/shard_map/entering_states/pallas_call | solution.py:376
  70.9 4.2 %all-to-all-start.2 = ((s16[8,136,256]{2,1,0:T(8,128)(2,1)}), s16[8,136,256]{2,1,0:T(8,128)(2,1)}, u32[]{:S(2)}, u32[]{:S(2)}) async-start(s16[8,136,256]{2,1,0:T(8,128)(2,1)} %entering_states.1), calls=%async_computation.2 | async-start | bytes 1114112 | tf_op jit(solution)/shard_map/all_to_all | solution.py:456
  75.1 5.4 %local_attention.3 = (bf16[8,2,256,256]{3,2,1,0:T(8,128)(2,1)}, f32[2,5,256,128]{3,2,1,0:T(8,128)}) custom-call(s32[16]{0:T(128)} %net_flags.1.where_ref, s32[32,1,1]{2,1,0:T(1,128)S(1)} %all-to-all-done.lengths_ref, s32[64]{0:T(128)S(1)} %copy-done.1, f32[128,256]{1,0:T(8,128)} %map_ref.5, ...), custom_call_target="tpu_custom_call", output_to_operand_aliasing={{0}: (13, {}), {1}: (14, {})} | custom-call | flops 3000000000 | bytes 4000000 | tf_op jit(solution)/shard_map/local_attention/pallas_call | solution.py:305
  80.5 3.0 %all-to-all-done.2.state_ref = s16[8,136,256]{2,1,0:T(8,128)(2,1)} async-done(((s16[8,136,256]{2,1,0:T(8,128)(2,1)}), s16[8,136,256]{2,1,0:T(8,128)(2,1)}, u32[]{:S(2)}, u32[]{:S(2)}) %all-to-all-start.2) | async-done | bytes 557088 | tf_op jit(solution)/shard_map/all_to_all | solution.py:456
  83.5 3.6 %finish.1 = f32[256,1024]{1,0:T(8,128)} custom-call(s32[16]{0:T(128)} %net_flags.1.where_ref, s16[8,136,256]{2,1,0:T(8,128)(2,1)} %all-to-all-done.2.state_ref, bf16[8,2,256,256]{3,2,1,0:T(8,128)(2,1)} %get-tuple-element.23.feature_ref, f32[2,5,256,128]{3,2,1,0:T(8,128)} %get-tuple-element.24.local_ref), custom_call_target="tpu_custom_call" | custom-call | tf_op jit(solution)/shard_map/finish/pallas_call | solution.py:412
Async XLA Ops:
  0.0 32.6 %copy-start = (bf16[448,3072]{1,0:T(8,128)(2,1)S(1)}, bf16[448,3072]{1,0:T(8,128)(2,1)}, u32[]{:S(2)}) copy-start(bf16[448,3072]{1,0:T(8,128)(2,1)} %refs_6_.3) | copy-start | bytes 8257540
  3.1 29.5 %collective-permute-start = (bf16[104,3072]{1,0:T(8,128)(2,1)}, bf16[104,3072]{1,0:T(8,128)(2,1)S(1)}, u32[]{:S(2)}, u32[]{:S(2)}) collective-permute-start(bf16[104,3072]{1,0:T(8,128)(2,1)} %get-tuple-element.16), channel_id=1, source_target_pairs={{0,1},{1,2},{2,3},{3,4},{4,5},{5,6},{6,7},{7,8},{8,9},{9,10},{10,1... | collective-permute-start | bytes 1916936 | tf_op jit(solution)/shard_map/ppermute | solution.py:430
  6.6 26.0 %collective-permute-start.1 = (bf16[96,3072]{1,0:T(8,128)(2,1)}, bf16[96,3072]{1,0:T(8,128)(2,1)}, u32[]{:S(2)}, u32[]{:S(2)}) collective-permute-start(bf16[96,3072]{1,0:T(8,128)(2,1)} %get-tuple-element.17), channel_id=1, source_target_pairs={{1,0},{2,1},{3,2},{4,3},{5,4},{6,5},{7,6},{8,7},{9,8},{10,9},{11,1... | collective-permute-start | bytes 1769480 | tf_op jit(solution)/shard_map/ppermute | solution.py:430
  7.9 24.7 %all-to-all-start = ((s32[32,1,1]{2,1,0:T(1,128)}), s32[32,1,1]{2,1,0:T(1,128)S(1)}, u32[]{:S(2)}, u32[]{:S(2)}) async-start(s32[32,1,1]{2,1,0:T(1,128)} %get-tuple-element.15), calls=%async_computation | async-start | bytes 32768 | tf_op jit(solution)/shard_map/all_to_all | solution.py:442
  25.1 17.5 %copy-start.1 = (s32[64]{0:T(128)S(1)}, s32[64]{0:T(128)}, u32[]{:S(2)}) copy-start(s32[64]{0:T(128)} %nets_ref.5) | copy-start | bytes 772
  36.4 14.7 %all-to-all-start.1 = ((s16[8,136,256]{2,1,0:T(8,128)(2,1)}), s16[8,136,256]{2,1,0:T(8,128)(2,1)}, u32[]{:S(2)}, u32[]{:S(2)}) async-start(s16[8,136,256]{2,1,0:T(8,128)(2,1)} %local_states.1), calls=%async_computation.1 | async-start | bytes 1114112 | tf_op jit(solution)/shard_map/all_to_all | solution.py:445
  53.1 12.7 %collective-permute-start.3 = (s16[136,256]{1,0:T(8,128)(2,1)}, s16[136,256]{1,0:T(8,128)(2,1)S(1)}, u32[]{:S(2)}, u32[]{:S(2)}) collective-permute-start(s16[136,256]{1,0:T(8,128)(2,1)} %group_tail.1), channel_id=1, source_target_pairs={{0,16},{1,17},{2,18},{3,19},{4,20},{5,21},{6,22},{7,23},{8,24},{9,... | collective-permute-start | bytes 208904 | tf_op jit(solution)/shard_map/ppermute | solution.py:430
  57.4 10.5 %collective-permute-start.2 = (s16[136,256]{1,0:T(8,128)(2,1)}, s16[136,256]{1,0:T(8,128)(2,1)S(1)}, u32[]{:S(2)}, u32[]{:S(2)}) collective-permute-start(s16[136,256]{1,0:T(8,128)(2,1)} %group_tail.1), channel_id=1, source_target_pairs={{0,8},{1,9},{2,10},{3,11},{4,12},{5,13},{6,14},{7,15},{8,16},{9,17... | collective-permute-start | bytes 208904 | tf_op jit(solution)/shard_map/ppermute | solution.py:430
  65.8 2.0 %copy-start.2 = (s16[136,256]{1,0:T(8,128)(2,1)}, s16[136,256]{1,0:T(8,128)(2,1)S(1)}, u32[]{:S(2)}) copy-start(s16[136,256]{1,0:T(8,128)(2,1)S(1)} %collective-permute-done.3.far_ref) | copy-start | bytes 208900
  67.9 0.6 copy-start.3
  70.9 12.6 %all-to-all-start.2 = ((s16[8,136,256]{2,1,0:T(8,128)(2,1)}), s16[8,136,256]{2,1,0:T(8,128)(2,1)}, u32[]{:S(2)}, u32[]{:S(2)}) async-start(s16[8,136,256]{2,1,0:T(8,128)(2,1)} %entering_states.1), calls=%async_computation.2 | async-start | bytes 1114112 | tf_op jit(solution)/shard_map/all_to_all | solution.py:456

commit v6 on v5

--- a/solution.py
+++ b/solution.py
@@ -375,7 +375,8 @@
     vmem = pl.BlockSpec(memory_space=pltpu.VMEM)
     return pl.pallas_call(
         prefix_kernel,
-        out_shape=jax.ShapeDtypeStruct((GROUP, CODED, M), I16),
+        out_shape=pltpu.HBM((GROUP, CODED, M), I16),
+        grid=(1,),
         in_specs=[
             pl.BlockSpec(memory_space=pltpu.SMEM),
             vmem,
@@ -384,10 +385,11 @@
             pl.BlockSpec(memory_space=pl.ANY),
             vmem,
         ],
-        out_specs=vmem,
+        out_specs=pl.BlockSpec((GROUP, CODED, M), lambda i: (0, 0, 0)),
         scratch_shapes=[pltpu.VMEM((M, DH), F32), pltpu.SemaphoreType.DMA(())],
+        compiler_params=pltpu.CompilerParams(vmem_limit_bytes=24 << 20),
         name="entering_states",
-    )(where, states, in_hbm(near), in_hbm(far), in_hbm(carried_state), carried_norm)
+    )(where, states, near, far, in_hbm(carried_state), carried_norm)
 
 
 def finish_kernel(where_ref, state_ref, feature_ref, local_ref, out_ref):

time: 87.7 us -> 87 us (level)
  no operation moved by 1% of the time
where the time goes in v6:
time: 87 us; the launch traced here: 86.4 us
  starting transfers between devices  36.9 us (42%)
  Pallas kernels  26.9 us (31%)
  waiting for transfers between devices  21.7 us (25%)
  between operations  0.91 us (1%)
    all_to_all x1, starting transfers between devices, local(): lengths = lax.all_to_all(length, 'seq', 0, 0, tiled=True)  15 us
    ppermute x4, starting transfers between devices, shifted(): lax.ppermute(block, axis, [(i - distance, i) for i in range(ahead, count...  11.6 us
    pallas_call x2, Pallas kernels, local_attention(): pl.pallas_call(attention_kernel, out_shape=(pltpu.HBM((H, 2, TOK_DEV, M),...  10.8 us
    all_to_all x2, starting transfers between devices, local(): lax.all_to_all(states, 'seq', 0, 0, axis_index_groups=groups, tiled=True)  10.3 us
    ppermute x4, waiting for transfers between devices, shifted(): lax.ppermute(block, axis, [(i - distance, i) for i in range(ahead, count...  7.94 us
    all_to_all x1, waiting for transfers between devices, local(): lengths = lax.all_to_all(length, 'seq', 0, 0, tiled=True)  7.66 us
    all_to_all x2, waiting for transfers between devices, local(): lax.all_to_all(states, 'seq', 0, 0, axis_index_groups=groups, tiled=True)  6.1 us
    pallas_call x1, Pallas kernels, local_states(): pl.pallas_call(state_kernel, out_shape=pltpu.HBM((H, CODED, M), I16), gri...  3.76 us
  transfers between devices with their start and end apart: 7, of which 5 were waited for; matrix products, arithmetic and copies ran while one was open for 0% of the time, Pallas kernels for 15%

profile of v6, /device:TPU:32, one launch (start us, length us, event | category | flops | bytes accessed | tf_op | source)
XLA Modules:
  0.0 86.4 jit_solution(14190744898242394103)
XLA Ops:
  0.0 0.0 copy-start
  0.8 2.3 %windows.1 = (bf16[104,3072]{1,0:T(8,128)(2,1)}, bf16[96,3072]{1,0:T(8,128)(2,1)}, s32[32,1,1]{2,1,0:T(1,128)}) custom-call(s32[1,1]{1,0:T(1,128)S(6)} %copy.11.length_ref, bf16[448,3072]{1,0:T(8,128)(2,1)} %refs_6_.3), custom_call_target="tpu_custom_call" | custom-call | tf_op jit(solution)/shard_map/windows/pallas_call | solution.py:69
  3.1 3.6 %collective-permute-start = (bf16[104,3072]{1,0:T(8,128)(2,1)}, bf16[104,3072]{1,0:T(8,128)(2,1)S(1)}, u32[]{:S(2)}, u32[]{:S(2)}) collective-permute-start(bf16[104,3072]{1,0:T(8,128)(2,1)} %get-tuple-element.16), channel_id=1, source_target_pairs={{0,1},{1,2},{2,3},{3,4},{4,5},{5,6},{6,7},{7,8},{8,9},{9,10},{10,1... | collective-permute-start | bytes 1916936 | tf_op jit(solution)/shard_map/ppermute | solution.py:432
  6.7 1.3 %collective-permute-start.1 = (bf16[96,3072]{1,0:T(8,128)(2,1)}, bf16[96,3072]{1,0:T(8,128)(2,1)}, u32[]{:S(2)}, u32[]{:S(2)}) collective-permute-start(bf16[96,3072]{1,0:T(8,128)(2,1)} %get-tuple-element.17), channel_id=1, source_target_pairs={{1,0},{2,1},{3,2},{4,3},{5,4},{6,5},{7,6},{8,7},{9,8},{10,9},{11,1... | collective-permute-start | bytes 1769480 | tf_op jit(solution)/shard_map/ppermute | solution.py:432
  8.0 15.0 %all-to-all-start = ((s32[32,1,1]{2,1,0:T(1,128)}), s32[32,1,1]{2,1,0:T(1,128)S(1)}, u32[]{:S(2)}, u32[]{:S(2)}) async-start(s32[32,1,1]{2,1,0:T(1,128)} %get-tuple-element.15), calls=%async_computation | async-start | bytes 32768 | tf_op jit(solution)/shard_map/all_to_all | solution.py:444
  23.0 2.1 %net_flags.1.where_ref = s32[16]{0:T(128)} custom-call(s32[1]{0:T(128)} %bitcast.place_ref, s32[64]{0:T(128)} %nets_ref.5), custom_call_target="tpu_custom_call" | custom-call | tf_op jit(solution)/shard_map/net_flags/pallas_call | solution.py:119
  25.1 0.0 copy-start.2
  25.1 7.7 %all-to-all-done.lengths_ref = s32[32,1,1]{2,1,0:T(1,128)S(1)} async-done(((s32[32,1,1]{2,1,0:T(1,128)}), s32[32,1,1]{2,1,0:T(1,128)S(1)}, u32[]{:S(2)}, u32[]{:S(2)}) %all-to-all-start) | async-done | bytes 160 | tf_op jit(solution)/shard_map/all_to_all | solution.py:444
  32.8 0.0 collective-permute-done.1.right_ref.refs_2_.refs_5_.refs_8_
  32.8 0.0 collective-permute-done.left_ref.refs_1_.refs_4_.refs_7_
  32.8 0.0 copy-done
  32.8 3.8 %local_states.1 = s16[8,136,256]{2,1,0:T(8,128)(2,1)} custom-call(s32[16]{0:T(128)} %net_flags.1.where_ref, s32[32,1,1]{2,1,0:T(1,128)S(1)} %all-to-all-done.lengths_ref, f32[128,256]{1,0:T(8,128)} %map_ref.5, bf16[448,3072]{1,0:T(8,128)(2,1)S(1)} %copy-done, bf16[104,3072]{1,0:T(8,128)(2,1)S(1)} %collective-permute-done.left_ref.refs_1_.refs_4_.refs_7_, ...), custom_call_target="tpu_custom_call" | custom-call | tf_op jit(solution)/shard_map/local_states/pallas_call | solution.py:240
  36.5 6.1 %all-to-all-start.1 = ((s16[8,136,256]{2,1,0:T(8,128)(2,1)}), s16[8,136,256]{2,1,0:T(8,128)(2,1)}, u32[]{:S(2)}, u32[]{:S(2)}) async-start(s16[8,136,256]{2,1,0:T(8,128)(2,1)} %local_states.1), calls=%async_computation.1 | async-start | bytes 1114112 | tf_op jit(solution)/shard_map/all_to_all | solution.py:447
  42.6 0.0 copy-done.2
  42.6 0.0 copy-start.1
  42.6 5.4 %local_attention.2 = (bf16[8,2,256,256]{3,2,1,0:T(8,128)(2,1)}, f32[2,5,256,128]{3,2,1,0:T(8,128)}) custom-call(s32[16]{0:T(128)} %net_flags.1.where_ref, s32[32,1,1]{2,1,0:T(1,128)S(1)} %all-to-all-done.lengths_ref, s32[64]{0:T(128)S(1)} %copy-done.2, f32[128,256]{1,0:T(8,128)} %map_ref.5, bf16[448,3072]{1,0:T(8,128)(2,1)S(1)} %copy-done, ...), custom_call_target="tpu_custom_call" | custom-call | flops 3000000000 | bytes 4000000 | tf_op jit(solution)/shard_map/local_attention/pallas_call | solution.py:305
  48.0 3.1 %all-to-all-done.1.states_ref = s16[8,136,256]{2,1,0:T(8,128)(2,1)} async-done(((s16[8,136,256]{2,1,0:T(8,128)(2,1)}), s16[8,136,256]{2,1,0:T(8,128)(2,1)}, u32[]{:S(2)}, u32[]{:S(2)}) %all-to-all-start.1) | async-done | bytes 557088 | tf_op jit(solution)/shard_map/all_to_all | solution.py:447
  51.1 2.0 %group_tail.1 = s16[136,256]{1,0:T(8,128)(2,1)} custom-call(s32[16]{0:T(128)} %net_flags.1.where_ref, s16[8,136,256]{2,1,0:T(8,128)(2,1)} %all-to-all-done.1.states_ref), custom_call_target="tpu_custom_call" | custom-call | tf_op jit(solution)/shard_map/group_tail/pallas_call | solution.py:337
  53.1 4.2 %collective-permute-start.3 = (s16[136,256]{1,0:T(8,128)(2,1)}, s16[136,256]{1,0:T(8,128)(2,1)S(1)}, u32[]{:S(2)}, u32[]{:S(2)}) collective-permute-start(s16[136,256]{1,0:T(8,128)(2,1)} %group_tail.1), channel_id=1, source_target_pairs={{0,16},{1,17},{2,18},{3,19},{4,20},{5,21},{6,22},{7,23},{8,24},{9,... | collective-permute-start | bytes 208904 | tf_op jit(solution)/shard_map/ppermute | solution.py:432
  57.3 2.5 %collective-permute-start.2 = (s16[136,256]{1,0:T(8,128)(2,1)}, s16[136,256]{1,0:T(8,128)(2,1)S(1)}, u32[]{:S(2)}, u32[]{:S(2)}) collective-permute-start(s16[136,256]{1,0:T(8,128)(2,1)} %group_tail.1), channel_id=1, source_target_pairs={{0,8},{1,9},{2,10},{3,11},{4,12},{5,13},{6,14},{7,15},{8,16},{9,17... | collective-permute-start | bytes 208904 | tf_op jit(solution)/shard_map/ppermute | solution.py:432
  59.9 5.9 %collective-permute-done.3.far_ref = s16[136,256]{1,0:T(8,128)(2,1)S(1)} collective-permute-done((s16[136,256]{1,0:T(8,128)(2,1)}, s16[136,256]{1,0:T(8,128)(2,1)S(1)}, u32[]{:S(2)}, u32[]{:S(2)}) %collective-permute-start.3) | collective-permute-done | bytes 69664 | tf_op jit(solution)/shard_map/ppermute | solution.py:432
  65.8 2.0 %collective-permute-done.2.near_ref = s16[136,256]{1,0:T(8,128)(2,1)S(1)} collective-permute-done((s16[136,256]{1,0:T(8,128)(2,1)}, s16[136,256]{1,0:T(8,128)(2,1)S(1)}, u32[]{:S(2)}, u32[]{:S(2)}) %collective-permute-start.2) | collective-permute-done | bytes 69664 | tf_op jit(solution)/shard_map/ppermute | solution.py:432
  67.8 0.0 copy-done.1
  67.8 2.3 %entering_states.1 = s16[8,136,256]{2,1,0:T(8,128)(2,1)} custom-call(s32[16]{0:T(128)} %net_flags.1.where_ref, s16[8,136,256]{2,1,0:T(8,128)(2,1)} %all-to-all-done.1.states_ref, s16[136,256]{1,0:T(8,128)(2,1)S(1)} %collective-permute-done.2.near_ref, s16[136,256]{1,0:T(8,128)(2,1)S(1)} %collective-permute-done.3.far_ref, f32[8,256,128]{2,1,0:T(8,128)} %state_ref.1, ...), custom_call_target="tpu_custom_call" | custom-call | tf_op jit(solution)/shard_map/entering_states/pallas_call | solution.py:376
  70.2 4.2 %all-to-all-start.2 = ((s16[8,136,256]{2,1,0:T(8,128)(2,1)}), s16[8,136,256]{2,1,0:T(8,128)(2,1)}, u32[]{:S(2)}, u32[]{:S(2)}) async-start(s16[8,136,256]{2,1,0:T(8,128)(2,1)} %entering_states.1), calls=%async_computation.2 | async-start | bytes 1114112 | tf_op jit(solution)/shard_map/all_to_all | solution.py:458
  74.4 5.4 %local_attention.3 = (bf16[8,2,256,256]{3,2,1,0:T(8,128)(2,1)}, f32[2,5,256,128]{3,2,1,0:T(8,128)}) custom-call(s32[16]{0:T(128)} %net_flags.1.where_ref, s32[32,1,1]{2,1,0:T(1,128)S(1)} %all-to-all-done.lengths_ref, s32[64]{0:T(128)S(1)} %copy-done.2, f32[128,256]{1,0:T(8,128)} %map_ref.5, ...), custom_call_target="tpu_custom_call", output_to_operand_aliasing={{0}: (13, {}), {1}: (14, {})} | custom-call | flops 3000000000 | bytes 4000000 | tf_op jit(solution)/shard_map/local_attention/pallas_call | solution.py:305
  79.8 3.0 %all-to-all-done.2.state_ref = s16[8,136,256]{2,1,0:T(8,128)(2,1)} async-done(((s16[8,136,256]{2,1,0:T(8,128)(2,1)}), s16[8,136,256]{2,1,0:T(8,128)(2,1)}, u32[]{:S(2)}, u32[]{:S(2)}) %all-to-all-start.2) | async-done | bytes 557088 | tf_op jit(solution)/shard_map/all_to_all | solution.py:458
  82.8 3.6 %finish.1 = f32[256,1024]{1,0:T(8,128)} custom-call(s32[16]{0:T(128)} %net_flags.1.where_ref, s16[8,136,256]{2,1,0:T(8,128)(2,1)} %all-to-all-done.2.state_ref, bf16[8,2,256,256]{3,2,1,0:T(8,128)(2,1)} %get-tuple-element.23.feature_ref, f32[2,5,256,128]{3,2,1,0:T(8,128)} %get-tuple-element.24.local_ref), custom_call_target="tpu_custom_call" | custom-call | tf_op jit(solution)/shard_map/finish/pallas_call | solution.py:414
Async XLA Ops:
  0.0 32.8 %copy-start = (bf16[448,3072]{1,0:T(8,128)(2,1)S(1)}, bf16[448,3072]{1,0:T(8,128)(2,1)}, u32[]{:S(2)}) copy-start(bf16[448,3072]{1,0:T(8,128)(2,1)} %refs_6_.3) | copy-start | bytes 8257540
  3.1 29.6 %collective-permute-start = (bf16[104,3072]{1,0:T(8,128)(2,1)}, bf16[104,3072]{1,0:T(8,128)(2,1)S(1)}, u32[]{:S(2)}, u32[]{:S(2)}) collective-permute-start(bf16[104,3072]{1,0:T(8,128)(2,1)} %get-tuple-element.16), channel_id=1, source_target_pairs={{0,1},{1,2},{2,3},{3,4},{4,5},{5,6},{6,7},{7,8},{8,9},{9,10},{10,1... | collective-permute-start | bytes 1916936 | tf_op jit(solution)/shard_map/ppermute | solution.py:432
  6.7 26.1 %collective-permute-start.1 = (bf16[96,3072]{1,0:T(8,128)(2,1)}, bf16[96,3072]{1,0:T(8,128)(2,1)}, u32[]{:S(2)}, u32[]{:S(2)}) collective-permute-start(bf16[96,3072]{1,0:T(8,128)(2,1)} %get-tuple-element.17), channel_id=1, source_target_pairs={{1,0},{2,1},{3,2},{4,3},{5,4},{6,5},{7,6},{8,7},{9,8},{10,9},{11,1... | collective-permute-start | bytes 1769480 | tf_op jit(solution)/shard_map/ppermute | solution.py:432
  8.0 24.8 %all-to-all-start = ((s32[32,1,1]{2,1,0:T(1,128)}), s32[32,1,1]{2,1,0:T(1,128)S(1)}, u32[]{:S(2)}, u32[]{:S(2)}) async-start(s32[32,1,1]{2,1,0:T(1,128)} %get-tuple-element.15), calls=%async_computation | async-start | bytes 32768 | tf_op jit(solution)/shard_map/all_to_all | solution.py:444
  25.1 17.5 %copy-start.2 = (s32[64]{0:T(128)S(1)}, s32[64]{0:T(128)}, u32[]{:S(2)}) copy-start(s32[64]{0:T(128)} %nets_ref.5) | copy-start | bytes 772
  36.5 14.6 %all-to-all-start.1 = ((s16[8,136,256]{2,1,0:T(8,128)(2,1)}), s16[8,136,256]{2,1,0:T(8,128)(2,1)}, u32[]{:S(2)}, u32[]{:S(2)}) async-start(s16[8,136,256]{2,1,0:T(8,128)(2,1)} %local_states.1), calls=%async_computation.1 | async-start | bytes 1114112 | tf_op jit(solution)/shard_map/all_to_all | solution.py:447
  42.6 25.2 %copy-start.1 = (f32[8,256]{1,0:T(8,128)S(1)}, f32[8,256]{1,0:T(8,128)}, u32[]{:S(2)}) copy-start(f32[8,256]{1,0:T(8,128)} %norm_ref.1) | copy-start | bytes 24580
  53.1 12.7 %collective-permute-start.3 = (s16[136,256]{1,0:T(8,128)(2,1)}, s16[136,256]{1,0:T(8,128)(2,1)S(1)}, u32[]{:S(2)}, u32[]{:S(2)}) collective-permute-start(s16[136,256]{1,0:T(8,128)(2,1)} %group_tail.1), channel_id=1, source_target_pairs={{0,16},{1,17},{2,18},{3,19},{4,20},{5,21},{6,22},{7,23},{8,24},{9,... | collective-permute-start | bytes 208904 | tf_op jit(solution)/shard_map/ppermute | solution.py:432
  57.3 10.5 %collective-permute-start.2 = (s16[136,256]{1,0:T(8,128)(2,1)}, s16[136,256]{1,0:T(8,128)(2,1)S(1)}, u32[]{:S(2)}, u32[]{:S(2)}) collective-permute-start(s16[136,256]{1,0:T(8,128)(2,1)} %group_tail.1), channel_id=1, source_target_pairs={{0,8},{1,9},{2,10},{3,11},{4,12},{5,13},{6,14},{7,15},{8,16},{9,17... | collective-permute-start | bytes 208904 | tf_op jit(solution)/shard_map/ppermute | solution.py:432
  70.2 12.6 %all-to-all-start.2 = ((s16[8,136,256]{2,1,0:T(8,128)(2,1)}), s16[8,136,256]{2,1,0:T(8,128)(2,1)}, u32[]{:S(2)}, u32[]{:S(2)}) async-start(s16[8,136,256]{2,1,0:T(8,128)(2,1)} %entering_states.1), calls=%async_computation.2 | async-start | bytes 1114112 | tf_op jit(solution)/shard_map/all_to_all | solution.py:458
